TPU v7x, 256 devices: a whole 4x4x8 slice. The times are simulated.
256 devices in a mesh: row: 32 (over x_hi, z, core), off: 8 (over y, x_lo).
Axes of the slice: x: 4 (x_hi: 2, x_lo: 2; x = x_hi * 2 + x_lo), y: 4, z: 8, core: 2. Of those that a mesh axis runs over, the one named last changes fastest.
Arguments:
- vectors: float32 [64, 32768], P(None, 'row'), may hold values from -6 to 6
- tiles: float32 [32768, 16384], P('row', 'off'), may hold values from -0.03125 to 0.03125
- live: int32 [32, 16], P('row', 'off'), may hold values from 256 to 1024
- energies: float32 [32768], P('row'), may hold values from 0.25 to 5.25
- precond: float32 [32768], P('row'), may hold values from 0.03 to 0.3
Outputs:
- basis: float32 [64, 32768], P(None, 'row')
- ritz: float32 [64, 64], replicated
All inputs are finite; a program needn't handle non-finite values.
Results may differ from a plain program's by a relative error of at most 0.00025.
Values sent between devices are 32-bit elements; how exact they have to be, the bound alone decides.
No kernel may reach another device: no remote copies, remote signals or barrier semaphores. Data moves between devices by JAX's collectives and lax.ppermute only.
A program may use at most 64 MiB of HBM per device.

v0:
```python
import jax
import jax.numpy as jnp
from jax import lax
from jax.sharding import PartitionSpec as P


AXES = ("row", "off")


class Layout:
    def __init__(self, rows, offs, per_device):
        self.rows, self.offs, self.per = rows, offs, per_device
        number = lambda row, off: (row % rows) * offs + off
        every = [(row, p) for row in range(rows) for p in range(offs)]
        self.row = [[number(row, p) for p in range(offs)] for row in range(rows)]
        self.line = [
            [number(2 * chip + core, p) for chip in range(rows // 2)]
            for core in range(2)
            for p in range(offs)
        ]
        self.flip = {
            bit: [(number(row, p), number(row ^ bit, p)) for row, p in every]
            for bit in (1 << n for n in range(rows.bit_length() - 1))
        }
        self.fetch = [(number(row, p), number(row - per_device * p, p)) for row, p in every]
        self.back = [(b, a) for a, b in self.fetch]
        self.up = [(number(row, p), number(row + 1, p)) for row, p in every]
        self.down = [(b, a) for a, b in self.up]


def exchange(array, groups):
    return lax.all_to_all(array, AXES, 0, 0, axis_index_groups=groups, tiled=True)


def sent_to_all(array, groups):
    peers = len(groups[0])
    return exchange(jnp.broadcast_to(array[None], (peers, *array.shape)), groups)


def exact(left, right):
    return jnp.dot(left, right, precision=lax.Precision.HIGHEST, preferred_element_type=jnp.float32)


def gram(left, right):
    return lax.dot_general(
        left,
        right,
        (((1,), (1,)), ((), ())),
        precision=lax.Precision.HIGHEST,
        preferred_element_type=jnp.float32,
    )


def cut(array, parts):
    k, width = array.shape
    return array.reshape(k, parts, width // parts).transpose(1, 0, 2)


def joined(array):
    parts, k, w = array.shape
    return array.transpose(1, 0, 2).reshape(k, parts * w)


def folded(square):
    half = square.shape[0] // 2
    return jnp.concatenate([square[:half], square[half:]], axis=1)


def unfolded(array):
    half = array.shape[0]
    return jnp.concatenate([array[:, : 2 * half], array[:, 2 * half :]], axis=0)


def permuted(array, pairs):
    return lax.ppermute(array, AXES, pairs)


def row_total(part, lay):
    for pairs in lay.flip.values():
        part = part + permuted(part, pairs)
    return part


def line_total(part, lay):
    part = jnp.sum(sent_to_all(part, lay.line), axis=0)
    return part + permuted(part, lay.flip[1])


def direct_product(piece, block, mask):
    term = lax.dot_general(
        piece,
        block,
        (((1,), (1,)), ((), ())),
        precision=lax.Precision.HIGH,
        preferred_element_type=jnp.float32,
    )
    return mask * term


def back_product(vectors, block, mask):
    return jnp.dot(
        vectors * mask, block, precision=lax.Precision.HIGH, preferred_element_type=jnp.float32
    )


def local(vectors, tiles, live, energies, precond):
    count, width = vectors.shape
    per_device = tiles.shape[1] // width
    rows, offs = lax.axis_size("row"), lax.axis_size("off")
    lay = Layout(rows, offs, per_device)
    total_rows = width * rows
    part = width // offs
    off_index = lax.axis_index("off")
    row_ids = jnp.arange(width, dtype=jnp.int32)
    masks = [(row_ids < live[0, s]).astype(jnp.float32) for s in range(per_device)]
    blocks = [tiles[:, s * width : (s + 1) * width] for s in range(per_device)]
    identity = jnp.eye(count, dtype=jnp.float32)
    own = lambda array: lax.dynamic_index_in_dim(cut(array, offs), off_index, 0, keepdims=False)

    def products(vecs, extra):
        near = permuted(vecs, lay.fetch)
        up = permuted(back_product(vecs, blocks[1], masks[1]), lay.up)
        back = lax.optimization_barrier(back_product(vecs, blocks[0], masks[0])) + up
        returned = permuted(back, lay.back)
        far = permuted(near, lay.down)
        pair = gram(near, back)
        share = folded(pair + pair.T + gram(vecs, energies * vecs) * (1.0 / offs))
        share = row_total(jnp.concatenate([share] + extra, axis=0), lay)
        direct = direct_product(near, blocks[0], masks[0]) + direct_product(far, blocks[1], masks[1])
        return lax.optimization_barrier(direct) + returned, share

    def spread(chunk, share):
        got = sent_to_all(jnp.concatenate([chunk, share], axis=0), lay.row)
        return joined(got[:, :count]), unfolded(jnp.sum(got[:, count:], axis=0)) / total_rows

    chunk, precond_chunk, energy_chunk = own(vectors), own(precond[None]), own(energies[None])
    part, share = products(vectors, [])
    image = energy_chunk * chunk + jnp.sum(exchange(cut(part, offs), lay.row), axis=0)
    stepped, ritz = spread(chunk - precond_chunk * image, share)
    moved = stepped + precond * exact(ritz.T, vectors)

    moved_chunk = own(moved)
    part, share = products(moved, [folded(gram(moved, moved))])
    image = energy_chunk * moved_chunk + jnp.sum(exchange(cut(part, offs), lay.row), axis=0)
    fix = 1.5 * identity - 0.5 * unfolded(share[count // 2 :]) / total_rows
    chunk = exact(fix.T, moved_chunk - precond_chunk * image)
    stepped, ritz = spread(chunk, share[: count // 2])
    ritz = exact(exact(fix.T, ritz), fix)
    moved = stepped + precond * exact(ritz.T, exact(fix.T, moved))

    correlation = unfolded(line_total(folded(gram(moved, moved)), lay)) / total_rows
    return exact((1.5 * identity - 0.5 * correlation).T, moved), ritz


def solution(mesh):
    placed = (P(None, "row"), P("row", "off"), P("row", "off"), P("row"), P("row"))
    return jax.shard_map(
        local, mesh=mesh, in_specs=placed, out_specs=(P(None, "row"), P()), check_vma=False
    )
```

profile of v0, /device:TPU:1, one launch (start us, length us, event | category | flops | bytes accessed | tf_op | source)
XLA Modules:
  0.0 215.0 jit_solution(15021060221636784630)
XLA Ops:
  0.7 1.7 collective-permute-start
  2.4 1.3 fusion.93
  3.7 0.6 fusion.72
  4.4 3.7 %fusion.4 = f32[64,1024]{1,0:T(8,128)S(1)} fusion(f32[1024,2048]{1,0:T(8,128)} %param.6, f32[64,1024]{1,0:T(8,128)} %param.5, f32[1024]{0:T(1024)S(1)} %fusion.72), kind=kOutput, calls=%fused_computation.4 | convolution fusion | flops 402718720 | bytes 4722688 | tf_op jit(solution)/shard_map/dot_general | solution.py:101
  8.1 3.1 %collective-permute-start.2 = (f32[64,1024]{1,0:T(8,128)S(1)}, f32[64,1024]{1,0:T(8,128)S(1)}, u32[]{:S(2)}, u32[]{:S(2)}) collective-permute-start(f32[64,1024]{1,0:T(8,128)S(1)} %fusion.4), channel_id=1, source_target_pairs={{0,8},{1,9},{2,10},{3,11},{4,12},{5,13},{6,14},{7,15},{8,16},{9,17... | collective-permute-start | bytes 786440 | tf_op jit(solution)/shard_map/ppermute | solution.py:75
  11.2 0.6 fusion.71
  11.8 3.7 %fusion.12 = f32[64,1024]{1,0:T(8,128)S(1)} fusion(f32[1024,2048]{1,0:T(8,128)} %param.6, f32[64,1024]{1,0:T(8,128)} %param.5, f32[1024]{0:T(1024)S(1)} %fusion.71), kind=kOutput, calls=%fused_computation.12 | convolution fusion | flops 402718720 | bytes 4722688 | tf_op jit(solution)/shard_map/dot_general | solution.py:101
  15.5 0.4 fusion.36
  16.0 0.4 fusion.94
  16.4 0.1 pad_maximum_fusion.2
  16.5 5.5 %collective-permute-start.4 = (f32[32,128]{1,0:T(8,128)S(1)}, f32[32,128]{1,0:T(8,128)S(1)}, u32[]{:S(2)}, u32[]{:S(2)}) collective-permute-start(f32[32,128]{1,0:T(8,128)S(1)} %pad_maximum_fusion.2), channel_id=1, source_target_pairs={{0,8},{1,9},{2,10},{3,11},{4,12},{5,13},{6,14},{7,15},{8,0},{9,1},... | collective-permute-start | bytes 49160 | tf_op jit(solution)/shard_map/ppermute | solution.py:75
  22.1 0.7 collective-permute-start.3
  22.7 0.1 collective-permute-start.1
  22.9 0.1 fusion.119
  23.0 4.2 %fusion.16 = f32[64,1024]{1,0:T(8,128)S(1)} fusion(f32[64,1024]{1,0:T(8,128)S(1)} %collective-permute-done, f32[1024,2048]{1,0:T(8,128)} %param.6, f32[1024]{0:T(1024)S(1)} %fusion.71), kind=kOutput, calls=%fused_computation.16 | convolution fusion | flops 402718720 | bytes 4722688 | tf_op jit(solution)/shard_map/dot_general | solution.py:90
  27.3 0.8 collective-permute-start.6
  28.1 0.5 collective-permute-done.1
  28.6 4.2 %fusion.25 = f32[64,1024]{1,0:T(8,128)S(1)} fusion(f32[64,1024]{1,0:T(8,128)S(1)} %fusion.16, f32[64,1024]{1,0:T(8,128)S(1)} %collective-permute-done.1, f32[1024,2048]{1,0:T(8,128)} %param.6, f32[1024]{0:T(1024)S(1)} %fusion.72), kind=kOutput, calls=%fused_computation.19 | convolution fusion | flops 402784256 | bytes 4984832 | tf_op jit(solution)/shard_map/dot_general | solution.py:90
  32.8 0.7 bitcast_bitcast_fusion.1
  33.6 35.0 %all-to-all-start = ((f32[8,64,128]{2,1,0:T(8,128)}), f32[8,64,128]{2,1,0:T(8,128)S(1)}, u32[]{:S(2)}, u32[]{:S(2)}) async-start(f32[8,64,128]{2,1,0:T(8,128)} %bitcast_bitcast_fusion.1), calls=%async_computation | async-start | bytes 524288 | tf_op jit(solution)/shard_map/all_to_all | solution.py:32
  68.7 4.4 %collective-permute-start.7 = (f32[32,128]{1,0:T(8,128)S(1)}, f32[32,128]{1,0:T(8,128)S(1)}, u32[]{:S(2)}, u32[]{:S(2)}) collective-permute-start(f32[32,128]{1,0:T(8,128)S(1)} %add.92), channel_id=1, source_target_pairs={{0,64},{1,65},{2,66},{3,67},{4,68},{5,69},{6,70},{7,71},{8,72},{9,... | collective-permute-start | bytes 49160 | tf_op jit(solution)/shard_map/ppermute | solution.py:75
  73.1 2.1 collective-permute-done.7
  75.3 2.4 %collective-permute-start.8 = (f32[32,128]{1,0:T(8,128)S(1)}, f32[32,128]{1,0:T(8,128)S(1)}, u32[]{:S(2)}, u32[]{:S(2)}) collective-permute-start(f32[32,128]{1,0:T(8,128)S(1)} %add.93), channel_id=1, source_target_pairs={{0,128},{1,129},{2,130},{3,131},{4,132},{5,133},{6,134},{7,135},{8... | collective-permute-start | bytes 49160 | tf_op jit(solution)/shard_map/ppermute | solution.py:75
  77.6 1.7 collective-permute-done.8
  79.5 12.0 %all_to_all.25 = f32[8,96,128]{2,1,0:T(8,128)S(1)} all-to-all(f32[8,96,128]{2,1,0:T(8,128)S(1)} %broadcast_in_dim.6), channel_id=1, replica_groups={{0,1,2,3,4,5,6,7},{8,9,10,11,12,13,14,15},{16,17,18,19,20,21,22,23},{24..., dimensions={0} | all-to-all | bytes 786432 | tf_op jit(solution)/shard_map/all_to_all | solution.py:32
  91.5 0.4 fusion.35
  92.0 0.4 fusion.96
  92.3 3.6 %fusion.2 = f32[64,1024]{1,0:T(8,128)S(1)} fusion(f32[1024,2048]{1,0:T(8,128)} %param.6, f32[64,1024]{1,0:T(8,128)S(1)} %fusion.35, f32[1024]{0:T(1024)S(1)} %fusion.72), kind=kOutput, calls=%fused_computation.2 | convolution fusion | flops 402718720 | bytes 4722688 | tf_op jit(solution)/shard_map/dot_general | solution.py:101
  96.0 3.6 %fusion.10 = f32[64,1024]{1,0:T(8,128)S(1)} fusion(f32[1024,2048]{1,0:T(8,128)} %param.6, f32[64,1024]{1,0:T(8,128)S(1)} %fusion.35, f32[1024]{0:T(1024)S(1)} %fusion.71), kind=kOutput, calls=%fused_computation.10 | convolution fusion | flops 402718720 | bytes 4722688 | tf_op jit(solution)/shard_map/dot_general | solution.py:101
  99.6 0.7 collective-permute-start.9
  100.3 6.3 %collective-permute-start.10 = (f32[64,1024]{1,0:T(8,128)S(1)}, f32[64,1024]{1,0:T(8,128)S(1)}, u32[]{:S(2)}, u32[]{:S(2)}) collective-permute-start(f32[64,1024]{1,0:T(8,128)S(1)} %fusion.2), channel_id=1, source_target_pairs={{0,8},{1,9},{2,10},{3,11},{4,12},{5,13},{6,14},{7,15},{8,16},{9,17... | collective-permute-start | bytes 786440 | tf_op jit(solution)/shard_map/ppermute | solution.py:75
  106.6 0.4 convolution_multiply_fusion.2
  106.9 2.9 %collective-permute-done.10 = f32[64,1024]{1,0:T(8,128)S(1)} collective-permute-done((f32[64,1024]{1,0:T(8,128)S(1)}, f32[64,1024]{1,0:T(8,128)S(1)}, u32[]{:S(2)}, u32[]{:S(2)}) %collective-permute-start.10) | collective-permute-done | bytes 262176 | tf_op jit(solution)/shard_map/ppermute | solution.py:75
  109.9 0.4 fusion.95
  110.6 0.1 maximum_maximum_fusion
  110.7 7.0 %collective-permute-start.11 = (f32[64,128]{1,0:T(8,128)S(1)}, f32[64,128]{1,0:T(8,128)S(1)}, u32[]{:S(2)}, u32[]{:S(2)}) collective-permute-start(f32[64,128]{1,0:T(8,128)S(1)} %maximum_maximum_fusion), channel_id=1, source_target_pairs={{0,8},{1,9},{2,10},{3,11},{4,12},{5,13},{6,14},{7,15},{8,0},{9,1},... | collective-permute-start | bytes 98312 | tf_op jit(solution)/shard_map/ppermute | solution.py:75
  117.7 0.9 collective-permute-done.11
  118.5 0.1 fusion.118
  118.7 2.8 %collective-permute-done.12 = f32[64,128]{1,0:T(8,128)S(1)} collective-permute-done((f32[64,128]{1,0:T(8,128)S(1)}, f32[64,128]{1,0:T(8,128)S(1)}, u32[]{:S(2)}, u32[]{:S(2)}) %collective-permute-start.12) | collective-permute-done | bytes 32800 | tf_op jit(solution)/shard_map/ppermute | solution.py:75
  121.5 0.7 collective-permute-start.17
  122.2 1.6 collective-permute-start.16
  123.7 1.4 collective-permute-done.13
  125.2 2.3 %collective-permute-start.14 = (f32[64,128]{1,0:T(8,128)S(1)}, f32[64,128]{1,0:T(8,128)S(1)}, u32[]{:S(2)}, u32[]{:S(2)}) collective-permute-start(f32[64,128]{1,0:T(8,128)S(1)} %add.101), channel_id=1, source_target_pairs={{0,64},{1,65},{2,66},{3,67},{4,68},{5,69},{6,70},{7,71},{8,72},{9,... | collective-permute-start | bytes 98312 | tf_op jit(solution)/shard_map/ppermute | solution.py:75
  127.5 4.2 %fusion.19 = f32[64,1024]{1,0:T(8,128)S(1)} fusion(f32[64,1024]{1,0:T(8,128)S(1)} %collective-permute-done.9, f32[1024,2048]{1,0:T(8,128)} %param.6, f32[1024]{0:T(1024)S(1)} %fusion.71), kind=kOutput, calls=%fused_computation.17 | convolution fusion | flops 402718720 | bytes 4722688 | tf_op jit(solution)/shard_map/dot_general | solution.py:90
  131.7 0.1 collective-permute-done.14
  131.8 2.5 %collective-permute-start.15 = (f32[64,128]{1,0:T(8,128)S(1)}, f32[64,128]{1,0:T(8,128)S(1)}, u32[]{:S(2)}, u32[]{:S(2)}) collective-permute-start(f32[64,128]{1,0:T(8,128)S(1)} %add.102), channel_id=1, source_target_pairs={{0,128},{1,129},{2,130},{3,131},{4,132},{5,133},{6,134},{7,135},{8... | collective-permute-start | bytes 98312 | tf_op jit(solution)/shard_map/ppermute | solution.py:75
  134.4 4.2 %fusion.31 = f32[64,1024]{1,0:T(8,128)S(1)} fusion(f32[64,1024]{1,0:T(8,128)S(1)} %fusion.19, f32[64,1024]{1,0:T(8,128)S(1)} %collective-permute-done.16, f32[1024,2048]{1,0:T(8,128)} %param.6, f32[1024]{0:T(1024)S(1)} %fusion.72), kind=kOutput, calls=%fused_computation.21 | convolution fusion | flops 402784256 | bytes 4984832 | tf_op jit(solution)/shard_map/dot_general | solution.py:90
  138.6 0.7 bitcast_bitcast_fusion
  139.3 29.1 %all-to-all-start.2 = ((f32[8,64,128]{2,1,0:T(8,128)}), f32[8,64,128]{2,1,0:T(8,128)S(1)}, u32[]{:S(2)}, u32[]{:S(2)}) async-start(f32[8,64,128]{2,1,0:T(8,128)} %bitcast_bitcast_fusion), calls=%async_computation.2 | async-start | bytes 524288 | tf_op jit(solution)/shard_map/all_to_all | solution.py:32
  168.6 6.0 %all-to-all-done.2 = f32[8,64,128]{2,1,0:T(8,128)S(1)} async-done(((f32[8,64,128]{2,1,0:T(8,128)}), f32[8,64,128]{2,1,0:T(8,128)S(1)}, u32[]{:S(2)}, u32[]{:S(2)}) %all-to-all-start.2) | async-done | bytes 262176 | tf_op jit(solution)/shard_map/all_to_all | solution.py:32
  174.6 0.2 fusion.59
  174.9 0.8 broadcast_in_dim.7
  175.6 3.5 %all-to-all-start.3 = ((f32[8,96,128]{2,1,0:T(8,128)}), f32[8,96,128]{2,1,0:T(8,128)S(1)}, u32[]{:S(2)}, u32[]{:S(2)}) async-start(f32[8,96,128]{2,1,0:T(8,128)} %broadcast_in_dim.7), calls=%async_computation.3 | async-start | bytes 786432 | tf_op jit(solution)/shard_map/all_to_all | solution.py:32
  179.1 0.4 fusion.83
  179.5 6.4 %all-to-all-done.3 = f32[8,96,128]{2,1,0:T(8,128)S(1)} async-done(((f32[8,96,128]{2,1,0:T(8,128)}), f32[8,96,128]{2,1,0:T(8,128)S(1)}, u32[]{:S(2)}, u32[]{:S(2)}) %all-to-all-start.3) | async-done | bytes 393248 | tf_op jit(solution)/shard_map/all_to_all | solution.py:32
  186.0 0.2 fusion.52
  186.2 0.2 fusion.84
  186.4 0.4 fusion.34
  186.8 0.4 fusion.97
  187.2 0.1 pad_maximum_fusion.3
  187.3 18.0 %all_to_all.26 = f32[16,32,128]{2,1,0:T(8,128)S(1)} all-to-all(f32[16,32,128]{2,1,0:T(8,128)S(1)} %broadcast_in_dim.8), channel_id=1, replica_groups={{0,16,32,48,64,80,96,112,128,144,160,176,192,208,224,240},{1,17,33,49,6..., dimensions={0} | all-to-all | bytes 524288 | tf_op jit(solution)/shard_map/all_to_all | solution.py:32
  205.3 7.6 %collective-permute-start.18 = (f32[32,128]{1,0:T(8,128)S(1)}, f32[32,128]{1,0:T(8,128)S(1)}, u32[]{:S(2)}, u32[]{:S(2)}) collective-permute-start(f32[32,128]{1,0:T(8,128)S(1)} %reduce_sum.49), channel_id=1, source_target_pairs={{0,8},{1,9},{2,10},{3,11},{4,12},{5,13},{6,14},{7,15},{8,0},{9,1},... | collective-permute-start | bytes 49160 | tf_op jit(solution)/shard_map/ppermute | solution.py:75
  213.0 0.8 collective-permute-done.18
  213.9 1.1 fusion.49
  (63 shorter events, 1.3 us)
Async XLA Ops:
  0.6 14.9 %copy-start = (f32[64,1024]{1,0:T(8,128)S(1)}, f32[64,1024]{1,0:T(8,128)}, u32[]{:S(2)}) copy-start(f32[64,1024]{1,0:T(8,128)} %param.5) | copy-start | bytes 786436
  0.6 14.9 %copy-start.2 = (f32[1024]{0:T(1024)S(1)}, f32[1024]{0:T(1024)}, u32[]{:S(2)}) copy-start(f32[1024]{0:T(1024)} %param.8) | copy-start | bytes 12292
  0.7 15.3 %collective-permute-start = (f32[64,1024]{1,0:T(8,128)}, f32[64,1024]{1,0:T(8,128)S(1)}, u32[]{:S(2)}, u32[]{:S(2)}) collective-permute-start(f32[64,1024]{1,0:T(8,128)} %param.5), channel_id=1, source_target_pairs={{0,0},{1,241},{2,226},{3,211},{4,196},{5,181},{6,166},{7,151},{8,8... | collective-permute-start | bytes 786440 | tf_op jit(solution)/shard_map/ppermute | solution.py:75
  8.1 7.8 %collective-permute-start.2 = (f32[64,1024]{1,0:T(8,128)S(1)}, f32[64,1024]{1,0:T(8,128)S(1)}, u32[]{:S(2)}, u32[]{:S(2)}) collective-permute-start(f32[64,1024]{1,0:T(8,128)S(1)} %fusion.4), channel_id=1, source_target_pairs={{0,8},{1,9},{2,10},{3,11},{4,12},{5,13},{6,14},{7,15},{8,16},{9,17... | collective-permute-start | bytes 786440 | tf_op jit(solution)/shard_map/ppermute | solution.py:75
  11.8 65.8 %copy-start.3 = (f32[1024]{0:T(1024)S(1)}, f32[1024]{0:T(1024)}, u32[]{:S(2)}) copy-start(f32[1024]{0:T(1024)} %param.9) | copy-start | bytes 12292
  16.5 6.4 %collective-permute-start.4 = (f32[32,128]{1,0:T(8,128)S(1)}, f32[32,128]{1,0:T(8,128)S(1)}, u32[]{:S(2)}, u32[]{:S(2)}) collective-permute-start(f32[32,128]{1,0:T(8,128)S(1)} %pad_maximum_fusion.2), channel_id=1, source_target_pairs={{0,8},{1,9},{2,10},{3,11},{4,12},{5,13},{6,14},{7,15},{8,0},{9,1},... | collective-permute-start | bytes 49160 | tf_op jit(solution)/shard_map/ppermute | solution.py:75
  22.1 10.8 %collective-permute-start.3 = (f32[64,1024]{1,0:T(8,128)S(1)}, f32[64,1024]{1,0:T(8,128)S(1)}, u32[]{:S(2)}, u32[]{:S(2)}) collective-permute-start(f32[64,1024]{1,0:T(8,128)S(1)} %add.85), channel_id=1, source_target_pairs={{0,0},{241,1},{226,2},{211,3},{196,4},{181,5},{166,6},{151,7},{8,8... | collective-permute-start | bytes 786440 | tf_op jit(solution)/shard_map/ppermute | solution.py:75
  22.7 5.9 %collective-permute-start.1 = (f32[64,1024]{1,0:T(8,128)S(1)}, f32[64,1024]{1,0:T(8,128)S(1)}, u32[]{:S(2)}, u32[]{:S(2)}) collective-permute-start(f32[64,1024]{1,0:T(8,128)S(1)} %collective-permute-done), channel_id=1, source_target_pairs={{8,0},{9,1},{10,2},{11,3},{12,4},{13,5},{14,6},{15,7},{16,8},{17,9... | collective-permute-start | bytes 786440 | tf_op jit(solution)/shard_map/ppermute | solution.py:75
  23.0 4.3 %collective-permute-start.5 = (f32[32,128]{1,0:T(8,128)S(1)}, f32[32,128]{1,0:T(8,128)S(1)}, u32[]{:S(2)}, u32[]{:S(2)}) collective-permute-start(f32[32,128]{1,0:T(8,128)S(1)} %fusion.119), channel_id=1, source_target_pairs={{0,16},{1,17},{2,18},{3,19},{4,20},{5,21},{6,22},{7,23},{8,24},{9,... | collective-permute-start | bytes 49160 | tf_op jit(solution)/shard_map/ppermute | solution.py:75
  27.3 41.4 %collective-permute-start.6 = (f32[32,128]{1,0:T(8,128)S(1)}, f32[32,128]{1,0:T(8,128)S(1)}, u32[]{:S(2)}, u32[]{:S(2)}) collective-permute-start(f32[32,128]{1,0:T(8,128)S(1)} %add.91), channel_id=1, source_target_pairs={{0,32},{1,33},{2,34},{3,35},{4,36},{5,37},{6,38},{7,39},{8,40},{9,... | collective-permute-start | bytes 49160 | tf_op jit(solution)/shard_map/ppermute | solution.py:75
  33.6 45.8 %all-to-all-start = ((f32[8,64,128]{2,1,0:T(8,128)}), f32[8,64,128]{2,1,0:T(8,128)S(1)}, u32[]{:S(2)}, u32[]{:S(2)}) async-start(f32[8,64,128]{2,1,0:T(8,128)} %bitcast_bitcast_fusion.1), calls=%async_computation | async-start | bytes 524288 | tf_op jit(solution)/shard_map/all_to_all | solution.py:32
  68.7 6.6 %collective-permute-start.7 = (f32[32,128]{1,0:T(8,128)S(1)}, f32[32,128]{1,0:T(8,128)S(1)}, u32[]{:S(2)}, u32[]{:S(2)}) collective-permute-start(f32[32,128]{1,0:T(8,128)S(1)} %add.92), channel_id=1, source_target_pairs={{0,64},{1,65},{2,66},{3,67},{4,68},{5,69},{6,70},{7,71},{8,72},{9,... | collective-permute-start | bytes 49160 | tf_op jit(solution)/shard_map/ppermute | solution.py:75
  75.3 4.1 %collective-permute-start.8 = (f32[32,128]{1,0:T(8,128)S(1)}, f32[32,128]{1,0:T(8,128)S(1)}, u32[]{:S(2)}, u32[]{:S(2)}) collective-permute-start(f32[32,128]{1,0:T(8,128)S(1)} %add.93), channel_id=1, source_target_pairs={{0,128},{1,129},{2,130},{3,131},{4,132},{5,133},{6,134},{7,135},{8... | collective-permute-start | bytes 49160 | tf_op jit(solution)/shard_map/ppermute | solution.py:75
  99.6 10.3 %collective-permute-start.9 = (f32[64,1024]{1,0:T(8,128)S(1)}, f32[64,1024]{1,0:T(8,128)S(1)}, u32[]{:S(2)}, u32[]{:S(2)}) collective-permute-start(f32[64,1024]{1,0:T(8,128)S(1)} %fusion.35), channel_id=1, source_target_pairs={{0,0},{1,241},{2,226},{3,211},{4,196},{5,181},{6,166},{7,151},{8,8... | collective-permute-start | bytes 786440 | tf_op jit(solution)/shard_map/ppermute | solution.py:75
  100.3 9.6 %collective-permute-start.10 = (f32[64,1024]{1,0:T(8,128)S(1)}, f32[64,1024]{1,0:T(8,128)S(1)}, u32[]{:S(2)}, u32[]{:S(2)}) collective-permute-start(f32[64,1024]{1,0:T(8,128)S(1)} %fusion.2), channel_id=1, source_target_pairs={{0,8},{1,9},{2,10},{3,11},{4,12},{5,13},{6,14},{7,15},{8,16},{9,17... | collective-permute-start | bytes 786440 | tf_op jit(solution)/shard_map/ppermute | solution.py:75
  110.7 7.9 %collective-permute-start.11 = (f32[64,128]{1,0:T(8,128)S(1)}, f32[64,128]{1,0:T(8,128)S(1)}, u32[]{:S(2)}, u32[]{:S(2)}) collective-permute-start(f32[64,128]{1,0:T(8,128)S(1)} %maximum_maximum_fusion), channel_id=1, source_target_pairs={{0,8},{1,9},{2,10},{3,11},{4,12},{5,13},{6,14},{7,15},{8,0},{9,1},... | collective-permute-start | bytes 98312 | tf_op jit(solution)/shard_map/ppermute | solution.py:75
  118.6 2.8 %collective-permute-start.12 = (f32[64,128]{1,0:T(8,128)S(1)}, f32[64,128]{1,0:T(8,128)S(1)}, u32[]{:S(2)}, u32[]{:S(2)}) collective-permute-start(f32[64,128]{1,0:T(8,128)S(1)} %fusion.118), channel_id=1, source_target_pairs={{0,16},{1,17},{2,18},{3,19},{4,20},{5,21},{6,22},{7,23},{8,24},{9,... | collective-permute-start | bytes 98312 | tf_op jit(solution)/shard_map/ppermute | solution.py:75
  121.4 3.7 %collective-permute-start.13 = (f32[64,128]{1,0:T(8,128)S(1)}, f32[64,128]{1,0:T(8,128)S(1)}, u32[]{:S(2)}, u32[]{:S(2)}) collective-permute-start(f32[64,128]{1,0:T(8,128)S(1)} %add.100), channel_id=1, source_target_pairs={{0,32},{1,33},{2,34},{3,35},{4,36},{5,37},{6,38},{7,39},{8,40},{9,... | collective-permute-start | bytes 98312 | tf_op jit(solution)/shard_map/ppermute | solution.py:75
  121.5 17.1 %collective-permute-start.17 = (f32[64,1024]{1,0:T(8,128)S(1)}, f32[64,1024]{1,0:T(8,128)S(1)}, u32[]{:S(2)}, u32[]{:S(2)}) collective-permute-start(f32[64,1024]{1,0:T(8,128)S(1)} %add.96), channel_id=1, source_target_pairs={{0,0},{241,1},{226,2},{211,3},{196,4},{181,5},{166,6},{151,7},{8,8... | collective-permute-start | bytes 786440 | tf_op jit(solution)/shard_map/ppermute | solution.py:75
  122.2 12.2 %collective-permute-start.16 = (f32[64,1024]{1,0:T(8,128)S(1)}, f32[64,1024]{1,0:T(8,128)S(1)}, u32[]{:S(2)}, u32[]{:S(2)}) collective-permute-start(f32[64,1024]{1,0:T(8,128)S(1)} %collective-permute-done.9), channel_id=1, source_target_pairs={{8,0},{9,1},{10,2},{11,3},{12,4},{13,5},{14,6},{15,7},{16,8},{17,9... | collective-permute-start | bytes 786440 | tf_op jit(solution)/shard_map/ppermute | solution.py:75
  125.2 6.7 %collective-permute-start.14 = (f32[64,128]{1,0:T(8,128)S(1)}, f32[64,128]{1,0:T(8,128)S(1)}, u32[]{:S(2)}, u32[]{:S(2)}) collective-permute-start(f32[64,128]{1,0:T(8,128)S(1)} %add.101), channel_id=1, source_target_pairs={{0,64},{1,65},{2,66},{3,67},{4,68},{5,69},{6,70},{7,71},{8,72},{9,... | collective-permute-start | bytes 98312 | tf_op jit(solution)/shard_map/ppermute | solution.py:75
  131.8 36.6 %collective-permute-start.15 = (f32[64,128]{1,0:T(8,128)S(1)}, f32[64,128]{1,0:T(8,128)S(1)}, u32[]{:S(2)}, u32[]{:S(2)}) collective-permute-start(f32[64,128]{1,0:T(8,128)S(1)} %add.102), channel_id=1, source_target_pairs={{0,128},{1,129},{2,130},{3,131},{4,132},{5,133},{6,134},{7,135},{8... | collective-permute-start | bytes 98312 | tf_op jit(solution)/shard_map/ppermute | solution.py:75
  139.3 35.2 %all-to-all-start.2 = ((f32[8,64,128]{2,1,0:T(8,128)}), f32[8,64,128]{2,1,0:T(8,128)S(1)}, u32[]{:S(2)}, u32[]{:S(2)}) async-start(f32[8,64,128]{2,1,0:T(8,128)} %bitcast_bitcast_fusion), calls=%async_computation.2 | async-start | bytes 524288 | tf_op jit(solution)/shard_map/all_to_all | solution.py:32
  175.6 10.2 %all-to-all-start.3 = ((f32[8,96,128]{2,1,0:T(8,128)}), f32[8,96,128]{2,1,0:T(8,128)S(1)}, u32[]{:S(2)}, u32[]{:S(2)}) async-start(f32[8,96,128]{2,1,0:T(8,128)} %broadcast_in_dim.7), calls=%async_computation.3 | async-start | bytes 786432 | tf_op jit(solution)/shard_map/all_to_all | solution.py:32
  186.4 28.6 %copy-start.1 = (f32[64,64]{1,0:T(8,128)}, f32[64,64]{1,0:T(8,128)S(1)}, u32[]{:S(2)}) copy-start(f32[64,64]{1,0:T(8,128)S(1)} %fusion.84) | copy-start | bytes 49156
  205.3 8.5 %collective-permute-start.18 = (f32[32,128]{1,0:T(8,128)S(1)}, f32[32,128]{1,0:T(8,128)S(1)}, u32[]{:S(2)}, u32[]{:S(2)}) collective-permute-start(f32[32,128]{1,0:T(8,128)S(1)} %reduce_sum.49), channel_id=1, source_target_pairs={{0,8},{1,9},{2,10},{3,11},{4,12},{5,13},{6,14},{7,15},{8,0},{9,1},... | collective-permute-start | bytes 49160 | tf_op jit(solution)/shard_map/ppermute | solution.py:75
where the time goes:
time: 216 us; the launch traced here: 215 us
  starting transfers between devices  115 us (53%)
  matrix products  36.7 us (17%)
  blocking collectives  30 us (14%)
  waiting for transfers between devices  25.7 us (12%)
  other arithmetic  3.4 us (2%)
  local copies, waits for them, and re-layouts  2.99 us (1%)
    all_to_all x3, starting transfers between devices, exchange(): lax.all_to_all(array, AXES, 0, 0, axis_index_groups=groups, tiled=True)  67.6 us
    ppermute x19, starting transfers between devices, permuted(): return lax.ppermute(array, AXES, pairs)  47.6 us
    all_to_all x2, blocking collectives, exchange(): lax.all_to_all(array, AXES, 0, 0, axis_index_groups=groups, tiled=True)  30 us
    dot_general x4, matrix products, direct_product(): lax.dot_general(piece, block, (((1,), (1,)), ((), ())), precision=lax.Pre...  16.9 us
    dot_general x4, matrix products, back_product(): jnp.dot(vectors * mask, block, precision=lax.Precision.HIGH, preferred_el...  14.6 us
    ppermute x19, waiting for transfers between devices, permuted(): return lax.ppermute(array, AXES, pairs)  13.4 us
    all_to_all x3, waiting for transfers between devices, exchange(): lax.all_to_all(array, AXES, 0, 0, axis_index_groups=groups, tiled=True)  12.4 us
  transfers between devices with their start and end apart: 22, of which 12 were waited for; matrix products, arithmetic and copies ran while one was open for 14% of the time, Pallas kernels for 0%

commit v1 on v0

--- a/solution.py
+++ b/solution.py
@@ -22,7 +22,10 @@
             bit: [(number(row, p), number(row ^ bit, p)) for row, p in every]
             for bit in (1 << n for n in range(rows.bit_length() - 1))
         }
-        self.fetch = [(number(row, p), number(row - per_device * p, p)) for row, p in every]
+        turn = lambda row: row // 2 * 2 % offs
+        self.fetch = [
+            (number(row, p ^ turn(row)), number(row - per_device * p, p)) for row, p in every
+        ]
         self.back = [(b, a) for a, b in self.fetch]
         self.up = [(number(row, p), number(row + 1, p)) for row, p in every]
         self.down = [(b, a) for a, b in self.up]
@@ -76,8 +79,9 @@
 
 
 def row_total(part, lay):
-    for pairs in lay.flip.values():
-        part = part + permuted(part, pairs)
+    far = lay.rows // 2
+    for bit in [1, far] + [bit for bit in lay.flip if bit not in (1, far)]:
+        part = part + permuted(part, lay.flip[bit])
     return part
 
 
@@ -120,14 +124,17 @@
     def products(vecs, extra):
         near = permuted(vecs, lay.fetch)
         up = permuted(back_product(vecs, blocks[1], masks[1]), lay.up)
-        back = lax.optimization_barrier(back_product(vecs, blocks[0], masks[0])) + up
+        back = back_product(vecs, blocks[0], masks[0])
+        back = lax.optimization_barrier(back) + up
         returned = permuted(back, lay.back)
         far = permuted(near, lay.down)
         pair = gram(near, back)
         share = folded(pair + pair.T + gram(vecs, energies * vecs) * (1.0 / offs))
+        first = direct_product(near, blocks[0], masks[0])
+        second = direct_product(far, blocks[1], masks[1])
+        first, second = lax.optimization_barrier(first), lax.optimization_barrier(second)
         share = row_total(jnp.concatenate([share] + extra, axis=0), lay)
-        direct = direct_product(near, blocks[0], masks[0]) + direct_product(far, blocks[1], masks[1])
-        return lax.optimization_barrier(direct) + returned, share
+        return first + second + returned, share
 
     def spread(chunk, share):
         got = sent_to_all(jnp.concatenate([chunk, share], axis=0), lay.row)

time: 216 us -> 200 us (0.926)
  starting transfers between devices: 115 us -> 92.4 us
  waiting for transfers between devices: 25.7 us -> 31.8 us
    all_to_all x3, starting transfers between devices: 67.6 us -> 32.6 us  [exchange(): lax.all_to_all(array, AXES, 0, 0, axis_index_groups=groups, tiled=True)]
    ppermute x19, starting transfers between devices: 47.6 us -> 59.8 us  [permuted(): return lax.ppermute(array, AXES, pairs)]
    ppermute x19, waiting for transfers between devices: 13.4 us -> 19.4 us  [permuted(): return lax.ppermute(array, AXES, pairs)]
  transfers between devices with their start and end apart: 22 -> 22, of which waited for: 12 -> 10; matrix products, arithmetic and copies ran while one was open for 14% -> 15% of each run, Pallas kernels for 0% -> 0%
where the time goes in v1:
time: 200 us
  starting transfers between devices  92.4 us (46%)
  matrix products  36.7 us (18%)
  waiting for transfers between devices  31.8 us (16%)
  blocking collectives  31.3 us (16%)
  other arithmetic  3.42 us (2%)
  local copies, waits for them, and re-layouts  2.99 us (1%)
    ppermute x19, starting transfers between devices, permuted(): return lax.ppermute(array, AXES, pairs)  59.8 us
    all_to_all x3, starting transfers between devices, exchange(): lax.all_to_all(array, AXES, 0, 0, axis_index_groups=groups, tiled=True)  32.6 us
    all_to_all x2, blocking collectives, exchange(): lax.all_to_all(array, AXES, 0, 0, axis_index_groups=groups, tiled=True)  31.3 us
    ppermute x19, waiting for transfers between devices, permuted(): return lax.ppermute(array, AXES, pairs)  19.4 us
    dot_general x4, matrix products, direct_product(): lax.dot_general(piece, block, (((1,), (1,)), ((), ())), precision=lax.Pre...  16.9 us
    dot_general x4, matrix products, back_product(): jnp.dot(vectors * mask, block, precision=lax.Precision.HIGH, preferred_el...  14.6 us
    all_to_all x3, waiting for transfers between devices, exchange(): lax.all_to_all(array, AXES, 0, 0, axis_index_groups=groups, tiled=True)  12.4 us
  transfers between devices with their start and end apart: 22, of which 10 were waited for; matrix products, arithmetic and copies ran while one was open for 15% of the time, Pallas kernels for 0%

profile of v1, /device:TPU:1, one launch (start us, length us, event | category | flops | bytes accessed | tf_op | source)
XLA Modules:
  0.0 199.6 jit_solution(15155923210475127950)
XLA Ops:
  0.7 1.7 collective-permute-start
  2.4 1.3 fusion.87
  3.7 0.6 fusion.66
  4.4 3.7 %fusion.4 = f32[64,1024]{1,0:T(8,128)S(1)} fusion(f32[1024,2048]{1,0:T(8,128)} %param.6, f32[64,1024]{1,0:T(8,128)} %param.5, f32[1024]{0:T(1024)S(1)} %fusion.66), kind=kOutput, calls=%fused_computation.4 | convolution fusion | flops 402718720 | bytes 4722688 | tf_op jit(solution)/shard_map/dot_general | solution.py:105
  8.1 12.3 %collective-permute-start.2 = (f32[64,1024]{1,0:T(8,128)S(1)}, f32[64,1024]{1,0:T(8,128)S(1)}, u32[]{:S(2)}, u32[]{:S(2)}) collective-permute-start(f32[64,1024]{1,0:T(8,128)S(1)} %fusion.4), channel_id=1, source_target_pairs={{0,8},{1,9},{2,10},{3,11},{4,12},{5,13},{6,14},{7,15},{8,16},{9,17... | collective-permute-start | bytes 786440 | tf_op jit(solution)/shard_map/ppermute | solution.py:78
  20.3 0.6 fusion.65
  21.0 3.7 %fusion.12 = f32[64,1024]{1,0:T(8,128)S(1)} fusion(f32[1024,2048]{1,0:T(8,128)} %param.6, f32[64,1024]{1,0:T(8,128)} %param.5, f32[1024]{0:T(1024)S(1)} %fusion.65), kind=kOutput, calls=%fused_computation.12 | convolution fusion | flops 402718720 | bytes 4722688 | tf_op jit(solution)/shard_map/dot_general | solution.py:105
  24.7 0.4 fusion.30
  25.2 0.4 fusion.88
  25.6 0.1 pad_maximum_fusion.2
  25.7 3.2 %collective-permute-start.4 = (f32[32,128]{1,0:T(8,128)S(1)}, f32[32,128]{1,0:T(8,128)S(1)}, u32[]{:S(2)}, u32[]{:S(2)}) collective-permute-start(f32[32,128]{1,0:T(8,128)S(1)} %pad_maximum_fusion.2), channel_id=1, source_target_pairs={{0,8},{1,9},{2,10},{3,11},{4,12},{5,13},{6,14},{7,15},{8,0},{9,1},... | collective-permute-start | bytes 49160 | tf_op jit(solution)/shard_map/ppermute | solution.py:78
  29.0 0.7 collective-permute-start.3
  29.6 0.1 collective-permute-start.1
  29.8 0.1 fusion.113
  29.9 0.2 collective-permute-start.5
  30.1 4.2 %fusion.16 = f32[64,1024]{1,0:T(8,128)S(1)} fusion(f32[64,1024]{1,0:T(8,128)S(1)} %collective-permute-done, f32[1024,2048]{1,0:T(8,128)} %param.6, f32[1024]{0:T(1024)S(1)} %fusion.65), kind=kOutput, calls=%fused_computation.16 | convolution fusion | flops 402718720 | bytes 4722688 | tf_op jit(solution)/shard_map/dot_general | solution.py:94
  34.4 2.5 %collective-permute-start.6 = (f32[32,128]{1,0:T(8,128)S(1)}, f32[32,128]{1,0:T(8,128)S(1)}, u32[]{:S(2)}, u32[]{:S(2)}) collective-permute-start(f32[32,128]{1,0:T(8,128)S(1)} %add.91), channel_id=1, source_target_pairs={{0,16},{1,17},{2,18},{3,19},{4,20},{5,21},{6,22},{7,23},{8,24},{9,... | collective-permute-start | bytes 49160 | tf_op jit(solution)/shard_map/ppermute | solution.py:78
  36.9 4.2 %fusion.22 = f32[64,1024]{1,0:T(8,128)S(1)} fusion(f32[64,1024]{1,0:T(8,128)S(1)} %collective-permute-done.1, f32[1024,2048]{1,0:T(8,128)} %param.6, f32[1024]{0:T(1024)S(1)} %fusion.66), kind=kOutput, calls=%fused_computation.18 | convolution fusion | flops 402718720 | bytes 4722688 | tf_op jit(solution)/shard_map/dot_general | solution.py:94
  41.1 0.7 bitcast_bitcast_fusion.1
  41.8 15.6 %all-to-all-start = ((f32[8,64,128]{2,1,0:T(8,128)}), f32[8,64,128]{2,1,0:T(8,128)S(1)}, u32[]{:S(2)}, u32[]{:S(2)}) async-start(f32[8,64,128]{2,1,0:T(8,128)} %bitcast_bitcast_fusion.1), calls=%async_computation | async-start | bytes 524288 | tf_op jit(solution)/shard_map/all_to_all | solution.py:35
  57.5 6.0 %collective-permute-start.7 = (f32[32,128]{1,0:T(8,128)S(1)}, f32[32,128]{1,0:T(8,128)S(1)}, u32[]{:S(2)}, u32[]{:S(2)}) collective-permute-start(f32[32,128]{1,0:T(8,128)S(1)} %add.92), channel_id=1, source_target_pairs={{0,32},{1,33},{2,34},{3,35},{4,36},{5,37},{6,38},{7,39},{8,40},{9,... | collective-permute-start | bytes 49160 | tf_op jit(solution)/shard_map/ppermute | solution.py:78
  63.5 1.4 collective-permute-done.7
  65.0 4.2 %collective-permute-start.8 = (f32[32,128]{1,0:T(8,128)S(1)}, f32[32,128]{1,0:T(8,128)S(1)}, u32[]{:S(2)}, u32[]{:S(2)}) collective-permute-start(f32[32,128]{1,0:T(8,128)S(1)} %add.93), channel_id=1, source_target_pairs={{0,64},{1,65},{2,66},{3,67},{4,68},{5,69},{6,70},{7,71},{8,72},{9,... | collective-permute-start | bytes 49160 | tf_op jit(solution)/shard_map/ppermute | solution.py:78
  69.2 2.4 %collective-permute-done.8 = f32[32,128]{1,0:T(8,128)S(1)} collective-permute-done((f32[32,128]{1,0:T(8,128)S(1)}, f32[32,128]{1,0:T(8,128)S(1)}, u32[]{:S(2)}, u32[]{:S(2)}) %collective-permute-start.8) | collective-permute-done | bytes 16416 | tf_op jit(solution)/shard_map/ppermute | solution.py:78
  71.7 11.8 %all_to_all.25 = f32[8,96,128]{2,1,0:T(8,128)S(1)} all-to-all(f32[8,96,128]{2,1,0:T(8,128)S(1)} %broadcast_in_dim.6), channel_id=1, replica_groups={{0,1,2,3,4,5,6,7},{8,9,10,11,12,13,14,15},{16,17,18,19,20,21,22,23},{24..., dimensions={0} | all-to-all | bytes 786432 | tf_op jit(solution)/shard_map/all_to_all | solution.py:35
  83.6 0.4 fusion.29
  84.1 0.4 fusion.90
  84.4 3.6 %fusion.2 = f32[64,1024]{1,0:T(8,128)S(1)} fusion(f32[1024,2048]{1,0:T(8,128)} %param.6, f32[64,1024]{1,0:T(8,128)S(1)} %fusion.29, f32[1024]{0:T(1024)S(1)} %fusion.66), kind=kOutput, calls=%fused_computation.2 | convolution fusion | flops 402718720 | bytes 4722688 | tf_op jit(solution)/shard_map/dot_general | solution.py:105
  88.0 3.6 %fusion.10 = f32[64,1024]{1,0:T(8,128)S(1)} fusion(f32[1024,2048]{1,0:T(8,128)} %param.6, f32[64,1024]{1,0:T(8,128)S(1)} %fusion.29, f32[1024]{0:T(1024)S(1)} %fusion.65), kind=kOutput, calls=%fused_computation.10 | convolution fusion | flops 402718720 | bytes 4722688 | tf_op jit(solution)/shard_map/dot_general | solution.py:105
  91.7 0.7 collective-permute-start.9
  92.3 9.2 %collective-permute-start.10 = (f32[64,1024]{1,0:T(8,128)S(1)}, f32[64,1024]{1,0:T(8,128)S(1)}, u32[]{:S(2)}, u32[]{:S(2)}) collective-permute-start(f32[64,1024]{1,0:T(8,128)S(1)} %fusion.2), channel_id=1, source_target_pairs={{0,8},{1,9},{2,10},{3,11},{4,12},{5,13},{6,14},{7,15},{8,16},{9,17... | collective-permute-start | bytes 786440 | tf_op jit(solution)/shard_map/ppermute | solution.py:78
  101.6 0.4 convolution_multiply_fusion.2
  102.0 9.6 %collective-permute-done.10 = f32[64,1024]{1,0:T(8,128)S(1)} collective-permute-done((f32[64,1024]{1,0:T(8,128)S(1)}, f32[64,1024]{1,0:T(8,128)S(1)}, u32[]{:S(2)}, u32[]{:S(2)}) %collective-permute-start.10) | collective-permute-done | bytes 262176 | tf_op jit(solution)/shard_map/ppermute | solution.py:78
  111.7 0.4 fusion.89
  112.3 0.1 maximum_maximum_fusion
  112.4 3.6 %collective-permute-start.11 = (f32[64,128]{1,0:T(8,128)S(1)}, f32[64,128]{1,0:T(8,128)S(1)}, u32[]{:S(2)}, u32[]{:S(2)}) collective-permute-start(f32[64,128]{1,0:T(8,128)S(1)} %maximum_maximum_fusion), channel_id=1, source_target_pairs={{0,8},{1,9},{2,10},{3,11},{4,12},{5,13},{6,14},{7,15},{8,0},{9,1},... | collective-permute-start | bytes 98312 | tf_op jit(solution)/shard_map/ppermute | solution.py:78
  116.0 0.9 collective-permute-done.11
  116.9 0.1 fusion.112
  116.9 0.6 collective-permute-start.12
  117.5 3.7 %collective-permute-done.12 = f32[64,128]{1,0:T(8,128)S(1)} collective-permute-done((f32[64,128]{1,0:T(8,128)S(1)}, f32[64,128]{1,0:T(8,128)S(1)}, u32[]{:S(2)}, u32[]{:S(2)}) %collective-permute-start.12) | collective-permute-done | bytes 32800 | tf_op jit(solution)/shard_map/ppermute | solution.py:78
  121.3 0.7 collective-permute-start.17
  122.0 1.6 collective-permute-start.16
  123.6 0.4 collective-permute-done.13
  124.0 4.9 %collective-permute-start.14 = (f32[64,128]{1,0:T(8,128)S(1)}, f32[64,128]{1,0:T(8,128)S(1)}, u32[]{:S(2)}, u32[]{:S(2)}) collective-permute-start(f32[64,128]{1,0:T(8,128)S(1)} %add.101), channel_id=1, source_target_pairs={{0,32},{1,33},{2,34},{3,35},{4,36},{5,37},{6,38},{7,39},{8,40},{9,... | collective-permute-start | bytes 98312 | tf_op jit(solution)/shard_map/ppermute | solution.py:78
  128.9 4.2 %fusion.19 = f32[64,1024]{1,0:T(8,128)S(1)} fusion(f32[64,1024]{1,0:T(8,128)S(1)} %collective-permute-done.9, f32[1024,2048]{1,0:T(8,128)} %param.6, f32[1024]{0:T(1024)S(1)} %fusion.65), kind=kOutput, calls=%fused_computation.17 | convolution fusion | flops 402718720 | bytes 4722688 | tf_op jit(solution)/shard_map/dot_general | solution.py:94
  133.1 1.7 collective-permute-start.15
  134.8 4.2 %fusion.25 = f32[64,1024]{1,0:T(8,128)S(1)} fusion(f32[64,1024]{1,0:T(8,128)S(1)} %collective-permute-done.16, f32[1024,2048]{1,0:T(8,128)} %param.6, f32[1024]{0:T(1024)S(1)} %fusion.66), kind=kOutput, calls=%fused_computation.19 | convolution fusion | flops 402718720 | bytes 4722688 | tf_op jit(solution)/shard_map/dot_general | solution.py:94
  139.1 0.7 bitcast_bitcast_fusion
  139.8 13.5 %all-to-all-start.2 = ((f32[8,64,128]{2,1,0:T(8,128)}), f32[8,64,128]{2,1,0:T(8,128)S(1)}, u32[]{:S(2)}, u32[]{:S(2)}) async-start(f32[8,64,128]{2,1,0:T(8,128)} %bitcast_bitcast_fusion), calls=%async_computation.2 | async-start | bytes 524288 | tf_op jit(solution)/shard_map/all_to_all | solution.py:35
  153.5 6.0 %all-to-all-done.2 = f32[8,64,128]{2,1,0:T(8,128)S(1)} async-done(((f32[8,64,128]{2,1,0:T(8,128)}), f32[8,64,128]{2,1,0:T(8,128)S(1)}, u32[]{:S(2)}, u32[]{:S(2)}) %all-to-all-start.2) | async-done | bytes 262176 | tf_op jit(solution)/shard_map/all_to_all | solution.py:35
  159.5 0.2 fusion.53
  159.8 0.8 broadcast_in_dim.7
  160.5 3.5 %all-to-all-start.3 = ((f32[8,96,128]{2,1,0:T(8,128)}), f32[8,96,128]{2,1,0:T(8,128)S(1)}, u32[]{:S(2)}, u32[]{:S(2)}) async-start(f32[8,96,128]{2,1,0:T(8,128)} %broadcast_in_dim.7), calls=%async_computation.3 | async-start | bytes 786432 | tf_op jit(solution)/shard_map/all_to_all | solution.py:35
  164.0 0.4 fusion.77
  164.4 6.4 %all-to-all-done.3 = f32[8,96,128]{2,1,0:T(8,128)S(1)} async-done(((f32[8,96,128]{2,1,0:T(8,128)}), f32[8,96,128]{2,1,0:T(8,128)S(1)}, u32[]{:S(2)}, u32[]{:S(2)}) %all-to-all-start.3) | async-done | bytes 393248 | tf_op jit(solution)/shard_map/all_to_all | solution.py:35
  170.9 0.2 fusion.46
  171.1 0.2 fusion.78
  171.3 0.4 fusion.28
  171.7 0.4 fusion.91
  172.1 0.1 pad_maximum_fusion.3
  172.2 19.5 %all_to_all.26 = f32[16,32,128]{2,1,0:T(8,128)S(1)} all-to-all(f32[16,32,128]{2,1,0:T(8,128)S(1)} %broadcast_in_dim.8), channel_id=1, replica_groups={{0,16,32,48,64,80,96,112,128,144,160,176,192,208,224,240},{1,17,33,49,6..., dimensions={0} | all-to-all | bytes 524288 | tf_op jit(solution)/shard_map/all_to_all | solution.py:35
  191.7 5.8 %collective-permute-start.18 = (f32[32,128]{1,0:T(8,128)S(1)}, f32[32,128]{1,0:T(8,128)S(1)}, u32[]{:S(2)}, u32[]{:S(2)}) collective-permute-start(f32[32,128]{1,0:T(8,128)S(1)} %reduce_sum.49), channel_id=1, source_target_pairs={{0,8},{1,9},{2,10},{3,11},{4,12},{5,13},{6,14},{7,15},{8,0},{9,1},... | collective-permute-start | bytes 49160 | tf_op jit(solution)/shard_map/ppermute | solution.py:78
  197.6 0.8 collective-permute-done.18
  198.5 1.1 fusion.43
  (63 shorter events, 1.2 us)
Async XLA Ops:
  0.6 24.1 %copy-start = (f32[64,1024]{1,0:T(8,128)S(1)}, f32[64,1024]{1,0:T(8,128)}, u32[]{:S(2)}) copy-start(f32[64,1024]{1,0:T(8,128)} %param.5) | copy-start | bytes 786436
  0.6 24.1 %copy-start.2 = (f32[1024]{0:T(1024)S(1)}, f32[1024]{0:T(1024)}, u32[]{:S(2)}) copy-start(f32[1024]{0:T(1024)} %param.8) | copy-start | bytes 12292
  0.7 24.5 %collective-permute-start = (f32[64,1024]{1,0:T(8,128)}, f32[64,1024]{1,0:T(8,128)S(1)}, u32[]{:S(2)}, u32[]{:S(2)}) collective-permute-start(f32[64,1024]{1,0:T(8,128)} %param.5), channel_id=1, source_target_pairs={{0,0},{1,241},{2,226},{3,211},{4,196},{5,181},{6,166},{7,151},{8,8... | collective-permute-start | bytes 786440 | tf_op jit(solution)/shard_map/ppermute | solution.py:78
  8.1 17.0 %collective-permute-start.2 = (f32[64,1024]{1,0:T(8,128)S(1)}, f32[64,1024]{1,0:T(8,128)S(1)}, u32[]{:S(2)}, u32[]{:S(2)}) collective-permute-start(f32[64,1024]{1,0:T(8,128)S(1)} %fusion.4), channel_id=1, source_target_pairs={{0,8},{1,9},{2,10},{3,11},{4,12},{5,13},{6,14},{7,15},{8,16},{9,17... | collective-permute-start | bytes 786440 | tf_op jit(solution)/shard_map/ppermute | solution.py:78
  21.0 48.2 %copy-start.3 = (f32[1024]{0:T(1024)S(1)}, f32[1024]{0:T(1024)}, u32[]{:S(2)}) copy-start(f32[1024]{0:T(1024)} %param.9) | copy-start | bytes 12292
  25.7 4.1 %collective-permute-start.4 = (f32[32,128]{1,0:T(8,128)S(1)}, f32[32,128]{1,0:T(8,128)S(1)}, u32[]{:S(2)}, u32[]{:S(2)}) collective-permute-start(f32[32,128]{1,0:T(8,128)S(1)} %pad_maximum_fusion.2), channel_id=1, source_target_pairs={{0,8},{1,9},{2,10},{3,11},{4,12},{5,13},{6,14},{7,15},{8,0},{9,1},... | collective-permute-start | bytes 49160 | tf_op jit(solution)/shard_map/ppermute | solution.py:78
  29.0 12.1 %collective-permute-start.3 = (f32[64,1024]{1,0:T(8,128)S(1)}, f32[64,1024]{1,0:T(8,128)S(1)}, u32[]{:S(2)}, u32[]{:S(2)}) collective-permute-start(f32[64,1024]{1,0:T(8,128)S(1)} %add.85), channel_id=1, source_target_pairs={{0,0},{241,1},{226,2},{211,3},{196,4},{181,5},{166,6},{151,7},{8,8... | collective-permute-start | bytes 786440 | tf_op jit(solution)/shard_map/ppermute | solution.py:78
  29.6 7.2 %collective-permute-start.1 = (f32[64,1024]{1,0:T(8,128)S(1)}, f32[64,1024]{1,0:T(8,128)S(1)}, u32[]{:S(2)}, u32[]{:S(2)}) collective-permute-start(f32[64,1024]{1,0:T(8,128)S(1)} %collective-permute-done), channel_id=1, source_target_pairs={{8,0},{9,1},{10,2},{11,3},{12,4},{13,5},{14,6},{15,7},{16,8},{17,9... | collective-permute-start | bytes 786440 | tf_op jit(solution)/shard_map/ppermute | solution.py:78
  29.9 4.5 %collective-permute-start.5 = (f32[32,128]{1,0:T(8,128)S(1)}, f32[32,128]{1,0:T(8,128)S(1)}, u32[]{:S(2)}, u32[]{:S(2)}) collective-permute-start(f32[32,128]{1,0:T(8,128)S(1)} %fusion.113), channel_id=1, source_target_pairs={{0,128},{1,129},{2,130},{3,131},{4,132},{5,133},{6,134},{7,135},{8... | collective-permute-start | bytes 49160 | tf_op jit(solution)/shard_map/ppermute | solution.py:78
  34.4 23.1 %collective-permute-start.6 = (f32[32,128]{1,0:T(8,128)S(1)}, f32[32,128]{1,0:T(8,128)S(1)}, u32[]{:S(2)}, u32[]{:S(2)}) collective-permute-start(f32[32,128]{1,0:T(8,128)S(1)} %add.91), channel_id=1, source_target_pairs={{0,16},{1,17},{2,18},{3,19},{4,20},{5,21},{6,22},{7,23},{8,24},{9,... | collective-permute-start | bytes 49160 | tf_op jit(solution)/shard_map/ppermute | solution.py:78
  41.8 29.8 %all-to-all-start = ((f32[8,64,128]{2,1,0:T(8,128)}), f32[8,64,128]{2,1,0:T(8,128)S(1)}, u32[]{:S(2)}, u32[]{:S(2)}) async-start(f32[8,64,128]{2,1,0:T(8,128)} %bitcast_bitcast_fusion.1), calls=%async_computation | async-start | bytes 524288 | tf_op jit(solution)/shard_map/all_to_all | solution.py:35
  57.5 7.4 %collective-permute-start.7 = (f32[32,128]{1,0:T(8,128)S(1)}, f32[32,128]{1,0:T(8,128)S(1)}, u32[]{:S(2)}, u32[]{:S(2)}) collective-permute-start(f32[32,128]{1,0:T(8,128)S(1)} %add.92), channel_id=1, source_target_pairs={{0,32},{1,33},{2,34},{3,35},{4,36},{5,37},{6,38},{7,39},{8,40},{9,... | collective-permute-start | bytes 49160 | tf_op jit(solution)/shard_map/ppermute | solution.py:78
  65.0 6.7 %collective-permute-start.8 = (f32[32,128]{1,0:T(8,128)S(1)}, f32[32,128]{1,0:T(8,128)S(1)}, u32[]{:S(2)}, u32[]{:S(2)}) collective-permute-start(f32[32,128]{1,0:T(8,128)S(1)} %add.93), channel_id=1, source_target_pairs={{0,64},{1,65},{2,66},{3,67},{4,68},{5,69},{6,70},{7,71},{8,72},{9,... | collective-permute-start | bytes 49160 | tf_op jit(solution)/shard_map/ppermute | solution.py:78
  91.7 20.0 %collective-permute-start.9 = (f32[64,1024]{1,0:T(8,128)S(1)}, f32[64,1024]{1,0:T(8,128)S(1)}, u32[]{:S(2)}, u32[]{:S(2)}) collective-permute-start(f32[64,1024]{1,0:T(8,128)S(1)} %fusion.29), channel_id=1, source_target_pairs={{0,0},{1,241},{2,226},{3,211},{4,196},{5,181},{6,166},{7,151},{8,8... | collective-permute-start | bytes 786440 | tf_op jit(solution)/shard_map/ppermute | solution.py:78
  92.3 19.3 %collective-permute-start.10 = (f32[64,1024]{1,0:T(8,128)S(1)}, f32[64,1024]{1,0:T(8,128)S(1)}, u32[]{:S(2)}, u32[]{:S(2)}) collective-permute-start(f32[64,1024]{1,0:T(8,128)S(1)} %fusion.2), channel_id=1, source_target_pairs={{0,8},{1,9},{2,10},{3,11},{4,12},{5,13},{6,14},{7,15},{8,16},{9,17... | collective-permute-start | bytes 786440 | tf_op jit(solution)/shard_map/ppermute | solution.py:78
  112.4 4.4 %collective-permute-start.11 = (f32[64,128]{1,0:T(8,128)S(1)}, f32[64,128]{1,0:T(8,128)S(1)}, u32[]{:S(2)}, u32[]{:S(2)}) collective-permute-start(f32[64,128]{1,0:T(8,128)S(1)} %maximum_maximum_fusion), channel_id=1, source_target_pairs={{0,8},{1,9},{2,10},{3,11},{4,12},{5,13},{6,14},{7,15},{8,0},{9,1},... | collective-permute-start | bytes 98312 | tf_op jit(solution)/shard_map/ppermute | solution.py:78
  116.9 4.3 %collective-permute-start.12 = (f32[64,128]{1,0:T(8,128)S(1)}, f32[64,128]{1,0:T(8,128)S(1)}, u32[]{:S(2)}, u32[]{:S(2)}) collective-permute-start(f32[64,128]{1,0:T(8,128)S(1)} %fusion.112), channel_id=1, source_target_pairs={{0,128},{1,129},{2,130},{3,131},{4,132},{5,133},{6,134},{7,135},{8... | collective-permute-start | bytes 98312 | tf_op jit(solution)/shard_map/ppermute | solution.py:78
  121.2 2.8 %collective-permute-start.13 = (f32[64,128]{1,0:T(8,128)S(1)}, f32[64,128]{1,0:T(8,128)S(1)}, u32[]{:S(2)}, u32[]{:S(2)}) collective-permute-start(f32[64,128]{1,0:T(8,128)S(1)} %add.100), channel_id=1, source_target_pairs={{0,16},{1,17},{2,18},{3,19},{4,20},{5,21},{6,22},{7,23},{8,24},{9,... | collective-permute-start | bytes 98312 | tf_op jit(solution)/shard_map/ppermute | solution.py:78
  121.3 17.7 %collective-permute-start.17 = (f32[64,1024]{1,0:T(8,128)S(1)}, f32[64,1024]{1,0:T(8,128)S(1)}, u32[]{:S(2)}, u32[]{:S(2)}) collective-permute-start(f32[64,1024]{1,0:T(8,128)S(1)} %add.96), channel_id=1, source_target_pairs={{0,0},{241,1},{226,2},{211,3},{196,4},{181,5},{166,6},{151,7},{8,8... | collective-permute-start | bytes 786440 | tf_op jit(solution)/shard_map/ppermute | solution.py:78
  122.0 12.8 %collective-permute-start.16 = (f32[64,1024]{1,0:T(8,128)S(1)}, f32[64,1024]{1,0:T(8,128)S(1)}, u32[]{:S(2)}, u32[]{:S(2)}) collective-permute-start(f32[64,1024]{1,0:T(8,128)S(1)} %collective-permute-done.9), channel_id=1, source_target_pairs={{8,0},{9,1},{10,2},{11,3},{12,4},{13,5},{14,6},{15,7},{16,8},{17,9... | collective-permute-start | bytes 786440 | tf_op jit(solution)/shard_map/ppermute | solution.py:78
  124.0 9.1 %collective-permute-start.14 = (f32[64,128]{1,0:T(8,128)S(1)}, f32[64,128]{1,0:T(8,128)S(1)}, u32[]{:S(2)}, u32[]{:S(2)}) collective-permute-start(f32[64,128]{1,0:T(8,128)S(1)} %add.101), channel_id=1, source_target_pairs={{0,32},{1,33},{2,34},{3,35},{4,36},{5,37},{6,38},{7,39},{8,40},{9,... | collective-permute-start | bytes 98312 | tf_op jit(solution)/shard_map/ppermute | solution.py:78
  133.1 20.3 %collective-permute-start.15 = (f32[64,128]{1,0:T(8,128)S(1)}, f32[64,128]{1,0:T(8,128)S(1)}, u32[]{:S(2)}, u32[]{:S(2)}) collective-permute-start(f32[64,128]{1,0:T(8,128)S(1)} %add.102), channel_id=1, source_target_pairs={{0,64},{1,65},{2,66},{3,67},{4,68},{5,69},{6,70},{7,71},{8,72},{9,... | collective-permute-start | bytes 98312 | tf_op jit(solution)/shard_map/ppermute | solution.py:78
  139.8 19.7 %all-to-all-start.2 = ((f32[8,64,128]{2,1,0:T(8,128)}), f32[8,64,128]{2,1,0:T(8,128)S(1)}, u32[]{:S(2)}, u32[]{:S(2)}) async-start(f32[8,64,128]{2,1,0:T(8,128)} %bitcast_bitcast_fusion), calls=%async_computation.2 | async-start | bytes 524288 | tf_op jit(solution)/shard_map/all_to_all | solution.py:35
  160.5 10.2 %all-to-all-start.3 = ((f32[8,96,128]{2,1,0:T(8,128)}), f32[8,96,128]{2,1,0:T(8,128)S(1)}, u32[]{:S(2)}, u32[]{:S(2)}) async-start(f32[8,96,128]{2,1,0:T(8,128)} %broadcast_in_dim.7), calls=%async_computation.3 | async-start | bytes 786432 | tf_op jit(solution)/shard_map/all_to_all | solution.py:35
  171.3 28.3 %copy-start.1 = (f32[64,64]{1,0:T(8,128)}, f32[64,64]{1,0:T(8,128)S(1)}, u32[]{:S(2)}) copy-start(f32[64,64]{1,0:T(8,128)S(1)} %fusion.78) | copy-start | bytes 49156
  191.7 6.7 %collective-permute-start.18 = (f32[32,128]{1,0:T(8,128)S(1)}, f32[32,128]{1,0:T(8,128)S(1)}, u32[]{:S(2)}, u32[]{:S(2)}) collective-permute-start(f32[32,128]{1,0:T(8,128)S(1)} %reduce_sum.49), channel_id=1, source_target_pairs={{0,8},{1,9},{2,10},{3,11},{4,12},{5,13},{6,14},{7,15},{8,0},{9,1},... | collective-permute-start | bytes 49160 | tf_op jit(solution)/shard_map/ppermute | solution.py:78

commit v2 on v1

--- a/solution.py
+++ b/solution.py
@@ -90,21 +90,27 @@
     return part + permuted(part, lay.flip[1])
 
 
-def direct_product(piece, block, mask):
-    term = lax.dot_general(
-        piece,
-        block,
-        (((1,), (1,)), ((), ())),
-        precision=lax.Precision.HIGH,
-        preferred_element_type=jnp.float32,
-    )
-    return mask * term
-
-
-def back_product(vectors, block, mask):
-    return jnp.dot(
-        vectors * mask, block, precision=lax.Precision.HIGH, preferred_element_type=jnp.float32
-    )
+def halves(array):
+    high = lax.reduce_precision(array, 8, 7)
+    return high.astype(jnp.bfloat16), (array - high).astype(jnp.bfloat16)
+
+
+def block_product(vecs, block, dims):
+    high, low = halves(vecs)
+    count = vecs.shape[0]
+    dot = lambda left, right: lax.dot_general(
+        left, right, (dims, ((), ())), preferred_element_type=jnp.float32
+    )
+    main = dot(jnp.concatenate([high, low], axis=0), block[0])
+    return main[:count] + (main[count:] + dot(high, block[1]))
+
+
+def direct_product(piece, block):
+    return block_product(piece, block, ((1,), (1,)))
+
+
+def back_product(vecs, block):
+    return block_product(vecs, block, ((1,), (0,)))
 
 
 def local(vectors, tiles, live, energies, precond):
@@ -115,24 +121,47 @@
     total_rows = width * rows
     part = width // offs
     off_index = lax.axis_index("off")
-    row_ids = jnp.arange(width, dtype=jnp.int32)
-    masks = [(row_ids < live[0, s]).astype(jnp.float32) for s in range(per_device)]
-    blocks = [tiles[:, s * width : (s + 1) * width] for s in range(per_device)]
+    row_ids = jnp.arange(width, dtype=jnp.int32)[:, None]
+    block_of = lambda array, s: array[:, s * width : (s + 1) * width]
+
+    def split_of(array, s):
+        return lax.optimization_barrier(
+            halves(jnp.where(row_ids < live[0, s], block_of(array, s), 0.0))
+        )
+
+    masks = [(row_ids[:, 0] < live[0, s]).astype(jnp.float32) for s in range(per_device)]
+
+    def back_first(vecs, s):
+        return jnp.dot(
+            vecs * masks[s],
+            block_of(tiles, s),
+            precision=lax.Precision.HIGH,
+            preferred_element_type=jnp.float32,
+        )
+
+    def direct_first(piece, s):
+        return masks[s] * lax.dot_general(
+            piece,
+            block_of(tiles, s),
+            (((1,), (1,)), ((), ())),
+            precision=lax.Precision.HIGH,
+            preferred_element_type=jnp.float32,
+        )
+
     identity = jnp.eye(count, dtype=jnp.float32)
     own = lambda array: lax.dynamic_index_in_dim(cut(array, offs), off_index, 0, keepdims=False)
 
-    def products(vecs, extra):
+    def products(vecs, extra, back_of, direct_of):
         near = permuted(vecs, lay.fetch)
-        up = permuted(back_product(vecs, blocks[1], masks[1]), lay.up)
-        back = back_product(vecs, blocks[0], masks[0])
-        back = lax.optimization_barrier(back) + up
+        up = permuted(back_of(vecs, 1), lay.up)
+        back = lax.optimization_barrier(back_of(vecs, 0))
+        back = back + up
         returned = permuted(back, lay.back)
         far = permuted(near, lay.down)
         pair = gram(near, back)
         share = folded(pair + pair.T + gram(vecs, energies * vecs) * (1.0 / offs))
-        first = direct_product(near, blocks[0], masks[0])
-        second = direct_product(far, blocks[1], masks[1])
-        first, second = lax.optimization_barrier(first), lax.optimization_barrier(second)
+        first = lax.optimization_barrier(direct_of(near, 0))
+        second = lax.optimization_barrier(direct_of(far, 1))
         share = row_total(jnp.concatenate([share] + extra, axis=0), lay)
         return first + second + returned, share
 
@@ -141,13 +170,24 @@
         return joined(got[:, :count]), unfolded(jnp.sum(got[:, count:], axis=0)) / total_rows
 
     chunk, precond_chunk, energy_chunk = own(vectors), own(precond[None]), own(energies[None])
-    part, share = products(vectors, [])
-    image = energy_chunk * chunk + jnp.sum(exchange(cut(part, offs), lay.row), axis=0)
+    part, share = products(vectors, [], back_first, direct_first)
+    part, later = lax.optimization_barrier((part, tiles))
+    blocks = []
+    for s in range(per_device):
+        blocks.append(split_of(later, s))
+        blocks[-1], later = lax.optimization_barrier((blocks[-1], later))
+    image = jnp.sum(exchange(cut(part, offs), lay.row), axis=0)
+    image = energy_chunk * chunk + image
     stepped, ritz = spread(chunk - precond_chunk * image, share)
     moved = stepped + precond * exact(ritz.T, vectors)
 
     moved_chunk = own(moved)
-    part, share = products(moved, [folded(gram(moved, moved))])
+    part, share = products(
+        moved,
+        [folded(gram(moved, moved))],
+        lambda vecs, s: back_product(vecs, blocks[s]),
+        lambda piece, s: direct_product(piece, blocks[s]),
+    )
     image = energy_chunk * moved_chunk + jnp.sum(exchange(cut(part, offs), lay.row), axis=0)
     fix = 1.5 * identity - 0.5 * unfolded(share[count // 2 :]) / total_rows
     chunk = exact(fix.T, moved_chunk - precond_chunk * image)

time: 200 us -> 193 us (0.965)
  blocking collectives: 31.3 us -> 15.8 us
  other arithmetic: 3.42 us -> 13 us
  matrix products: 36.7 us -> 29.2 us
  waiting for transfers between devices: 31.8 us -> 34.6 us
  local copies, waits for them, and re-layouts: 2.99 us -> 5.61 us
    all_to_all x2 -> x1, blocking collectives: 31.3 us -> 15.8 us  [exchange(): lax.all_to_all(array, AXES, 0, 0, axis_index_groups=groups, tiled=True)]
    convert_element_type x2 -> x6, other arithmetic: 1.29 us -> 10.3 us  [the longest x4 9 us: halves(): return (high.astype(jnp.bfloat16), (array - high).astype(jnp.bfloat16))]
    dot_general x8 -> x12, matrix products: 31.5 us -> 24 us  [the longest x2 8.44 us: direct_first(): lax.dot_general(piece, block_of(tiles, s), (((1,), (1,)), ((), ())), prec...]
    all_to_all x3 -> x4, waiting for transfers between devices: 12.4 us -> 18.8 us  [exchange(): lax.all_to_all(array, AXES, 0, 0, axis_index_groups=groups, tiled=True)]
    ppermute x19, waiting for transfers between devices: 19.4 us -> 15.8 us  [permuted(): return lax.ppermute(array, AXES, pairs)]
    ppermute x19, starting transfers between devices: 59.8 us -> 56.2 us  [permuted(): return lax.ppermute(array, AXES, pairs)]
    all_to_all x3 -> x4, starting transfers between devices: 32.6 us -> 35.9 us  [exchange(): lax.all_to_all(array, AXES, 0, 0, axis_index_groups=groups, tiled=True)]
  transfers between devices with their start and end apart: 22 -> 23, of which waited for: 10 -> 12; matrix products, arithmetic and copies ran while one was open for 15% -> 20% of each run, Pallas kernels for 0% -> 0%
where the time goes in v2:
time: 193 us; the launch traced here: 192 us
  starting transfers between devices  92.1 us (48%)
  waiting for transfers between devices  34.6 us (18%)
  matrix products  29.2 us (15%)
  blocking collectives  15.8 us (8%)
  other arithmetic  13 us (7%)
  local copies, waits for them, and re-layouts  5.61 us (3%)
    ppermute x19, starting transfers between devices, permuted(): return lax.ppermute(array, AXES, pairs)  56.2 us
    all_to_all x4, starting transfers between devices, exchange(): lax.all_to_all(array, AXES, 0, 0, axis_index_groups=groups, tiled=True)  35.9 us
    all_to_all x4, waiting for transfers between devices, exchange(): lax.all_to_all(array, AXES, 0, 0, axis_index_groups=groups, tiled=True)  18.8 us
    all_to_all x1, blocking collectives, exchange(): lax.all_to_all(array, AXES, 0, 0, axis_index_groups=groups, tiled=True)  15.8 us
    ppermute x19, waiting for transfers between devices, permuted(): return lax.ppermute(array, AXES, pairs)  15.8 us
    convert_element_type x4, other arithmetic, halves(): return (high.astype(jnp.bfloat16), (array - high).astype(jnp.bfloat16))  9 us
    dot_general x2, matrix products, direct_first(): lax.dot_general(piece, block_of(tiles, s), (((1,), (1,)), ((), ())), prec...  8.44 us
    dot_general x8, matrix products, block_product(): lax.dot_general(left, right, (dims, ((), ())), preferred_element_type=jnp...  8.21 us
  transfers between devices with their start and end apart: 23, of which 12 were waited for; matrix products, arithmetic and copies ran while one was open for 20% of the time, Pallas kernels for 0%

profile of v2, /device:TPU:1, one launch (start us, length us, event | category | flops | bytes accessed | tf_op | source)
XLA Modules:
  0.0 191.6 jit_solution(3054448825404689519)
XLA Ops:
  0.6 1.6 collective-permute-start
  2.2 1.3 fusion.92
  3.6 0.6 fusion.69
  4.2 3.7 %fusion.2 = f32[64,1024]{1,0:T(8,128)S(1)} fusion(f32[1024,2048]{1,0:T(8,128)} %param.6, f32[64,1024]{1,0:T(8,128)} %param.5, f32[1024]{0:T(1024)S(1)} %fusion.69), kind=kOutput, calls=%fused_computation.8 | convolution fusion | flops 402718720 | bytes 4722688 | tf_op jit(solution)/shard_map/dot_general | solution.py:135
  7.9 12.3 %collective-permute-start.2 = (f32[64,1024]{1,0:T(8,128)S(1)}, f32[64,1024]{1,0:T(8,128)S(1)}, u32[]{:S(2)}, u32[]{:S(2)}) collective-permute-start(f32[64,1024]{1,0:T(8,128)S(1)} %fusion.2), channel_id=1, source_target_pairs={{0,8},{1,9},{2,10},{3,11},{4,12},{5,13},{6,14},{7,15},{8,16},{9,17... | collective-permute-start | bytes 786440 | tf_op jit(solution)/shard_map/ppermute | solution.py:78
  20.2 0.6 fusion.68
  20.9 3.6 %fusion.6 = f32[64,1024]{1,0:T(8,128)S(1)} fusion(f32[1024,2048]{1,0:T(8,128)} %param.6, f32[64,1024]{1,0:T(8,128)S(1)} %copy-done.4, f32[1024]{0:T(1024)S(1)} %fusion.68), kind=kOutput, calls=%fused_computation.12 | convolution fusion | flops 402718720 | bytes 4722688 | tf_op jit(solution)/shard_map/dot_general | solution.py:135
  24.6 0.4 fusion.22
  25.6 3.2 %collective-permute-start.4 = (f32[32,128]{1,0:T(8,128)S(1)}, f32[32,128]{1,0:T(8,128)S(1)}, u32[]{:S(2)}, u32[]{:S(2)}) collective-permute-start(f32[32,128]{1,0:T(8,128)S(1)} %pad_maximum_fusion.5), channel_id=1, source_target_pairs={{0,8},{1,9},{2,10},{3,11},{4,12},{5,13},{6,14},{7,15},{8,0},{9,1},... | collective-permute-start | bytes 49160 | tf_op jit(solution)/shard_map/ppermute | solution.py:78
  28.8 0.8 collective-permute-done.4
  30.0 0.6 iota_compare_fusion.2
  30.6 3.2 %collective-permute-done.5 = f32[32,128]{1,0:T(8,128)S(1)} collective-permute-done((f32[32,128]{1,0:T(8,128)S(1)}, f32[32,128]{1,0:T(8,128)S(1)}, u32[]{:S(2)}, u32[]{:S(2)}) %collective-permute-start.5) | collective-permute-done | bytes 16416 | tf_op jit(solution)/shard_map/ppermute | solution.py:78
  33.8 0.4 collective-permute-start.6
  34.2 0.6 iota_compare_fusion.3
  34.9 1.5 collective-permute-done.6
  36.4 1.7 collective-permute-start.7
  38.2 0.7 collective-permute-start.3
  38.8 2.5 %collective-permute-start.1 = (f32[64,1024]{1,0:T(8,128)S(1)}, f32[64,1024]{1,0:T(8,128)S(1)}, u32[]{:S(2)}, u32[]{:S(2)}) collective-permute-start(f32[64,1024]{1,0:T(8,128)S(1)} %collective-permute-done), channel_id=1, source_target_pairs={{8,0},{9,1},{10,2},{11,3},{12,4},{13,5},{14,6},{15,7},{16,8},{17,9... | collective-permute-start | bytes 786440 | tf_op jit(solution)/shard_map/ppermute | solution.py:78
  41.4 4.7 %collective-permute-start.8 = (f32[32,128]{1,0:T(8,128)S(1)}, f32[32,128]{1,0:T(8,128)S(1)}, u32[]{:S(2)}, u32[]{:S(2)}) collective-permute-start(f32[32,128]{1,0:T(8,128)S(1)} %add.117), channel_id=1, source_target_pairs={{0,64},{1,65},{2,66},{3,67},{4,68},{5,69},{6,70},{7,71},{8,72},{9,... | collective-permute-start | bytes 49160 | tf_op jit(solution)/shard_map/ppermute | solution.py:78
  46.1 4.2 %fusion.10 = f32[64,1024]{1,0:T(8,128)S(1)} fusion(f32[64,1024]{1,0:T(8,128)S(1)} %collective-permute-done, f32[1024,2048]{1,0:T(8,128)} %param.6, f32[1024]{0:T(1024)S(1)} %fusion.68), kind=kOutput, calls=%fused_computation.16 | convolution fusion | flops 402718720 | bytes 4722688 | tf_op jit(solution)/shard_map/dot_general | solution.py:143
  50.3 4.2 %fusion.13 = f32[64,1024]{1,0:T(8,128)S(1)} fusion(f32[64,1024]{1,0:T(8,128)S(1)} %collective-permute-done.1, f32[1024,2048]{1,0:T(8,128)} %param.6, f32[1024]{0:T(1024)S(1)} %fusion.69), kind=kOutput, calls=%fused_computation.17 | convolution fusion | flops 402718720 | bytes 4722688 | tf_op jit(solution)/shard_map/dot_general | solution.py:143
  54.6 0.7 bitcast_bitcast_fusion.1
  55.3 17.5 %all-to-all-start = ((f32[8,64,128]{2,1,0:T(8,128)}), f32[8,64,128]{2,1,0:T(8,128)S(1)}, u32[]{:S(2)}, u32[]{:S(2)}) async-start(f32[8,64,128]{2,1,0:T(8,128)} %bitcast_bitcast_fusion.1), calls=%async_computation | async-start | bytes 524288 | tf_op jit(solution)/shard_map/all_to_all | solution.py:35
  72.8 4.2 %fusion = (bf16[1024,1024]{1,0:T(8,128)(2,1)S(1)}, bf16[1024,1024]{1,0:T(8,128)(2,1)}) fusion(f32[1024,2048]{1,0:T(8,128)} %param.6, pred[1024]{0:T(1024)(128)(4,1)S(1)} %iota_compare_fusion.3), kind=kLoop, calls=%fused_computation.4 | loop fusion | flops 5242880 | bytes 8389632 | tf_op jit(solution)/shard_map/convert_element_type | solution.py:95
  77.0 2.7 %all-to-all-done = f32[8,64,128]{2,1,0:T(8,128)S(1)} async-done(((f32[8,64,128]{2,1,0:T(8,128)}), f32[8,64,128]{2,1,0:T(8,128)S(1)}, u32[]{:S(2)}, u32[]{:S(2)}) %all-to-all-start) | async-done | bytes 262176 | tf_op jit(solution)/shard_map/all_to_all | solution.py:35
  79.8 0.8 broadcast_in_dim.24
  80.6 3.6 %all-to-all-start.1 = ((f32[8,96,128]{2,1,0:T(8,128)}), f32[8,96,128]{2,1,0:T(8,128)S(1)}, u32[]{:S(2)}, u32[]{:S(2)}) async-start(f32[8,96,128]{2,1,0:T(8,128)} %broadcast_in_dim.24), calls=%async_computation.1 | async-start | bytes 786432 | tf_op jit(solution)/shard_map/all_to_all | solution.py:35
  84.2 4.8 %fusion.1 = (bf16[1024,1024]{1,0:T(8,128)(2,1)}, bf16[1024,1024]{1,0:T(8,128)(2,1)}) fusion(f32[1024,2048]{1,0:T(8,128)} %param.6, pred[1024]{0:T(1024)(128)(4,1)S(1)} %iota_compare_fusion.2), kind=kLoop, calls=%fused_computation.5 | loop fusion | flops 5242880 | bytes 8389632 | tf_op jit(solution)/shard_map/convert_element_type | solution.py:95
  89.0 3.7 %all-to-all-done.1 = f32[8,96,128]{2,1,0:T(8,128)S(1)} async-done(((f32[8,96,128]{2,1,0:T(8,128)}), f32[8,96,128]{2,1,0:T(8,128)S(1)}, u32[]{:S(2)}, u32[]{:S(2)}) %all-to-all-start.1) | async-done | bytes 393248 | tf_op jit(solution)/shard_map/all_to_all | solution.py:35
  92.8 0.5 fusion.25
  93.6 0.7 collective-permute-start.9
  94.3 2.0 %fusion.39 = f32[128,1024]{1,0:T(8,128)S(1)} fusion(bf16[1024,1024]{1,0:T(8,128)(2,1)} %get-tuple-element.17, bf16[64,1024]{1,0:T(8,128)(2,1)S(1)} %get-tuple-element.32, bf16[64,1024]{1,0:T(8,128)(2,1)S(1)} %get-tuple-element.33), kind=kOutput, calls=%fused_computation.62 | convolution fusion | flops 268959744 | bytes 2883584 | tf_op jit(solution)/shard_map/dot_general | solution.py:101
  96.4 0.4 fusion.38
  96.8 1.1 copy-done
  98.0 0.5 fusion.19
  98.4 8.1 %collective-permute-start.10 = (f32[64,1024]{1,0:T(8,128)S(1)}, f32[64,1024]{1,0:T(8,128)S(1)}, u32[]{:S(2)}, u32[]{:S(2)}) collective-permute-start(f32[64,1024]{1,0:T(8,128)S(1)} %fusion.19), channel_id=1, source_target_pairs={{0,8},{1,9},{2,10},{3,11},{4,12},{5,13},{6,14},{7,15},{8,16},{9,17... | collective-permute-start | bytes 786440 | tf_op jit(solution)/shard_map/ppermute | solution.py:78
  106.5 0.5 fusion.20
  107.0 0.4 convolution_multiply_fusion.2
  107.4 4.0 %collective-permute-done.10 = f32[64,1024]{1,0:T(8,128)S(1)} collective-permute-done((f32[64,1024]{1,0:T(8,128)S(1)}, f32[64,1024]{1,0:T(8,128)S(1)}, u32[]{:S(2)}, u32[]{:S(2)}) %collective-permute-start.10) | collective-permute-done | bytes 262176 | tf_op jit(solution)/shard_map/ppermute | solution.py:78
  112.2 3.7 %collective-permute-start.11 = (f32[64,128]{1,0:T(8,128)S(1)}, f32[64,128]{1,0:T(8,128)S(1)}, u32[]{:S(2)}, u32[]{:S(2)}) collective-permute-start(f32[64,128]{1,0:T(8,128)S(1)} %maximum_maximum_fusion), channel_id=1, source_target_pairs={{0,8},{1,9},{2,10},{3,11},{4,12},{5,13},{6,14},{7,15},{8,0},{9,1},... | collective-permute-start | bytes 98312 | tf_op jit(solution)/shard_map/ppermute | solution.py:78
  115.9 0.7 collective-permute-start.17
  116.8 0.5 collective-permute-start.12
  117.4 3.8 %collective-permute-done.12 = f32[64,128]{1,0:T(8,128)S(1)} collective-permute-done((f32[64,128]{1,0:T(8,128)S(1)}, f32[64,128]{1,0:T(8,128)S(1)}, u32[]{:S(2)}, u32[]{:S(2)}) %collective-permute-start.12) | collective-permute-done | bytes 32800 | tf_op jit(solution)/shard_map/ppermute | solution.py:78
  121.2 2.4 %fusion.28 = f32[128,1024]{1,0:T(8,128)S(1)} fusion(bf16[1024,1024]{1,0:T(8,128)(2,1)} %get-tuple-element.17, bf16[64,1024]{1,0:T(8,128)(2,1)S(1)} %get-tuple-element.30, bf16[64,1024]{1,0:T(8,128)(2,1)S(1)} %get-tuple-element.31), kind=kOutput, calls=%fused_computation.49 | convolution fusion | flops 268959744 | bytes 2883584 | tf_op jit(solution)/shard_map/dot_general | solution.py:101
  123.7 1.5 collective-permute-start.16
  125.2 1.8 collective-permute-start.14
  127.0 0.8 fusion.18
  127.8 1.5 collective-permute-done.14
  129.3 5.7 %collective-permute-start.15 = (f32[64,128]{1,0:T(8,128)S(1)}, f32[64,128]{1,0:T(8,128)S(1)}, u32[]{:S(2)}, u32[]{:S(2)}) collective-permute-start(f32[64,128]{1,0:T(8,128)S(1)} %add.130), channel_id=1, source_target_pairs={{0,64},{1,65},{2,66},{3,67},{4,68},{5,69},{6,70},{7,71},{8,72},{9,... | collective-permute-start | bytes 98312 | tf_op jit(solution)/shard_map/ppermute | solution.py:78
  135.1 0.8 fusion.32
  135.9 0.8 fusion.17
  136.7 0.7 bitcast_bitcast_fusion
  137.5 11.3 %all-to-all-start.2 = ((f32[8,64,128]{2,1,0:T(8,128)}), f32[8,64,128]{2,1,0:T(8,128)S(1)}, u32[]{:S(2)}, u32[]{:S(2)}) async-start(f32[8,64,128]{2,1,0:T(8,128)} %bitcast_bitcast_fusion), calls=%async_computation.2 | async-start | bytes 524288 | tf_op jit(solution)/shard_map/all_to_all | solution.py:35
  148.9 6.0 %all-to-all-done.2 = f32[8,64,128]{2,1,0:T(8,128)S(1)} async-done(((f32[8,64,128]{2,1,0:T(8,128)}), f32[8,64,128]{2,1,0:T(8,128)S(1)}, u32[]{:S(2)}, u32[]{:S(2)}) %all-to-all-start.2) | async-done | bytes 262176 | tf_op jit(solution)/shard_map/all_to_all | solution.py:35
  155.2 0.8 broadcast_in_dim.28
  156.0 3.5 %all-to-all-start.3 = ((f32[8,96,128]{2,1,0:T(8,128)}), f32[8,96,128]{2,1,0:T(8,128)S(1)}, u32[]{:S(2)}, u32[]{:S(2)}) async-start(f32[8,96,128]{2,1,0:T(8,128)} %broadcast_in_dim.28), calls=%async_computation.3 | async-start | bytes 786432 | tf_op jit(solution)/shard_map/all_to_all | solution.py:35
  159.4 0.4 fusion.82
  159.9 6.4 %all-to-all-done.3 = f32[8,96,128]{2,1,0:T(8,128)S(1)} async-done(((f32[8,96,128]{2,1,0:T(8,128)}), f32[8,96,128]{2,1,0:T(8,128)S(1)}, u32[]{:S(2)}, u32[]{:S(2)}) %all-to-all-start.3) | async-done | bytes 393248 | tf_op jit(solution)/shard_map/all_to_all | solution.py:35
  166.7 0.4 fusion.16
  167.2 0.4 fusion.96
  167.6 15.8 %all_to_all.25 = f32[16,32,128]{2,1,0:T(8,128)S(1)} all-to-all(f32[16,32,128]{2,1,0:T(8,128)S(1)} %broadcast_in_dim.50), channel_id=1, replica_groups={{0,16,32,48,64,80,96,112,128,144,160,176,192,208,224,240},{1,17,33,49,6..., dimensions={0} | all-to-all | bytes 524288 | tf_op jit(solution)/shard_map/all_to_all | solution.py:35
  183.5 6.0 %collective-permute-start.18 = (f32[32,128]{1,0:T(8,128)S(1)}, f32[32,128]{1,0:T(8,128)S(1)}, u32[]{:S(2)}, u32[]{:S(2)}) collective-permute-start(f32[32,128]{1,0:T(8,128)S(1)} %reduce_sum.49), channel_id=1, source_target_pairs={{0,8},{1,9},{2,10},{3,11},{4,12},{5,13},{6,14},{7,15},{8,0},{9,1},... | collective-permute-start | bytes 49160 | tf_op jit(solution)/shard_map/ppermute | solution.py:78
  189.5 0.8 collective-permute-done.18
  190.4 1.1 fusion.44
  (83 shorter events, 3.8 us)
Async XLA Ops:
  0.6 24.4 %collective-permute-start = (f32[64,1024]{1,0:T(8,128)}, f32[64,1024]{1,0:T(8,128)S(1)}, u32[]{:S(2)}, u32[]{:S(2)}) collective-permute-start(f32[64,1024]{1,0:T(8,128)} %param.5), channel_id=1, source_target_pairs={{0,0},{1,241},{2,226},{3,211},{4,196},{5,181},{6,166},{7,151},{8,8... | collective-permute-start | bytes 786440 | tf_op jit(solution)/shard_map/ppermute | solution.py:78
  4.2 16.7 %copy-start.4 = (f32[64,1024]{1,0:T(8,128)S(1)}, f32[64,1024]{1,0:T(8,128)}, u32[]{:S(2)}) copy-start(f32[64,1024]{1,0:T(8,128)} %param.5) | copy-start | bytes 786436
  7.9 17.0 %collective-permute-start.2 = (f32[64,1024]{1,0:T(8,128)S(1)}, f32[64,1024]{1,0:T(8,128)S(1)}, u32[]{:S(2)}, u32[]{:S(2)}) collective-permute-start(f32[64,1024]{1,0:T(8,128)S(1)} %fusion.2), channel_id=1, source_target_pairs={{0,8},{1,9},{2,10},{3,11},{4,12},{5,13},{6,14},{7,15},{8,16},{9,17... | collective-permute-start | bytes 786440 | tf_op jit(solution)/shard_map/ppermute | solution.py:78
  20.9 3.7 %copy-start.6 = (f32[1024]{0:T(1024)S(1)}, f32[1024]{0:T(1024)}, u32[]{:S(2)}) copy-start(f32[1024]{0:T(1024)} %param.8) | copy-start | bytes 12292
  24.5 13.7 %copy-start.7 = (f32[1024]{0:T(1024)S(1)}, f32[1024]{0:T(1024)}, u32[]{:S(2)}) copy-start(f32[1024]{0:T(1024)} %param.9) | copy-start | bytes 12292
  25.6 4.1 %collective-permute-start.4 = (f32[32,128]{1,0:T(8,128)S(1)}, f32[32,128]{1,0:T(8,128)S(1)}, u32[]{:S(2)}, u32[]{:S(2)}) collective-permute-start(f32[32,128]{1,0:T(8,128)S(1)} %pad_maximum_fusion.5), channel_id=1, source_target_pairs={{0,8},{1,9},{2,10},{3,11},{4,12},{5,13},{6,14},{7,15},{8,0},{9,1},... | collective-permute-start | bytes 49160 | tf_op jit(solution)/shard_map/ppermute | solution.py:78
  29.7 4.1 %collective-permute-start.5 = (f32[32,128]{1,0:T(8,128)S(1)}, f32[32,128]{1,0:T(8,128)S(1)}, u32[]{:S(2)}, u32[]{:S(2)}) collective-permute-start(f32[32,128]{1,0:T(8,128)S(1)} %fusion.128), channel_id=1, source_target_pairs={{0,128},{1,129},{2,130},{3,131},{4,132},{5,133},{6,134},{7,135},{8... | collective-permute-start | bytes 49160 | tf_op jit(solution)/shard_map/ppermute | solution.py:78
  33.8 2.6 %collective-permute-start.6 = (f32[32,128]{1,0:T(8,128)S(1)}, f32[32,128]{1,0:T(8,128)S(1)}, u32[]{:S(2)}, u32[]{:S(2)}) collective-permute-start(f32[32,128]{1,0:T(8,128)S(1)} %add.115), channel_id=1, source_target_pairs={{0,16},{1,17},{2,18},{3,19},{4,20},{5,21},{6,22},{7,23},{8,24},{9,... | collective-permute-start | bytes 49160 | tf_op jit(solution)/shard_map/ppermute | solution.py:78
  36.4 5.0 %collective-permute-start.7 = (f32[32,128]{1,0:T(8,128)S(1)}, f32[32,128]{1,0:T(8,128)S(1)}, u32[]{:S(2)}, u32[]{:S(2)}) collective-permute-start(f32[32,128]{1,0:T(8,128)S(1)} %add.116), channel_id=1, source_target_pairs={{0,32},{1,33},{2,34},{3,35},{4,36},{5,37},{6,38},{7,39},{8,40},{9,... | collective-permute-start | bytes 49160 | tf_op jit(solution)/shard_map/ppermute | solution.py:78
  38.2 16.4 %collective-permute-start.3 = (f32[64,1024]{1,0:T(8,128)S(1)}, f32[64,1024]{1,0:T(8,128)S(1)}, u32[]{:S(2)}, u32[]{:S(2)}) collective-permute-start(f32[64,1024]{1,0:T(8,128)S(1)} %add.109), channel_id=1, source_target_pairs={{0,0},{241,1},{226,2},{211,3},{196,4},{181,5},{166,6},{151,7},{8,8... | collective-permute-start | bytes 786440 | tf_op jit(solution)/shard_map/ppermute | solution.py:78
  38.8 11.5 %collective-permute-start.1 = (f32[64,1024]{1,0:T(8,128)S(1)}, f32[64,1024]{1,0:T(8,128)S(1)}, u32[]{:S(2)}, u32[]{:S(2)}) collective-permute-start(f32[64,1024]{1,0:T(8,128)S(1)} %collective-permute-done), channel_id=1, source_target_pairs={{8,0},{9,1},{10,2},{11,3},{12,4},{13,5},{14,6},{15,7},{16,8},{17,9... | collective-permute-start | bytes 786440 | tf_op jit(solution)/shard_map/ppermute | solution.py:78
  41.4 8.9 %collective-permute-start.8 = (f32[32,128]{1,0:T(8,128)S(1)}, f32[32,128]{1,0:T(8,128)S(1)}, u32[]{:S(2)}, u32[]{:S(2)}) collective-permute-start(f32[32,128]{1,0:T(8,128)S(1)} %add.117), channel_id=1, source_target_pairs={{0,64},{1,65},{2,66},{3,67},{4,68},{5,69},{6,70},{7,71},{8,72},{9,... | collective-permute-start | bytes 49160 | tf_op jit(solution)/shard_map/ppermute | solution.py:78
  55.3 24.4 %all-to-all-start = ((f32[8,64,128]{2,1,0:T(8,128)}), f32[8,64,128]{2,1,0:T(8,128)S(1)}, u32[]{:S(2)}, u32[]{:S(2)}) async-start(f32[8,64,128]{2,1,0:T(8,128)} %bitcast_bitcast_fusion.1), calls=%async_computation | async-start | bytes 524288 | tf_op jit(solution)/shard_map/all_to_all | solution.py:35
  80.6 12.2 %all-to-all-start.1 = ((f32[8,96,128]{2,1,0:T(8,128)}), f32[8,96,128]{2,1,0:T(8,128)S(1)}, u32[]{:S(2)}, u32[]{:S(2)}) async-start(f32[8,96,128]{2,1,0:T(8,128)} %broadcast_in_dim.24), calls=%async_computation.1 | async-start | bytes 786432 | tf_op jit(solution)/shard_map/all_to_all | solution.py:35
  92.8 3.6 %copy-start.2 = (bf16[1024,1024]{1,0:T(8,128)(2,1)S(1)}, bf16[1024,1024]{1,0:T(8,128)(2,1)}, u32[]{:S(2)}) copy-start(bf16[1024,1024]{1,0:T(8,128)(2,1)} %get-tuple-element.22) | copy-start | bytes 6291460
  93.6 17.8 %collective-permute-start.9 = (f32[64,1024]{1,0:T(8,128)S(1)}, f32[64,1024]{1,0:T(8,128)S(1)}, u32[]{:S(2)}, u32[]{:S(2)}) collective-permute-start(f32[64,1024]{1,0:T(8,128)S(1)} %get-tuple-element.52), channel_id=1, source_target_pairs={{0,0},{1,241},{2,226},{3,211},{4,196},{5,181},{6,166},{7,151},{8,8... | collective-permute-start | bytes 786440 | tf_op jit(solution)/shard_map/ppermute | solution.py:78
  96.4 1.6 copy-start
  98.4 13.0 %collective-permute-start.10 = (f32[64,1024]{1,0:T(8,128)S(1)}, f32[64,1024]{1,0:T(8,128)S(1)}, u32[]{:S(2)}, u32[]{:S(2)}) collective-permute-start(f32[64,1024]{1,0:T(8,128)S(1)} %fusion.19), channel_id=1, source_target_pairs={{0,8},{1,9},{2,10},{3,11},{4,12},{5,13},{6,14},{7,15},{8,16},{9,17... | collective-permute-start | bytes 786440 | tf_op jit(solution)/shard_map/ppermute | solution.py:78
  112.2 4.5 %collective-permute-start.11 = (f32[64,128]{1,0:T(8,128)S(1)}, f32[64,128]{1,0:T(8,128)S(1)}, u32[]{:S(2)}, u32[]{:S(2)}) collective-permute-start(f32[64,128]{1,0:T(8,128)S(1)} %maximum_maximum_fusion), channel_id=1, source_target_pairs={{0,8},{1,9},{2,10},{3,11},{4,12},{5,13},{6,14},{7,15},{8,0},{9,1},... | collective-permute-start | bytes 98312 | tf_op jit(solution)/shard_map/ppermute | solution.py:78
  115.9 20.8 %collective-permute-start.17 = (f32[64,1024]{1,0:T(8,128)S(1)}, f32[64,1024]{1,0:T(8,128)S(1)}, u32[]{:S(2)}, u32[]{:S(2)}) collective-permute-start(f32[64,1024]{1,0:T(8,128)S(1)} %add.124), channel_id=1, source_target_pairs={{0,0},{241,1},{226,2},{211,3},{196,4},{181,5},{166,6},{151,7},{8,8... | collective-permute-start | bytes 786440 | tf_op jit(solution)/shard_map/ppermute | solution.py:78
  116.8 4.3 %collective-permute-start.12 = (f32[64,128]{1,0:T(8,128)S(1)}, f32[64,128]{1,0:T(8,128)S(1)}, u32[]{:S(2)}, u32[]{:S(2)}) collective-permute-start(f32[64,128]{1,0:T(8,128)S(1)} %fusion.127), channel_id=1, source_target_pairs={{0,128},{1,129},{2,130},{3,131},{4,132},{5,133},{6,134},{7,135},{8... | collective-permute-start | bytes 98312 | tf_op jit(solution)/shard_map/ppermute | solution.py:78
  121.1 4.1 %collective-permute-start.13 = (f32[64,128]{1,0:T(8,128)S(1)}, f32[64,128]{1,0:T(8,128)S(1)}, u32[]{:S(2)}, u32[]{:S(2)}) collective-permute-start(f32[64,128]{1,0:T(8,128)S(1)} %add.128), channel_id=1, source_target_pairs={{0,16},{1,17},{2,18},{3,19},{4,20},{5,21},{6,22},{7,23},{8,24},{9,... | collective-permute-start | bytes 98312 | tf_op jit(solution)/shard_map/ppermute | solution.py:78
  123.6 11.4 %copy-start.3 = (bf16[1024,1024]{1,0:T(8,128)(2,1)S(1)}, bf16[1024,1024]{1,0:T(8,128)(2,1)}, u32[]{:S(2)}) copy-start(bf16[1024,1024]{1,0:T(8,128)(2,1)} %get-tuple-element.22) | copy-start | bytes 6291460
  123.7 11.4 %collective-permute-start.16 = (f32[64,1024]{1,0:T(8,128)S(1)}, f32[64,1024]{1,0:T(8,128)S(1)}, u32[]{:S(2)}, u32[]{:S(2)}) collective-permute-start(f32[64,1024]{1,0:T(8,128)S(1)} %collective-permute-done.9), channel_id=1, source_target_pairs={{8,0},{9,1},{10,2},{11,3},{12,4},{13,5},{14,6},{15,7},{16,8},{17,9... | collective-permute-start | bytes 786440 | tf_op jit(solution)/shard_map/ppermute | solution.py:78
  125.2 4.1 %collective-permute-start.14 = (f32[64,128]{1,0:T(8,128)S(1)}, f32[64,128]{1,0:T(8,128)S(1)}, u32[]{:S(2)}, u32[]{:S(2)}) collective-permute-start(f32[64,128]{1,0:T(8,128)S(1)} %add.129), channel_id=1, source_target_pairs={{0,32},{1,33},{2,34},{3,35},{4,36},{5,37},{6,38},{7,39},{8,40},{9,... | collective-permute-start | bytes 98312 | tf_op jit(solution)/shard_map/ppermute | solution.py:78
  127.8 8.2 %copy-start.1 = (bf16[1024,1024]{1,0:T(8,128)(2,1)S(1)}, bf16[1024,1024]{1,0:T(8,128)(2,1)}, u32[]{:S(2)}) copy-start(bf16[1024,1024]{1,0:T(8,128)(2,1)} %get-tuple-element.23) | copy-start | bytes 6291460
  129.3 19.5 %collective-permute-start.15 = (f32[64,128]{1,0:T(8,128)S(1)}, f32[64,128]{1,0:T(8,128)S(1)}, u32[]{:S(2)}, u32[]{:S(2)}) collective-permute-start(f32[64,128]{1,0:T(8,128)S(1)} %add.130), channel_id=1, source_target_pairs={{0,64},{1,65},{2,66},{3,67},{4,68},{5,69},{6,70},{7,71},{8,72},{9,... | collective-permute-start | bytes 98312 | tf_op jit(solution)/shard_map/ppermute | solution.py:78
  137.5 17.5 %all-to-all-start.2 = ((f32[8,64,128]{2,1,0:T(8,128)}), f32[8,64,128]{2,1,0:T(8,128)S(1)}, u32[]{:S(2)}, u32[]{:S(2)}) async-start(f32[8,64,128]{2,1,0:T(8,128)} %bitcast_bitcast_fusion), calls=%async_computation.2 | async-start | bytes 524288 | tf_op jit(solution)/shard_map/all_to_all | solution.py:35
  156.0 10.2 %all-to-all-start.3 = ((f32[8,96,128]{2,1,0:T(8,128)}), f32[8,96,128]{2,1,0:T(8,128)S(1)}, u32[]{:S(2)}, u32[]{:S(2)}) async-start(f32[8,96,128]{2,1,0:T(8,128)} %broadcast_in_dim.28), calls=%async_computation.3 | async-start | bytes 786432 | tf_op jit(solution)/shard_map/all_to_all | solution.py:35
  166.7 24.8 %copy-start.5 = (f32[64,64]{1,0:T(8,128)}, f32[64,64]{1,0:T(8,128)S(1)}, u32[]{:S(2)}) copy-start(f32[64,64]{1,0:T(8,128)S(1)} %fusion.83) | copy-start | bytes 49156
  183.5 6.9 %collective-permute-start.18 = (f32[32,128]{1,0:T(8,128)S(1)}, f32[32,128]{1,0:T(8,128)S(1)}, u32[]{:S(2)}, u32[]{:S(2)}) collective-permute-start(f32[32,128]{1,0:T(8,128)S(1)} %reduce_sum.49), channel_id=1, source_target_pairs={{0,8},{1,9},{2,10},{3,11},{4,12},{5,13},{6,14},{7,15},{8,0},{9,1},... | collective-permute-start | bytes 49160 | tf_op jit(solution)/shard_map/ppermute | solution.py:78

commit v3 on v2

--- a/solution.py
+++ b/solution.py
@@ -22,13 +22,18 @@
             bit: [(number(row, p), number(row ^ bit, p)) for row, p in every]
             for bit in (1 << n for n in range(rows.bit_length() - 1))
         }
-        turn = lambda row: row // 2 * 2 % offs
-        self.fetch = [
-            (number(row, p ^ turn(row)), number(row - per_device * p, p)) for row, p in every
-        ]
+        turn = lambda row: row % rows // 2 * 2 % offs
+
+        def couple(row, p, s):
+            far = row + per_device * p + s
+            return number(far, p ^ turn(far)), number(row, p)
+
+        self.fetch = [couple(row, p, 0) for row, p in every]
         self.back = [(b, a) for a, b in self.fetch]
-        self.up = [(number(row, p), number(row + 1, p)) for row, p in every]
-        self.down = [(b, a) for a, b in self.up]
+        self.fetch_odd = [couple(row, p, 1) for row, p in every if row % 2]
+        self.back_odd = [(b, a) for a, b in self.fetch_odd]
+        self.to_odd = [(number(row - 1, p), number(row, p)) for row, p in every if row % 2]
+        self.to_even = [(b, a) for a, b in self.to_odd]
 
 
 def exchange(array, groups):
@@ -121,6 +126,7 @@
     total_rows = width * rows
     part = width // offs
     off_index = lax.axis_index("off")
+    odd = (lax.axis_index("row") % 2).astype(jnp.float32)
     row_ids = jnp.arange(width, dtype=jnp.int32)[:, None]
     block_of = lambda array, s: array[:, s * width : (s + 1) * width]
 
@@ -129,7 +135,8 @@
             halves(jnp.where(row_ids < live[0, s], block_of(array, s), 0.0))
         )
 
-    masks = [(row_ids[:, 0] < live[0, s]).astype(jnp.float32) for s in range(per_device)]
+    masks = (lax.broadcasted_iota(jnp.int32, (per_device, width), 1) < live.T).astype(jnp.float32)
+    masks = lax.optimization_barrier(masks)
 
     def back_first(vecs, s):
         return jnp.dot(
@@ -139,43 +146,40 @@
             preferred_element_type=jnp.float32,
         )
 
-    def direct_first(piece, s):
-        return masks[s] * lax.dot_general(
-            piece,
-            block_of(tiles, s),
-            (((1,), (1,)), ((), ())),
-            precision=lax.Precision.HIGH,
-            preferred_element_type=jnp.float32,
-        )
-
     identity = jnp.eye(count, dtype=jnp.float32)
     own = lambda array: lax.dynamic_index_in_dim(cut(array, offs), off_index, 0, keepdims=False)
 
-    def products(vecs, extra, back_of, direct_of):
+    def products(vecs, extra, back_of, block_for):
         near = permuted(vecs, lay.fetch)
-        up = permuted(back_of(vecs, 1), lay.up)
-        back = lax.optimization_barrier(back_of(vecs, 0))
-        back = back + up
+        far = permuted(vecs, lay.fetch_odd)
+        back_far = lax.optimization_barrier(back_of(vecs, 1))
+        up = permuted(back_far, lay.to_odd)
+        returned_far = permuted(back_far, lay.back_odd)
+        own_back = lax.optimization_barrier(back_of(vecs, 0))
+        back = own_back + up
         returned = permuted(back, lay.back)
-        far = permuted(near, lay.down)
-        pair = gram(near, back)
+        far = far + permuted(near, lay.to_even)
+        pair = gram(near, back) + gram(far, back_far * odd)
         share = folded(pair + pair.T + gram(vecs, energies * vecs) * (1.0 / offs))
-        first = lax.optimization_barrier(direct_of(near, 0))
-        second = lax.optimization_barrier(direct_of(far, 1))
+        block = block_for(0, own_back)
+        first = lax.optimization_barrier(direct_product(near, block))
+        block = block_for(1, block)
+        second = lax.optimization_barrier(direct_product(far, block))
         share = row_total(jnp.concatenate([share] + extra, axis=0), lay)
-        return first + second + returned, share
+        return first + second + (returned + returned_far), share
 
     def spread(chunk, share):
         got = sent_to_all(jnp.concatenate([chunk, share], axis=0), lay.row)
         return joined(got[:, :count]), unfolded(jnp.sum(got[:, count:], axis=0)) / total_rows
 
     chunk, precond_chunk, energy_chunk = own(vectors), own(precond[None]), own(energies[None])
-    part, share = products(vectors, [], back_first, direct_first)
-    part, later = lax.optimization_barrier((part, tiles))
     blocks = []
-    for s in range(per_device):
-        blocks.append(split_of(later, s))
-        blocks[-1], later = lax.optimization_barrier((blocks[-1], later))
+
+    def split_after(s, earlier):
+        blocks.append(split_of(lax.optimization_barrier((tiles, earlier))[0], s))
+        return blocks[s]
+
+    part, share = products(vectors, [], back_first, split_after)
     image = jnp.sum(exchange(cut(part, offs), lay.row), axis=0)
     image = energy_chunk * chunk + image
     stepped, ritz = spread(chunk - precond_chunk * image, share)
@@ -186,7 +190,7 @@
         moved,
         [folded(gram(moved, moved))],
         lambda vecs, s: back_product(vecs, blocks[s]),
-        lambda piece, s: direct_product(piece, blocks[s]),
+        lambda s, _: blocks[s],
     )
     image = energy_chunk * moved_chunk + jnp.sum(exchange(cut(part, offs), lay.row), axis=0)
     fix = 1.5 * identity - 0.5 * unfolded(share[count // 2 :]) / total_rows

time: 193 us -> 200 us (1.036)
  blocking collectives: 15.8 us -> 33.7 us
  waiting for transfers between devices: 34.6 us -> 18 us
  starting transfers between devices: 92.1 us -> 98.9 us
    ppermute x19 -> x23, starting transfers between devices: 56.2 us -> 76.7 us  [permuted(): return lax.ppermute(array, AXES, pairs)]
    all_to_all x1 -> x2, blocking collectives: 15.8 us -> 33.7 us  [exchange(): lax.all_to_all(array, AXES, 0, 0, axis_index_groups=groups, tiled=True)]
    all_to_all x4 -> x3, starting transfers between devices: 35.9 us -> 22.2 us  [exchange(): lax.all_to_all(array, AXES, 0, 0, axis_index_groups=groups, tiled=True)]
    all_to_all x4 -> x3, waiting for transfers between devices: 18.8 us -> 6.42 us  [exchange(): lax.all_to_all(array, AXES, 0, 0, axis_index_groups=groups, tiled=True)]
    dot_general x2 -> x0, matrix products: 8.44 us -> none  [direct_first(): lax.dot_general(piece, block_of(tiles, s), (((1,), (1,)), ((), ())), prec...]
    dot_general x8 -> x12, matrix products: 8.21 us -> 14.6 us  [block_product(): lax.dot_general(left, right, (dims, ((), ())), preferred_element_type=jnp...]
    ppermute x19 -> x23, waiting for transfers between devices: 15.8 us -> 11.5 us  [permuted(): return lax.ppermute(array, AXES, pairs)]
    convert_element_type x4 -> x6, other arithmetic: 9 us -> 4.77 us  [halves(): return (high.astype(jnp.bfloat16), (array - high).astype(jnp.bfloat16))]
  transfers between devices with their start and end apart: 23 -> 26, of which waited for: 12 -> 9; matrix products, arithmetic and copies ran while one was open for 20% -> 21% of each run, Pallas kernels for 0% -> 0%
where the time goes in v3:
time: 200 us; the launch traced here: 199 us
  starting transfers between devices  98.9 us (49%)
  blocking collectives  33.7 us (17%)
  matrix products  29.7 us (15%)
  waiting for transfers between devices  18 us (9%)
  other arithmetic  12 us (6%)
  local copies, waits for them, and re-layouts  5.31 us (3%)
    ppermute x23, starting transfers between devices, permuted(): return lax.ppermute(array, AXES, pairs)  76.7 us
    all_to_all x2, blocking collectives, exchange(): lax.all_to_all(array, AXES, 0, 0, axis_index_groups=groups, tiled=True)  33.7 us
    all_to_all x3, starting transfers between devices, exchange(): lax.all_to_all(array, AXES, 0, 0, axis_index_groups=groups, tiled=True)  22.2 us
    dot_general x12, matrix products, block_product(): lax.dot_general(left, right, (dims, ((), ())), preferred_element_type=jnp...  14.6 us
    ppermute x23, waiting for transfers between devices, permuted(): return lax.ppermute(array, AXES, pairs)  11.5 us
    dot_general x2, matrix products, back_first(): jnp.dot(vecs * masks[s], block_of(tiles, s), precision=lax.Precision.HIGH...  8.22 us
    all_to_all x3, waiting for transfers between devices, exchange(): lax.all_to_all(array, AXES, 0, 0, axis_index_groups=groups, tiled=True)  6.42 us
    convert_element_type x6, other arithmetic, halves(): return (high.astype(jnp.bfloat16), (array - high).astype(jnp.bfloat16))  4.77 us
  transfers between devices with their start and end apart: 26, of which 9 were waited for; matrix products, arithmetic and copies ran while one was open for 21% of the time, Pallas kernels for 0%

profile of v3, /device:TPU:1, one launch (start us, length us, event | category | flops | bytes accessed | tf_op | source)
XLA Modules:
  0.0 198.8 jit_solution(16346234164703201777)
XLA Ops:
  0.6 1.6 collective-permute-start
  2.2 1.3 collective-permute-start.1
  3.5 0.7 compare_convert_fusion
  4.3 4.5 %fusion.2 = f32[64,1024]{1,0:T(8,128)} fusion(f32[1024,2048]{1,0:T(8,128)} %param.6, f32[64,1024]{1,0:T(8,128)} %param.5, f32[1024]{0:T(1024)S(1)} %bitcast.108), kind=kOutput, calls=%fused_computation.6 | convolution fusion | flops 402718720 | bytes 4722688 | tf_op jit(solution)/shard_map/dot_general | solution.py:142
  8.8 1.3 collective-permute-start.3
  10.1 8.3 %collective-permute-start.5 = (f32[64,1024]{1,0:T(8,128)}, f32[64,1024]{1,0:T(8,128)}, u32[]{:S(2)}, u32[]{:S(2)}) collective-permute-start(f32[64,1024]{1,0:T(8,128)} %fusion.2), channel_id=1, source_target_pairs={{8,18},{9,37},{10,52},{11,67},{12,86},{13,97},{14,112},{15,135},{2... | collective-permute-start | bytes 786440 | tf_op jit(solution)/shard_map/ppermute | solution.py:83
  18.4 1.3 fusion.104
  19.7 3.7 %fusion.4 = f32[64,1024]{1,0:T(8,128)S(1)} fusion(f32[1024,2048]{1,0:T(8,128)} %param.6, f32[64,1024]{1,0:T(8,128)} %param.5, f32[1024]{0:T(1024)S(1)} %bitcast.107), kind=kOutput, calls=%fused_computation.10 | convolution fusion | flops 402718720 | bytes 4722688 | tf_op jit(solution)/shard_map/dot_general | solution.py:142
  23.4 0.6 iota_compare_fusion.3
  24.0 2.6 %fusion = (bf16[1024,1024]{1,0:T(8,128)(2,1)}, bf16[1024,1024]{1,0:T(8,128)(2,1)}) fusion(f32[1024,2048]{1,0:T(8,128)S(1)} %copy-done.4, pred[1024]{0:T(1024)(128)(4,1)S(1)} %iota_compare_fusion.3), kind=kLoop, calls=%fused_computation.4 | loop fusion | flops 5242880 | bytes 8389632 | tf_op jit(solution)/shard_map/convert_element_type | solution.py:100
  26.7 0.6 iota_compare_fusion.2
  27.4 2.0 %fusion.1 = (bf16[1024,1024]{1,0:T(8,128)(2,1)S(1)}, bf16[1024,1024]{1,0:T(8,128)(2,1)}) fusion(f32[1024,2048]{1,0:T(8,128)S(1)} %copy-done.4, pred[1024]{0:T(1024)(128)(4,1)S(1)} %iota_compare_fusion.2), kind=kLoop, calls=%fused_computation.5 | loop fusion | flops 5242880 | bytes 8389632 | tf_op jit(solution)/shard_map/convert_element_type | solution.py:100
  29.7 1.0 add.155
  30.7 1.4 collective-permute-start.4
  32.6 2.6 %fusion.23 = f32[128,1024]{1,0:T(8,128)S(1)} fusion(bf16[1024,1024]{1,0:T(8,128)(2,1)} %get-tuple-element.9, bf16[64,1024]{1,0:T(8,128)(2,1)S(1)} %get-tuple-element.26, bf16[64,1024]{1,0:T(8,128)(2,1)S(1)} %get-tuple-element.27), kind=kOutput, calls=%fused_computation.54 | convolution fusion | flops 268959744 | bytes 2883584 | tf_op jit(solution)/shard_map/dot_general | solution.py:106
  35.1 6.8 %collective-permute-start.2 = (f32[64,1024]{1,0:T(8,128)S(1)}, f32[64,1024]{1,0:T(8,128)S(1)}, u32[]{:S(2)}, u32[]{:S(2)}) collective-permute-start(f32[64,1024]{1,0:T(8,128)S(1)} %collective-permute-done), channel_id=1, source_target_pairs={{8,0},{9,1},{10,2},{11,3},{12,4},{13,5},{14,6},{15,7},{24,16},{25,... | collective-permute-start | bytes 786440 | tf_op jit(solution)/shard_map/ppermute | solution.py:83
  41.9 1.5 fusion.14
  43.4 1.3 fusion.40
  45.0 2.4 %fusion.27 = f32[128,1024]{1,0:T(8,128)S(1)} fusion(bf16[1024,1024]{1,0:T(8,128)(2,1)} %get-tuple-element.12, bf16[64,1024]{1,0:T(8,128)(2,1)S(1)} %get-tuple-element.20, bf16[64,1024]{1,0:T(8,128)(2,1)S(1)} %get-tuple-element.21), kind=kOutput, calls=%fused_computation.58 | convolution fusion | flops 268959744 | bytes 2883584 | tf_op jit(solution)/shard_map/dot_general | solution.py:106
  47.8 0.8 fusion.12
  48.5 3.1 %collective-permute-done.7 = f32[32,128]{1,0:T(8,128)S(1)} collective-permute-done((f32[32,128]{1,0:T(8,128)S(1)}, f32[32,128]{1,0:T(8,128)S(1)}, u32[]{:S(2)}, u32[]{:S(2)}) %collective-permute-start.7) | collective-permute-done | bytes 16416 | tf_op jit(solution)/shard_map/ppermute | solution.py:83
  51.7 6.3 %collective-permute-start.8 = (f32[32,128]{1,0:T(8,128)S(1)}, f32[32,128]{1,0:T(8,128)S(1)}, u32[]{:S(2)}, u32[]{:S(2)}) collective-permute-start(f32[32,128]{1,0:T(8,128)S(1)} %add.165), channel_id=1, source_target_pairs={{0,16},{1,17},{2,18},{3,19},{4,20},{5,21},{6,22},{7,23},{8,24},{9,... | collective-permute-start | bytes 49160 | tf_op jit(solution)/shard_map/ppermute | solution.py:83
  58.0 1.8 bitcast_bitcast_fusion.1
  59.8 7.9 %all-to-all-start = ((f32[8,64,128]{2,1,0:T(8,128)}), f32[8,64,128]{2,1,0:T(8,128)S(1)}, u32[]{:S(2)}, u32[]{:S(2)}) async-start(f32[8,64,128]{2,1,0:T(8,128)} %bitcast_bitcast_fusion.1), calls=%async_computation | async-start | bytes 524288 | tf_op jit(solution)/shard_map/all_to_all | solution.py:40
  67.7 5.2 %collective-permute-start.9 = (f32[32,128]{1,0:T(8,128)S(1)}, f32[32,128]{1,0:T(8,128)S(1)}, u32[]{:S(2)}, u32[]{:S(2)}) collective-permute-start(f32[32,128]{1,0:T(8,128)S(1)} %add.166), channel_id=1, source_target_pairs={{0,32},{1,33},{2,34},{3,35},{4,36},{5,37},{6,38},{7,39},{8,40},{9,... | collective-permute-start | bytes 49160 | tf_op jit(solution)/shard_map/ppermute | solution.py:83
  73.0 1.4 collective-permute-done.9
  74.4 2.8 %collective-permute-start.10 = (f32[32,128]{1,0:T(8,128)S(1)}, f32[32,128]{1,0:T(8,128)S(1)}, u32[]{:S(2)}, u32[]{:S(2)}) collective-permute-start(f32[32,128]{1,0:T(8,128)S(1)} %add.167), channel_id=1, source_target_pairs={{0,64},{1,65},{2,66},{3,67},{4,68},{5,69},{6,70},{7,71},{8,72},{9,... | collective-permute-start | bytes 49160 | tf_op jit(solution)/shard_map/ppermute | solution.py:83
  77.2 3.8 %collective-permute-done.10 = f32[32,128]{1,0:T(8,128)S(1)} collective-permute-done((f32[32,128]{1,0:T(8,128)S(1)}, f32[32,128]{1,0:T(8,128)S(1)}, u32[]{:S(2)}, u32[]{:S(2)}) %collective-permute-start.10) | collective-permute-done | bytes 16416 | tf_op jit(solution)/shard_map/ppermute | solution.py:83
  81.1 11.6 %all_to_all.25 = f32[8,96,128]{2,1,0:T(8,128)S(1)} all-to-all(f32[8,96,128]{2,1,0:T(8,128)S(1)} %broadcast_in_dim.44), channel_id=1, replica_groups={{0,1,2,3,4,5,6,7},{8,9,10,11,12,13,14,15},{16,17,18,19,20,21,22,23},{24..., dimensions={0} | all-to-all | bytes 786432 | tf_op jit(solution)/shard_map/all_to_all | solution.py:40
  92.8 0.5 fusion.20
  93.3 0.4 fusion.44
  93.7 0.6 copy-done.3
  94.3 0.4 fusion.45
  94.8 0.8 collective-permute-start.11
  95.6 1.5 collective-permute-start.13
  97.4 0.5 fusion.9
  97.9 1.3 collective-permute-start.12
  99.2 8.4 %collective-permute-start.21 = (f32[64,1024]{1,0:T(8,128)S(1)}, f32[64,1024]{1,0:T(8,128)}, u32[]{:S(2)}, u32[]{:S(2)}) collective-permute-start(f32[64,1024]{1,0:T(8,128)S(1)} %fusion.9), channel_id=1, source_target_pairs={{8,18},{9,37},{10,52},{11,67},{12,86},{13,97},{14,112},{15,135},{2... | collective-permute-start | bytes 786440 | tf_op jit(solution)/shard_map/ppermute | solution.py:83
  107.6 0.5 fusion.10
  108.1 0.8 copy.40
  109.3 0.8 fusion.31
  110.1 1.6 collective-permute-start.14
  111.7 1.5 fusion.8
  113.2 1.4 collective-permute-start.20
  115.8 1.1 collective-permute-done.15
  117.1 2.3 %collective-permute-start.16 = (f32[64,128]{1,0:T(8,128)S(1)}, f32[64,128]{1,0:T(8,128)S(1)}, u32[]{:S(2)}, u32[]{:S(2)}) collective-permute-start(f32[64,128]{1,0:T(8,128)S(1)} %fusion.143), channel_id=1, source_target_pairs={{0,128},{1,129},{2,130},{3,131},{4,132},{5,133},{6,134},{7,135},{8... | collective-permute-start | bytes 98312 | tf_op jit(solution)/shard_map/ppermute | solution.py:83
  119.4 2.4 %fusion.35 = f32[128,1024]{1,0:T(8,128)S(1)} fusion(bf16[1024,1024]{1,0:T(8,128)(2,1)} %get-tuple-element.12, bf16[64,1024]{1,0:T(8,128)(2,1)S(1)} %get-tuple-element.18, bf16[64,1024]{1,0:T(8,128)(2,1)S(1)} %get-tuple-element.19), kind=kOutput, calls=%fused_computation.67 | convolution fusion | flops 268959744 | bytes 2883584 | tf_op jit(solution)/shard_map/dot_general | solution.py:106
  122.2 6.1 %collective-permute-start.17 = (f32[64,128]{1,0:T(8,128)S(1)}, f32[64,128]{1,0:T(8,128)S(1)}, u32[]{:S(2)}, u32[]{:S(2)}) collective-permute-start(f32[64,128]{1,0:T(8,128)S(1)} %add.181), channel_id=1, source_target_pairs={{0,16},{1,17},{2,18},{3,19},{4,20},{5,21},{6,22},{7,23},{8,24},{9,... | collective-permute-start | bytes 98312 | tf_op jit(solution)/shard_map/ppermute | solution.py:83
  128.3 0.8 fusion.7
  129.1 0.5 collective-permute-done.17
  129.6 6.8 %collective-permute-start.18 = (f32[64,128]{1,0:T(8,128)S(1)}, f32[64,128]{1,0:T(8,128)S(1)}, u32[]{:S(2)}, u32[]{:S(2)}) collective-permute-start(f32[64,128]{1,0:T(8,128)S(1)} %add.182), channel_id=1, source_target_pairs={{0,32},{1,33},{2,34},{3,35},{4,36},{5,37},{6,38},{7,39},{8,40},{9,... | collective-permute-start | bytes 98312 | tf_op jit(solution)/shard_map/ppermute | solution.py:83
  136.4 1.8 bitcast_bitcast_fusion
  138.2 9.2 %all-to-all-start.2 = ((f32[8,64,128]{2,1,0:T(8,128)}), f32[8,64,128]{2,1,0:T(8,128)S(1)}, u32[]{:S(2)}, u32[]{:S(2)}) async-start(f32[8,64,128]{2,1,0:T(8,128)} %bitcast_bitcast_fusion), calls=%async_computation.2 | async-start | bytes 524288 | tf_op jit(solution)/shard_map/all_to_all | solution.py:40
  147.5 6.1 %collective-permute-start.19 = (f32[64,128]{1,0:T(8,128)S(1)}, f32[64,128]{1,0:T(8,128)S(1)}, u32[]{:S(2)}, u32[]{:S(2)}) collective-permute-start(f32[64,128]{1,0:T(8,128)S(1)} %add.183), channel_id=1, source_target_pairs={{0,64},{1,65},{2,66},{3,67},{4,68},{5,69},{6,70},{7,71},{8,72},{9,... | collective-permute-start | bytes 98312 | tf_op jit(solution)/shard_map/ppermute | solution.py:83
  153.6 1.0 constant_dynamic-slice_fusion
  155.2 0.8 broadcast_in_dim.45
  156.0 5.1 %all-to-all-start.3 = ((f32[8,96,128]{2,1,0:T(8,128)}), f32[8,96,128]{2,1,0:T(8,128)S(1)}, u32[]{:S(2)}, u32[]{:S(2)}) async-start(f32[8,96,128]{2,1,0:T(8,128)} %broadcast_in_dim.45), calls=%async_computation.3 | async-start | bytes 786432 | tf_op jit(solution)/shard_map/all_to_all | solution.py:40
  161.1 0.4 fusion.91
  161.6 6.4 %all-to-all-done.3 = f32[8,96,128]{2,1,0:T(8,128)S(1)} async-done(((f32[8,96,128]{2,1,0:T(8,128)}), f32[8,96,128]{2,1,0:T(8,128)S(1)}, u32[]{:S(2)}, u32[]{:S(2)}) %all-to-all-start.3) | async-done | bytes 393248 | tf_op jit(solution)/shard_map/all_to_all | solution.py:40
  168.5 0.4 fusion.6
  169.4 22.1 %all_to_all.26 = f32[16,32,128]{2,1,0:T(8,128)S(1)} all-to-all(f32[16,32,128]{2,1,0:T(8,128)S(1)} %broadcast_in_dim.46), channel_id=1, replica_groups={{0,16,32,48,64,80,96,112,128,144,160,176,192,208,224,240},{1,17,33,49,6..., dimensions={0} | all-to-all | bytes 524288 | tf_op jit(solution)/shard_map/all_to_all | solution.py:40
  191.5 5.2 %collective-permute-start.22 = (f32[32,128]{1,0:T(8,128)S(1)}, f32[32,128]{1,0:T(8,128)S(1)}, u32[]{:S(2)}, u32[]{:S(2)}) collective-permute-start(f32[32,128]{1,0:T(8,128)S(1)} %reduce_sum.49), channel_id=1, source_target_pairs={{0,8},{1,9},{2,10},{3,11},{4,12},{5,13},{6,14},{7,15},{8,0},{9,1},... | collective-permute-start | bytes 49160 | tf_op jit(solution)/shard_map/ppermute | solution.py:83
  196.8 0.8 collective-permute-done.22
  197.7 1.1 fusion.52
  (102 shorter events, 6.0 us)
Async XLA Ops:
  0.6 31.5 %collective-permute-start = (f32[64,1024]{1,0:T(8,128)}, f32[64,1024]{1,0:T(8,128)S(1)}, u32[]{:S(2)}, u32[]{:S(2)}) collective-permute-start(f32[64,1024]{1,0:T(8,128)} %param.5), channel_id=1, source_target_pairs={{0,0},{19,1},{38,2},{53,3},{68,4},{87,5},{98,6},{113,7},{8,8},{27,... | collective-permute-start | bytes 786440 | tf_op jit(solution)/shard_map/ppermute | solution.py:83
  2.2 41.1 %collective-permute-start.1 = (f32[64,1024]{1,0:T(8,128)}, f32[64,1024]{1,0:T(8,128)S(1)}, u32[]{:S(2)}, u32[]{:S(2)}) collective-permute-start(f32[64,1024]{1,0:T(8,128)} %param.5), channel_id=1, source_target_pairs={{18,8},{37,9},{52,10},{67,11},{86,12},{97,13},{112,14},{135,15},{3... | collective-permute-start | bytes 786440 | tf_op jit(solution)/shard_map/ppermute | solution.py:83
  4.3 19.8 %copy-start.4 = (f32[1024,2048]{1,0:T(8,128)S(1)}, f32[1024,2048]{1,0:T(8,128)}, u32[]{:S(2)}) copy-start(f32[1024,2048]{1,0:T(8,128)} %param.6) | copy-start | bytes 25165828
  8.8 20.9 %collective-permute-start.3 = (f32[64,1024]{1,0:T(8,128)}, f32[64,1024]{1,0:T(8,128)}, u32[]{:S(2)}, u32[]{:S(2)}) collective-permute-start(f32[64,1024]{1,0:T(8,128)} %fusion.2), channel_id=1, source_target_pairs={{0,8},{1,9},{2,10},{3,11},{4,12},{5,13},{6,14},{7,15},{16,24},{17,... | collective-permute-start | bytes 786440 | tf_op jit(solution)/shard_map/ppermute | solution.py:83
  10.1 47.9 %collective-permute-start.5 = (f32[64,1024]{1,0:T(8,128)}, f32[64,1024]{1,0:T(8,128)}, u32[]{:S(2)}, u32[]{:S(2)}) collective-permute-start(f32[64,1024]{1,0:T(8,128)} %fusion.2), channel_id=1, source_target_pairs={{8,18},{9,37},{10,52},{11,67},{12,86},{13,97},{14,112},{15,135},{2... | collective-permute-start | bytes 786440 | tf_op jit(solution)/shard_map/ppermute | solution.py:83
  27.3 2.0 %copy-start.5 = (f32[64,1024]{1,0:T(8,128)S(1)}, f32[64,1024]{1,0:T(8,128)}, u32[]{:S(2)}) copy-start(f32[64,1024]{1,0:T(8,128)} %param.5) | copy-start | bytes 786436
  27.3 2.0 %copy-start.9 = (f32[1024]{0:T(1024)S(1)}, f32[1024]{0:T(1024)}, u32[]{:S(2)}) copy-start(f32[1024]{0:T(1024)} %param.8) | copy-start | bytes 12292
  30.7 27.3 %collective-permute-start.4 = (f32[64,1024]{1,0:T(8,128)S(1)}, f32[64,1024]{1,0:T(8,128)}, u32[]{:S(2)}, u32[]{:S(2)}) collective-permute-start(f32[64,1024]{1,0:T(8,128)S(1)} %add.155), channel_id=1, source_target_pairs={{0,0},{1,19},{2,38},{3,53},{4,68},{5,87},{6,98},{7,113},{8,8},{9,2... | collective-permute-start | bytes 786440 | tf_op jit(solution)/shard_map/ppermute | solution.py:83
  32.5 9.4 %copy-start.1 = (bf16[1024,1024]{1,0:T(8,128)(2,1)S(1)}, bf16[1024,1024]{1,0:T(8,128)(2,1)}, u32[]{:S(2)}) copy-start(bf16[1024,1024]{1,0:T(8,128)(2,1)} %get-tuple-element.10) | copy-start | bytes 6291460
  35.1 8.2 %collective-permute-start.2 = (f32[64,1024]{1,0:T(8,128)S(1)}, f32[64,1024]{1,0:T(8,128)S(1)}, u32[]{:S(2)}, u32[]{:S(2)}) collective-permute-start(f32[64,1024]{1,0:T(8,128)S(1)} %collective-permute-done), channel_id=1, source_target_pairs={{8,0},{9,1},{10,2},{11,3},{12,4},{13,5},{14,6},{15,7},{24,16},{25,... | collective-permute-start | bytes 786440 | tf_op jit(solution)/shard_map/ppermute | solution.py:83
  44.9 2.5 %collective-permute-start.6 = (f32[32,128]{1,0:T(8,128)S(1)}, f32[32,128]{1,0:T(8,128)S(1)}, u32[]{:S(2)}, u32[]{:S(2)}) collective-permute-start(f32[32,128]{1,0:T(8,128)S(1)} %pad_maximum_fusion.5), channel_id=1, source_target_pairs={{0,8},{1,9},{2,10},{3,11},{4,12},{5,13},{6,14},{7,15},{8,0},{9,1},... | collective-permute-start | bytes 49160 | tf_op jit(solution)/shard_map/ppermute | solution.py:83
  47.4 10.6 %copy-start.7 = (f32[64,1024]{1,0:T(8,128)S(1)}, f32[64,1024]{1,0:T(8,128)}, u32[]{:S(2)}) copy-start(f32[64,1024]{1,0:T(8,128)} %fusion.14) | copy-start | bytes 786436
  47.5 29.7 %copy-start.10 = (f32[1024]{0:T(1024)S(1)}, f32[1024]{0:T(1024)}, u32[]{:S(2)}) copy-start(f32[1024]{0:T(1024)} %param.9) | copy-start | bytes 12292
  47.5 4.1 %collective-permute-start.7 = (f32[32,128]{1,0:T(8,128)S(1)}, f32[32,128]{1,0:T(8,128)S(1)}, u32[]{:S(2)}, u32[]{:S(2)}) collective-permute-start(f32[32,128]{1,0:T(8,128)S(1)} %fusion.144), channel_id=1, source_target_pairs={{0,128},{1,129},{2,130},{3,131},{4,132},{5,133},{6,134},{7,135},{8... | collective-permute-start | bytes 49160 | tf_op jit(solution)/shard_map/ppermute | solution.py:83
  51.7 16.0 %collective-permute-start.8 = (f32[32,128]{1,0:T(8,128)S(1)}, f32[32,128]{1,0:T(8,128)S(1)}, u32[]{:S(2)}, u32[]{:S(2)}) collective-permute-start(f32[32,128]{1,0:T(8,128)S(1)} %add.165), channel_id=1, source_target_pairs={{0,16},{1,17},{2,18},{3,19},{4,20},{5,21},{6,22},{7,23},{8,24},{9,... | collective-permute-start | bytes 49160 | tf_op jit(solution)/shard_map/ppermute | solution.py:83
  59.8 21.2 %all-to-all-start = ((f32[8,64,128]{2,1,0:T(8,128)}), f32[8,64,128]{2,1,0:T(8,128)S(1)}, u32[]{:S(2)}, u32[]{:S(2)}) async-start(f32[8,64,128]{2,1,0:T(8,128)} %bitcast_bitcast_fusion.1), calls=%async_computation | async-start | bytes 524288 | tf_op jit(solution)/shard_map/all_to_all | solution.py:40
  67.7 6.7 %collective-permute-start.9 = (f32[32,128]{1,0:T(8,128)S(1)}, f32[32,128]{1,0:T(8,128)S(1)}, u32[]{:S(2)}, u32[]{:S(2)}) collective-permute-start(f32[32,128]{1,0:T(8,128)S(1)} %add.166), channel_id=1, source_target_pairs={{0,32},{1,33},{2,34},{3,35},{4,36},{5,37},{6,38},{7,39},{8,40},{9,... | collective-permute-start | bytes 49160 | tf_op jit(solution)/shard_map/ppermute | solution.py:83
  74.4 6.6 %collective-permute-start.10 = (f32[32,128]{1,0:T(8,128)S(1)}, f32[32,128]{1,0:T(8,128)S(1)}, u32[]{:S(2)}, u32[]{:S(2)}) collective-permute-start(f32[32,128]{1,0:T(8,128)S(1)} %add.167), channel_id=1, source_target_pairs={{0,64},{1,65},{2,66},{3,67},{4,68},{5,69},{6,70},{7,71},{8,72},{9,... | collective-permute-start | bytes 49160 | tf_op jit(solution)/shard_map/ppermute | solution.py:83
  81.0 12.3 %copy-start = (bf16[1024,1024]{1,0:T(8,128)(2,1)S(1)}, bf16[1024,1024]{1,0:T(8,128)(2,1)}, u32[]{:S(2)}) copy-start(bf16[1024,1024]{1,0:T(8,128)(2,1)} %get-tuple-element.12) | copy-start | bytes 6291460
  92.7 1.6 copy-start.3
  94.8 12.8 %copy-start.2 = (bf16[1024,1024]{1,0:T(8,128)(2,1)S(1)}, bf16[1024,1024]{1,0:T(8,128)(2,1)}, u32[]{:S(2)}) copy-start(bf16[1024,1024]{1,0:T(8,128)(2,1)} %get-tuple-element.10) | copy-start | bytes 6291460
  94.8 14.5 %collective-permute-start.11 = (f32[64,1024]{1,0:T(8,128)S(1)}, f32[64,1024]{1,0:T(8,128)S(1)}, u32[]{:S(2)}, u32[]{:S(2)}) collective-permute-start(f32[64,1024]{1,0:T(8,128)S(1)} %get-tuple-element.48), channel_id=1, source_target_pairs={{0,0},{19,1},{38,2},{53,3},{68,4},{87,5},{98,6},{113,7},{8,8},{27,... | collective-permute-start | bytes 786440 | tf_op jit(solution)/shard_map/ppermute | solution.py:83
  95.6 19.4 %collective-permute-start.13 = (f32[64,1024]{1,0:T(8,128)S(1)}, f32[64,1024]{1,0:T(8,128)S(1)}, u32[]{:S(2)}, u32[]{:S(2)}) collective-permute-start(f32[64,1024]{1,0:T(8,128)S(1)} %get-tuple-element.48), channel_id=1, source_target_pairs={{18,8},{37,9},{52,10},{67,11},{86,12},{97,13},{112,14},{135,15},{3... | collective-permute-start | bytes 786440 | tf_op jit(solution)/shard_map/ppermute | solution.py:83
  97.9 15.2 %collective-permute-start.12 = (f32[64,1024]{1,0:T(8,128)S(1)}, f32[64,1024]{1,0:T(8,128)S(1)}, u32[]{:S(2)}, u32[]{:S(2)}) collective-permute-start(f32[64,1024]{1,0:T(8,128)S(1)} %fusion.9), channel_id=1, source_target_pairs={{0,8},{1,9},{2,10},{3,11},{4,12},{5,13},{6,14},{7,15},{16,24},{17,... | collective-permute-start | bytes 786440 | tf_op jit(solution)/shard_map/ppermute | solution.py:83
  99.2 37.2 %collective-permute-start.21 = (f32[64,1024]{1,0:T(8,128)S(1)}, f32[64,1024]{1,0:T(8,128)}, u32[]{:S(2)}, u32[]{:S(2)}) collective-permute-start(f32[64,1024]{1,0:T(8,128)S(1)} %fusion.9), channel_id=1, source_target_pairs={{8,18},{9,37},{10,52},{11,67},{12,86},{13,97},{14,112},{15,135},{2... | collective-permute-start | bytes 786440 | tf_op jit(solution)/shard_map/ppermute | solution.py:83
  110.1 4.8 %collective-permute-start.14 = (f32[64,1024]{1,0:T(8,128)S(1)}, f32[64,1024]{1,0:T(8,128)S(1)}, u32[]{:S(2)}, u32[]{:S(2)}) collective-permute-start(f32[64,1024]{1,0:T(8,128)S(1)} %collective-permute-done.11), channel_id=1, source_target_pairs={{8,0},{9,1},{10,2},{11,3},{12,4},{13,5},{14,6},{15,7},{24,16},{25,... | collective-permute-start | bytes 786440 | tf_op jit(solution)/shard_map/ppermute | solution.py:83
  113.2 23.2 %collective-permute-start.20 = (f32[64,1024]{1,0:T(8,128)S(1)}, f32[64,1024]{1,0:T(8,128)}, u32[]{:S(2)}, u32[]{:S(2)}) collective-permute-start(f32[64,1024]{1,0:T(8,128)S(1)} %add.174), channel_id=1, source_target_pairs={{0,0},{1,19},{2,38},{3,53},{4,68},{5,87},{6,98},{7,113},{8,8},{9,2... | collective-permute-start | bytes 786440 | tf_op jit(solution)/shard_map/ppermute | solution.py:83
  115.7 1.2 collective-permute-start.15
  117.1 5.1 %collective-permute-start.16 = (f32[64,128]{1,0:T(8,128)S(1)}, f32[64,128]{1,0:T(8,128)S(1)}, u32[]{:S(2)}, u32[]{:S(2)}) collective-permute-start(f32[64,128]{1,0:T(8,128)S(1)} %fusion.143), channel_id=1, source_target_pairs={{0,128},{1,129},{2,130},{3,131},{4,132},{5,133},{6,134},{7,135},{8... | collective-permute-start | bytes 98312 | tf_op jit(solution)/shard_map/ppermute | solution.py:83
  121.8 14.6 %copy-start.6 = (f32[64,1024]{1,0:T(8,128)S(1)}, f32[64,1024]{1,0:T(8,128)}, u32[]{:S(2)}) copy-start(f32[64,1024]{1,0:T(8,128)} %fusion.8) | copy-start | bytes 786436
  122.2 7.4 %collective-permute-start.17 = (f32[64,128]{1,0:T(8,128)S(1)}, f32[64,128]{1,0:T(8,128)S(1)}, u32[]{:S(2)}, u32[]{:S(2)}) collective-permute-start(f32[64,128]{1,0:T(8,128)S(1)} %add.181), channel_id=1, source_target_pairs={{0,16},{1,17},{2,18},{3,19},{4,20},{5,21},{6,22},{7,23},{8,24},{9,... | collective-permute-start | bytes 98312 | tf_op jit(solution)/shard_map/ppermute | solution.py:83
  129.6 17.9 %collective-permute-start.18 = (f32[64,128]{1,0:T(8,128)S(1)}, f32[64,128]{1,0:T(8,128)S(1)}, u32[]{:S(2)}, u32[]{:S(2)}) collective-permute-start(f32[64,128]{1,0:T(8,128)S(1)} %add.182), channel_id=1, source_target_pairs={{0,32},{1,33},{2,34},{3,35},{4,36},{5,37},{6,38},{7,39},{8,40},{9,... | collective-permute-start | bytes 98312 | tf_op jit(solution)/shard_map/ppermute | solution.py:83
  138.2 16.7 %all-to-all-start.2 = ((f32[8,64,128]{2,1,0:T(8,128)}), f32[8,64,128]{2,1,0:T(8,128)S(1)}, u32[]{:S(2)}, u32[]{:S(2)}) async-start(f32[8,64,128]{2,1,0:T(8,128)} %bitcast_bitcast_fusion), calls=%async_computation.2 | async-start | bytes 524288 | tf_op jit(solution)/shard_map/all_to_all | solution.py:40
  147.5 7.4 %collective-permute-start.19 = (f32[64,128]{1,0:T(8,128)S(1)}, f32[64,128]{1,0:T(8,128)S(1)}, u32[]{:S(2)}, u32[]{:S(2)}) collective-permute-start(f32[64,128]{1,0:T(8,128)S(1)} %add.183), channel_id=1, source_target_pairs={{0,64},{1,65},{2,66},{3,67},{4,68},{5,69},{6,70},{7,71},{8,72},{9,... | collective-permute-start | bytes 98312 | tf_op jit(solution)/shard_map/ppermute | solution.py:83
  156.0 12.0 %all-to-all-start.3 = ((f32[8,96,128]{2,1,0:T(8,128)}), f32[8,96,128]{2,1,0:T(8,128)S(1)}, u32[]{:S(2)}, u32[]{:S(2)}) async-start(f32[8,96,128]{2,1,0:T(8,128)} %broadcast_in_dim.45), calls=%async_computation.3 | async-start | bytes 786432 | tf_op jit(solution)/shard_map/all_to_all | solution.py:40
  168.5 30.3 %copy-start.8 = (f32[64,64]{1,0:T(8,128)}, f32[64,64]{1,0:T(8,128)S(1)}, u32[]{:S(2)}) copy-start(f32[64,64]{1,0:T(8,128)S(1)} %fusion.92) | copy-start | bytes 49156
  191.5 6.1 %collective-permute-start.22 = (f32[32,128]{1,0:T(8,128)S(1)}, f32[32,128]{1,0:T(8,128)S(1)}, u32[]{:S(2)}, u32[]{:S(2)}) collective-permute-start(f32[32,128]{1,0:T(8,128)S(1)} %reduce_sum.49), channel_id=1, source_target_pairs={{0,8},{1,9},{2,10},{3,11},{4,12},{5,13},{6,14},{7,15},{8,0},{9,1},... | collective-permute-start | bytes 49160 | tf_op jit(solution)/shard_map/ppermute | solution.py:83

commit v4 on v3

--- a/solution.py
+++ b/solution.py
@@ -22,18 +22,13 @@
             bit: [(number(row, p), number(row ^ bit, p)) for row, p in every]
             for bit in (1 << n for n in range(rows.bit_length() - 1))
         }
-        turn = lambda row: row % rows // 2 * 2 % offs
-
-        def couple(row, p, s):
-            far = row + per_device * p + s
-            return number(far, p ^ turn(far)), number(row, p)
-
-        self.fetch = [couple(row, p, 0) for row, p in every]
+        turn = lambda row: row // 2 * 2 % offs
+        self.fetch = [
+            (number(row, p ^ turn(row)), number(row - per_device * p, p)) for row, p in every
+        ]
         self.back = [(b, a) for a, b in self.fetch]
-        self.fetch_odd = [couple(row, p, 1) for row, p in every if row % 2]
-        self.back_odd = [(b, a) for a, b in self.fetch_odd]
-        self.to_odd = [(number(row - 1, p), number(row, p)) for row, p in every if row % 2]
-        self.to_even = [(b, a) for a, b in self.to_odd]
+        self.up = [(number(row, p), number(row + 1, p)) for row, p in every]
+        self.down = [(b, a) for a, b in self.up]
 
 
 def exchange(array, groups):
@@ -84,8 +79,7 @@
 
 
 def row_total(part, lay):
-    far = lay.rows // 2
-    for bit in [1, far] + [bit for bit in lay.flip if bit not in (1, far)]:
+    for bit in sorted(lay.flip, reverse=True):
         part = part + permuted(part, lay.flip[bit])
     return part
 
@@ -126,7 +120,6 @@
     total_rows = width * rows
     part = width // offs
     off_index = lax.axis_index("off")
-    odd = (lax.axis_index("row") % 2).astype(jnp.float32)
     row_ids = jnp.arange(width, dtype=jnp.int32)[:, None]
     block_of = lambda array, s: array[:, s * width : (s + 1) * width]
 
@@ -151,22 +144,19 @@
 
     def products(vecs, extra, back_of, block_for):
         near = permuted(vecs, lay.fetch)
-        far = permuted(vecs, lay.fetch_odd)
-        back_far = lax.optimization_barrier(back_of(vecs, 1))
-        up = permuted(back_far, lay.to_odd)
-        returned_far = permuted(back_far, lay.back_odd)
+        up = permuted(back_of(vecs, 1), lay.up)
         own_back = lax.optimization_barrier(back_of(vecs, 0))
         back = own_back + up
         returned = permuted(back, lay.back)
-        far = far + permuted(near, lay.to_even)
-        pair = gram(near, back) + gram(far, back_far * odd)
+        far = permuted(near, lay.down)
+        pair = gram(near, back)
         share = folded(pair + pair.T + gram(vecs, energies * vecs) * (1.0 / offs))
         block = block_for(0, own_back)
         first = lax.optimization_barrier(direct_product(near, block))
         block = block_for(1, block)
         second = lax.optimization_barrier(direct_product(far, block))
         share = row_total(jnp.concatenate([share] + extra, axis=0), lay)
-        return first + second + (returned + returned_far), share
+        return first + second + returned, share
 
     def spread(chunk, share):
         got = sent_to_all(jnp.concatenate([chunk, share], axis=0), lay.row)

time: 200 us -> 189 us (0.945)
  waiting for transfers between devices: 18 us -> 38.2 us
  starting transfers between devices: 98.9 us -> 83.5 us
  blocking collectives: 33.7 us -> 27.5 us
  matrix products: 29.7 us -> 24.3 us
  other arithmetic: 12 us -> 9.02 us
    ppermute x23 -> x19, starting transfers between devices: 76.7 us -> 55.9 us  [permuted(): return lax.ppermute(array, AXES, pairs)]
    ppermute x23 -> x19, waiting for transfers between devices: 11.5 us -> 24.1 us  [permuted(): return lax.ppermute(array, AXES, pairs)]
    all_to_all x3, waiting for transfers between devices: 6.42 us -> 14.1 us  [exchange(): lax.all_to_all(array, AXES, 0, 0, axis_index_groups=groups, tiled=True)]
    all_to_all x2, blocking collectives: 33.7 us -> 27.5 us  [exchange(): lax.all_to_all(array, AXES, 0, 0, axis_index_groups=groups, tiled=True)]
    all_to_all x3, starting transfers between devices: 22.2 us -> 27.7 us  [exchange(): lax.all_to_all(array, AXES, 0, 0, axis_index_groups=groups, tiled=True)]
    dot_general x12, matrix products: 14.6 us -> 11.6 us  [block_product(): lax.dot_general(left, right, (dims, ((), ())), preferred_element_type=jnp...]
    transpose x2, other arithmetic: 3.6 us -> 1.5 us  [cut(): return array.reshape(k, parts, width // parts).transpose(1, 0, 2)]
  transfers between devices with their start and end apart: 26 -> 22, of which waited for: 9 -> 11; matrix products, arithmetic and copies ran while one was open for 21% -> 16% of each run, Pallas kernels for 0% -> 0%
where the time goes in v4:
time: 189 us; the launch traced here: 188 us
  starting transfers between devices  83.5 us (44%)
  waiting for transfers between devices  38.2 us (20%)
  blocking collectives  27.5 us (15%)
  matrix products  24.3 us (13%)
  other arithmetic  9.02 us (5%)
  local copies, waits for them, and re-layouts  4.16 us (2%)
    ppermute x19, starting transfers between devices, permuted(): return lax.ppermute(array, AXES, pairs)  55.9 us
    all_to_all x3, starting transfers between devices, exchange(): lax.all_to_all(array, AXES, 0, 0, axis_index_groups=groups, tiled=True)  27.7 us
    all_to_all x2, blocking collectives, exchange(): lax.all_to_all(array, AXES, 0, 0, axis_index_groups=groups, tiled=True)  27.5 us
    ppermute x19, waiting for transfers between devices, permuted(): return lax.ppermute(array, AXES, pairs)  24.1 us
    all_to_all x3, waiting for transfers between devices, exchange(): lax.all_to_all(array, AXES, 0, 0, axis_index_groups=groups, tiled=True)  14.1 us
    dot_general x12, matrix products, block_product(): lax.dot_general(left, right, (dims, ((), ())), preferred_element_type=jnp...  11.6 us
    dot_general x2, matrix products, back_first(): jnp.dot(vecs * masks[s], block_of(tiles, s), precision=lax.Precision.HIGH...  7.51 us
    convert_element_type x6, other arithmetic, halves(): return (high.astype(jnp.bfloat16), (array - high).astype(jnp.bfloat16))  4.84 us
  transfers between devices with their start and end apart: 22, of which 11 were waited for; matrix products, arithmetic and copies ran while one was open for 16% of the time, Pallas kernels for 0%

profile of v4, /device:TPU:1, one launch (start us, length us, event | category | flops | bytes accessed | tf_op | source)
XLA Modules:
  0.0 188.1 jit_solution(1835961921691878824)
XLA Ops:
  0.6 1.6 collective-permute-start
  2.2 0.7 compare_convert_fusion
  3.0 3.8 %fusion.2 = f32[64,1024]{1,0:T(8,128)S(1)} fusion(f32[1024,2048]{1,0:T(8,128)} %param.6, f32[64,1024]{1,0:T(8,128)} %param.5, f32[1024]{0:T(1024)S(1)} %bitcast.108), kind=kOutput, calls=%fused_computation.6 | convolution fusion | flops 402718720 | bytes 4722688 | tf_op jit(solution)/shard_map/dot_general | solution.py:135
  6.8 12.3 %collective-permute-start.2 = (f32[64,1024]{1,0:T(8,128)S(1)}, f32[64,1024]{1,0:T(8,128)S(1)}, u32[]{:S(2)}, u32[]{:S(2)}) collective-permute-start(f32[64,1024]{1,0:T(8,128)S(1)} %fusion.2), channel_id=1, source_target_pairs={{0,8},{1,9},{2,10},{3,11},{4,12},{5,13},{6,14},{7,15},{8,16},{9,17... | collective-permute-start | bytes 786440 | tf_op jit(solution)/shard_map/ppermute | solution.py:78
  19.1 1.3 fusion.97
  20.4 3.7 %fusion.4 = f32[64,1024]{1,0:T(8,128)S(1)} fusion(f32[1024,2048]{1,0:T(8,128)} %param.6, f32[64,1024]{1,0:T(8,128)} %param.5, f32[1024]{0:T(1024)S(1)} %bitcast.107), kind=kOutput, calls=%fused_computation.10 | convolution fusion | flops 402718720 | bytes 4722688 | tf_op jit(solution)/shard_map/dot_general | solution.py:135
  24.1 0.7 iota_compare_fusion.3
  24.8 2.7 %fusion = (bf16[1024,1024]{1,0:T(8,128)(2,1)}, bf16[1024,1024]{1,0:T(8,128)(2,1)}) fusion(f32[1024,2048]{1,0:T(8,128)S(1)} %copy-done.7, pred[1024]{0:T(1024)(128)(4,1)S(1)} %iota_compare_fusion.3), kind=kLoop, calls=%fused_computation.4 | loop fusion | flops 5242880 | bytes 8389632 | tf_op jit(solution)/shard_map/convert_element_type | solution.py:94
  27.5 0.6 iota_compare_fusion.2
  28.2 2.0 %fusion.1 = (bf16[1024,1024]{1,0:T(8,128)(2,1)S(1)}, bf16[1024,1024]{1,0:T(8,128)(2,1)}) fusion(f32[1024,2048]{1,0:T(8,128)S(1)} %copy-done.7, pred[1024]{0:T(1024)(128)(4,1)S(1)} %iota_compare_fusion.2), kind=kLoop, calls=%fused_computation.5 | loop fusion | flops 5242880 | bytes 8389632 | tf_op jit(solution)/shard_map/convert_element_type | solution.py:94
  30.2 0.4 fusion.16
  30.6 0.7 collective-permute-start.3
  31.3 0.4 fusion.98
  32.1 2.6 %fusion.24 = f32[128,1024]{1,0:T(8,128)S(1)} fusion(bf16[1024,1024]{1,0:T(8,128)(2,1)} %get-tuple-element.9, bf16[64,1024]{1,0:T(8,128)(2,1)S(1)} %get-tuple-element.26, bf16[64,1024]{1,0:T(8,128)(2,1)S(1)} %get-tuple-element.27), kind=kOutput, calls=%fused_computation.54 | convolution fusion | flops 268959744 | bytes 2883584 | tf_op jit(solution)/shard_map/dot_general | solution.py:100
  34.9 1.1 collective-permute-done.4
  36.0 2.6 %collective-permute-start.5 = (f32[32,128]{1,0:T(8,128)S(1)}, f32[32,128]{1,0:T(8,128)S(1)}, u32[]{:S(2)}, u32[]{:S(2)}) collective-permute-start(f32[32,128]{1,0:T(8,128)S(1)} %fusion.137), channel_id=1, source_target_pairs={{0,64},{1,65},{2,66},{3,67},{4,68},{5,69},{6,70},{7,71},{8,72},{9,... | collective-permute-start | bytes 49160 | tf_op jit(solution)/shard_map/ppermute | solution.py:78
  38.7 0.8 fusion.15
  39.4 3.1 %collective-permute-done.5 = f32[32,128]{1,0:T(8,128)S(1)} collective-permute-done((f32[32,128]{1,0:T(8,128)S(1)}, f32[32,128]{1,0:T(8,128)S(1)}, u32[]{:S(2)}, u32[]{:S(2)}) %collective-permute-start.5) | collective-permute-done | bytes 16416 | tf_op jit(solution)/shard_map/ppermute | solution.py:78
  42.6 3.9 %collective-permute-start.6 = (f32[32,128]{1,0:T(8,128)S(1)}, f32[32,128]{1,0:T(8,128)S(1)}, u32[]{:S(2)}, u32[]{:S(2)}) collective-permute-start(f32[32,128]{1,0:T(8,128)S(1)} %add.131), channel_id=1, source_target_pairs={{0,32},{1,33},{2,34},{3,35},{4,36},{5,37},{6,38},{7,39},{8,40},{9,... | collective-permute-start | bytes 49160 | tf_op jit(solution)/shard_map/ppermute | solution.py:78
  46.5 0.8 fusion.28
  47.4 0.8 fusion.13
  48.2 0.8 bitcast_bitcast_fusion.1
  48.9 12.5 %all-to-all-start = ((f32[8,64,128]{2,1,0:T(8,128)}), f32[8,64,128]{2,1,0:T(8,128)S(1)}, u32[]{:S(2)}, u32[]{:S(2)}) async-start(f32[8,64,128]{2,1,0:T(8,128)} %bitcast_bitcast_fusion.1), calls=%async_computation | async-start | bytes 524288 | tf_op jit(solution)/shard_map/all_to_all | solution.py:35
  61.5 1.3 collective-permute-start.7
  62.8 1.4 collective-permute-done.7
  64.2 5.9 %collective-permute-start.8 = (f32[32,128]{1,0:T(8,128)S(1)}, f32[32,128]{1,0:T(8,128)S(1)}, u32[]{:S(2)}, u32[]{:S(2)}) collective-permute-start(f32[32,128]{1,0:T(8,128)S(1)} %add.133), channel_id=1, source_target_pairs={{0,8},{1,9},{2,10},{3,11},{4,12},{5,13},{6,14},{7,15},{8,0},{9,1},... | collective-permute-start | bytes 49160 | tf_op jit(solution)/shard_map/ppermute | solution.py:78
  70.1 0.8 collective-permute-done.8
  71.1 13.2 %all_to_all.25 = f32[8,96,128]{2,1,0:T(8,128)S(1)} all-to-all(f32[8,96,128]{2,1,0:T(8,128)S(1)} %broadcast_in_dim.44), channel_id=1, replica_groups={{0,1,2,3,4,5,6,7},{8,9,10,11,12,13,14,15},{16,17,18,19,20,21,22,23},{24..., dimensions={0} | all-to-all | bytes 786432 | tf_op jit(solution)/shard_map/all_to_all | solution.py:35
  84.3 0.5 fusion.21
  85.2 0.7 collective-permute-start.9
  85.9 0.4 fusion.43
  86.3 0.4 fusion.42
  86.8 1.1 copy-done.4
  87.9 0.5 fusion.10
  88.4 0.5 fusion.9
  88.9 7.6 %collective-permute-start.10 = (f32[64,1024]{1,0:T(8,128)S(1)}, f32[64,1024]{1,0:T(8,128)S(1)}, u32[]{:S(2)}, u32[]{:S(2)}) collective-permute-start(f32[64,1024]{1,0:T(8,128)S(1)} %fusion.9), channel_id=1, source_target_pairs={{0,8},{1,9},{2,10},{3,11},{4,12},{5,13},{6,14},{7,15},{8,16},{9,17... | collective-permute-start | bytes 786440 | tf_op jit(solution)/shard_map/ppermute | solution.py:78
  96.5 0.4 convolution_multiply_fusion.2
  96.8 9.2 %collective-permute-done.10 = f32[64,1024]{1,0:T(8,128)S(1)} collective-permute-done((f32[64,1024]{1,0:T(8,128)S(1)}, f32[64,1024]{1,0:T(8,128)S(1)}, u32[]{:S(2)}, u32[]{:S(2)}) %collective-permute-start.10) | collective-permute-done | bytes 262176 | tf_op jit(solution)/shard_map/ppermute | solution.py:78
  106.1 0.4 fusion.99
  106.9 3.1 %collective-permute-start.11 = (f32[64,128]{1,0:T(8,128)S(1)}, f32[64,128]{1,0:T(8,128)S(1)}, u32[]{:S(2)}, u32[]{:S(2)}) collective-permute-start(f32[64,128]{1,0:T(8,128)S(1)} %maximum_maximum_fusion), channel_id=1, source_target_pairs={{0,128},{1,129},{2,130},{3,131},{4,132},{5,133},{6,134},{7,135},{8... | collective-permute-start | bytes 98312 | tf_op jit(solution)/shard_map/ppermute | solution.py:78
  110.0 0.8 collective-permute-start.17
  110.9 0.4 collective-permute-done.11
  111.4 2.0 %collective-permute-start.12 = (f32[64,128]{1,0:T(8,128)S(1)}, f32[64,128]{1,0:T(8,128)S(1)}, u32[]{:S(2)}, u32[]{:S(2)}) collective-permute-start(f32[64,128]{1,0:T(8,128)S(1)} %fusion.136), channel_id=1, source_target_pairs={{0,64},{1,65},{2,66},{3,67},{4,68},{5,69},{6,70},{7,71},{8,72},{9,... | collective-permute-start | bytes 98312 | tf_op jit(solution)/shard_map/ppermute | solution.py:78
  113.4 5.0 %collective-permute-done.12 = f32[64,128]{1,0:T(8,128)S(1)} collective-permute-done((f32[64,128]{1,0:T(8,128)S(1)}, f32[64,128]{1,0:T(8,128)S(1)}, u32[]{:S(2)}, u32[]{:S(2)}) %collective-permute-start.12) | collective-permute-done | bytes 32800 | tf_op jit(solution)/shard_map/ppermute | solution.py:78
  118.4 2.4 %fusion.32 = f32[128,1024]{1,0:T(8,128)S(1)} fusion(bf16[1024,1024]{1,0:T(8,128)(2,1)} %get-tuple-element.9, bf16[64,1024]{1,0:T(8,128)(2,1)S(1)} %get-tuple-element.20, bf16[64,1024]{1,0:T(8,128)(2,1)S(1)} %get-tuple-element.21), kind=kOutput, calls=%fused_computation.63 | convolution fusion | flops 268959744 | bytes 2883584 | tf_op jit(solution)/shard_map/dot_general | solution.py:100
  120.8 6.2 %collective-permute-start.16 = (f32[64,1024]{1,0:T(8,128)S(1)}, f32[64,1024]{1,0:T(8,128)S(1)}, u32[]{:S(2)}, u32[]{:S(2)}) collective-permute-start(f32[64,1024]{1,0:T(8,128)S(1)} %collective-permute-done.9), channel_id=1, source_target_pairs={{8,0},{9,1},{10,2},{11,3},{12,4},{13,5},{14,6},{15,7},{16,8},{17,9... | collective-permute-start | bytes 786440 | tf_op jit(solution)/shard_map/ppermute | solution.py:78
  127.2 0.8 fusion.8
  127.9 2.2 %collective-permute-done.14 = f32[64,128]{1,0:T(8,128)S(1)} collective-permute-done((f32[64,128]{1,0:T(8,128)S(1)}, f32[64,128]{1,0:T(8,128)S(1)}, u32[]{:S(2)}, u32[]{:S(2)}) %collective-permute-start.14) | collective-permute-done | bytes 32800 | tf_op jit(solution)/shard_map/ppermute | solution.py:78
  130.1 3.2 %collective-permute-start.15 = (f32[64,128]{1,0:T(8,128)S(1)}, f32[64,128]{1,0:T(8,128)S(1)}, u32[]{:S(2)}, u32[]{:S(2)}) collective-permute-start(f32[64,128]{1,0:T(8,128)S(1)} %add.146), channel_id=1, source_target_pairs={{0,8},{1,9},{2,10},{3,11},{4,12},{5,13},{6,14},{7,15},{8,0},{9,1},... | collective-permute-start | bytes 98312 | tf_op jit(solution)/shard_map/ppermute | solution.py:78
  133.4 0.8 fusion.36
  134.2 0.8 fusion.7
  135.0 0.7 bitcast_bitcast_fusion
  135.8 11.7 %all-to-all-start.2 = ((f32[8,64,128]{2,1,0:T(8,128)}), f32[8,64,128]{2,1,0:T(8,128)S(1)}, u32[]{:S(2)}, u32[]{:S(2)}) async-start(f32[8,64,128]{2,1,0:T(8,128)} %bitcast_bitcast_fusion), calls=%async_computation.2 | async-start | bytes 524288 | tf_op jit(solution)/shard_map/all_to_all | solution.py:35
  147.6 6.9 %all-to-all-done.2 = f32[8,64,128]{2,1,0:T(8,128)S(1)} async-done(((f32[8,64,128]{2,1,0:T(8,128)}), f32[8,64,128]{2,1,0:T(8,128)S(1)}, u32[]{:S(2)}, u32[]{:S(2)}) %all-to-all-start.2) | async-done | bytes 262176 | tf_op jit(solution)/shard_map/all_to_all | solution.py:35
  154.9 0.8 broadcast_in_dim.45
  155.6 3.5 %all-to-all-start.3 = ((f32[8,96,128]{2,1,0:T(8,128)}), f32[8,96,128]{2,1,0:T(8,128)S(1)}, u32[]{:S(2)}, u32[]{:S(2)}) async-start(f32[8,96,128]{2,1,0:T(8,128)} %broadcast_in_dim.45), calls=%async_computation.3 | async-start | bytes 786432 | tf_op jit(solution)/shard_map/all_to_all | solution.py:35
  159.1 0.4 fusion.86
  159.5 7.1 %all-to-all-done.3 = f32[8,96,128]{2,1,0:T(8,128)S(1)} async-done(((f32[8,96,128]{2,1,0:T(8,128)}), f32[8,96,128]{2,1,0:T(8,128)S(1)}, u32[]{:S(2)}, u32[]{:S(2)}) %all-to-all-start.3) | async-done | bytes 393248 | tf_op jit(solution)/shard_map/all_to_all | solution.py:35
  167.2 0.4 fusion.6
  167.6 0.4 fusion.101
  168.1 14.3 %all_to_all.26 = f32[16,32,128]{2,1,0:T(8,128)S(1)} all-to-all(f32[16,32,128]{2,1,0:T(8,128)S(1)} %broadcast_in_dim.46), channel_id=1, replica_groups={{0,16,32,48,64,80,96,112,128,144,160,176,192,208,224,240},{1,17,33,49,6..., dimensions={0} | all-to-all | bytes 524288 | tf_op jit(solution)/shard_map/all_to_all | solution.py:35
  182.5 3.6 %collective-permute-start.18 = (f32[32,128]{1,0:T(8,128)S(1)}, f32[32,128]{1,0:T(8,128)S(1)}, u32[]{:S(2)}, u32[]{:S(2)}) collective-permute-start(f32[32,128]{1,0:T(8,128)S(1)} %reduce_sum.49), channel_id=1, source_target_pairs={{0,8},{1,9},{2,10},{3,11},{4,12},{5,13},{6,14},{7,15},{8,0},{9,1},... | collective-permute-start | bytes 49160 | tf_op jit(solution)/shard_map/ppermute | solution.py:78
  186.0 0.8 collective-permute-done.18
  186.9 1.1 fusion.48
  (93 shorter events, 3.2 us)
Async XLA Ops:
  0.6 30.7 %collective-permute-start = (f32[64,1024]{1,0:T(8,128)}, f32[64,1024]{1,0:T(8,128)S(1)}, u32[]{:S(2)}, u32[]{:S(2)}) collective-permute-start(f32[64,1024]{1,0:T(8,128)} %param.5), channel_id=1, source_target_pairs={{0,0},{1,241},{2,226},{3,211},{4,196},{5,181},{6,166},{7,151},{8,8... | collective-permute-start | bytes 786440 | tf_op jit(solution)/shard_map/ppermute | solution.py:78
  3.0 21.8 %copy-start.7 = (f32[1024,2048]{1,0:T(8,128)S(1)}, f32[1024,2048]{1,0:T(8,128)}, u32[]{:S(2)}) copy-start(f32[1024,2048]{1,0:T(8,128)} %param.6) | copy-start | bytes 25165828
  6.8 23.7 %collective-permute-start.2 = (f32[64,1024]{1,0:T(8,128)S(1)}, f32[64,1024]{1,0:T(8,128)S(1)}, u32[]{:S(2)}, u32[]{:S(2)}) collective-permute-start(f32[64,1024]{1,0:T(8,128)S(1)} %fusion.2), channel_id=1, source_target_pairs={{0,8},{1,9},{2,10},{3,11},{4,12},{5,13},{6,14},{7,15},{8,16},{9,17... | collective-permute-start | bytes 786440 | tf_op jit(solution)/shard_map/ppermute | solution.py:78
  28.1 2.0 %copy-start.8 = (f32[64,1024]{1,0:T(8,128)S(1)}, f32[64,1024]{1,0:T(8,128)}, u32[]{:S(2)}) copy-start(f32[64,1024]{1,0:T(8,128)} %param.5) | copy-start | bytes 786436
  28.1 2.0 %copy-start.10 = (f32[1024]{0:T(1024)S(1)}, f32[1024]{0:T(1024)}, u32[]{:S(2)}) copy-start(f32[1024]{0:T(1024)} %param.8) | copy-start | bytes 12292
  30.6 17.5 %collective-permute-start.3 = (f32[64,1024]{1,0:T(8,128)S(1)}, f32[64,1024]{1,0:T(8,128)S(1)}, u32[]{:S(2)}, u32[]{:S(2)}) collective-permute-start(f32[64,1024]{1,0:T(8,128)S(1)} %add.125), channel_id=1, source_target_pairs={{0,0},{241,1},{226,2},{211,3},{196,4},{181,5},{166,6},{151,7},{8,8... | collective-permute-start | bytes 786440 | tf_op jit(solution)/shard_map/ppermute | solution.py:78
  31.7 6.9 %copy-start.3 = (bf16[1024,1024]{1,0:T(8,128)(2,1)S(1)}, bf16[1024,1024]{1,0:T(8,128)(2,1)}, u32[]{:S(2)}) copy-start(bf16[1024,1024]{1,0:T(8,128)(2,1)} %get-tuple-element.10) | copy-start | bytes 6291460
  31.8 4.1 %collective-permute-start.4 = (f32[32,128]{1,0:T(8,128)S(1)}, f32[32,128]{1,0:T(8,128)S(1)}, u32[]{:S(2)}, u32[]{:S(2)}) collective-permute-start(f32[32,128]{1,0:T(8,128)S(1)} %pad_maximum_fusion.5), channel_id=1, source_target_pairs={{0,128},{1,129},{2,130},{3,131},{4,132},{5,133},{6,134},{7,135},{8... | collective-permute-start | bytes 49160 | tf_op jit(solution)/shard_map/ppermute | solution.py:78
  34.8 11.7 %copy-start = (bf16[1024,1024]{1,0:T(8,128)(2,1)S(1)}, bf16[1024,1024]{1,0:T(8,128)(2,1)}, u32[]{:S(2)}) copy-start(bf16[1024,1024]{1,0:T(8,128)(2,1)} %get-tuple-element.12) | copy-start | bytes 6291460
  34.8 11.7 %collective-permute-start.1 = (f32[64,1024]{1,0:T(8,128)S(1)}, f32[64,1024]{1,0:T(8,128)S(1)}, u32[]{:S(2)}, u32[]{:S(2)}) collective-permute-start(f32[64,1024]{1,0:T(8,128)S(1)} %collective-permute-done), channel_id=1, source_target_pairs={{8,0},{9,1},{10,2},{11,3},{12,4},{13,5},{14,6},{15,7},{16,8},{17,9... | collective-permute-start | bytes 786440 | tf_op jit(solution)/shard_map/ppermute | solution.py:78
  36.0 6.5 %collective-permute-start.5 = (f32[32,128]{1,0:T(8,128)S(1)}, f32[32,128]{1,0:T(8,128)S(1)}, u32[]{:S(2)}, u32[]{:S(2)}) collective-permute-start(f32[32,128]{1,0:T(8,128)S(1)} %fusion.137), channel_id=1, source_target_pairs={{0,64},{1,65},{2,66},{3,67},{4,68},{5,69},{6,70},{7,71},{8,72},{9,... | collective-permute-start | bytes 49160 | tf_op jit(solution)/shard_map/ppermute | solution.py:78
  42.6 18.9 %collective-permute-start.6 = (f32[32,128]{1,0:T(8,128)S(1)}, f32[32,128]{1,0:T(8,128)S(1)}, u32[]{:S(2)}, u32[]{:S(2)}) collective-permute-start(f32[32,128]{1,0:T(8,128)S(1)} %add.131), channel_id=1, source_target_pairs={{0,32},{1,33},{2,34},{3,35},{4,36},{5,37},{6,38},{7,39},{8,40},{9,... | collective-permute-start | bytes 49160 | tf_op jit(solution)/shard_map/ppermute | solution.py:78
  47.4 22.7 %copy-start.11 = (f32[1024]{0:T(1024)S(1)}, f32[1024]{0:T(1024)}, u32[]{:S(2)}) copy-start(f32[1024]{0:T(1024)} %param.9) | copy-start | bytes 12292
  48.9 22.1 %all-to-all-start = ((f32[8,64,128]{2,1,0:T(8,128)}), f32[8,64,128]{2,1,0:T(8,128)S(1)}, u32[]{:S(2)}, u32[]{:S(2)}) async-start(f32[8,64,128]{2,1,0:T(8,128)} %bitcast_bitcast_fusion.1), calls=%async_computation | async-start | bytes 524288 | tf_op jit(solution)/shard_map/all_to_all | solution.py:35
  61.5 2.7 %collective-permute-start.7 = (f32[32,128]{1,0:T(8,128)S(1)}, f32[32,128]{1,0:T(8,128)S(1)}, u32[]{:S(2)}, u32[]{:S(2)}) collective-permute-start(f32[32,128]{1,0:T(8,128)S(1)} %add.132), channel_id=1, source_target_pairs={{0,16},{1,17},{2,18},{3,19},{4,20},{5,21},{6,22},{7,23},{8,24},{9,... | collective-permute-start | bytes 49160 | tf_op jit(solution)/shard_map/ppermute | solution.py:78
  64.2 6.8 %collective-permute-start.8 = (f32[32,128]{1,0:T(8,128)S(1)}, f32[32,128]{1,0:T(8,128)S(1)}, u32[]{:S(2)}, u32[]{:S(2)}) collective-permute-start(f32[32,128]{1,0:T(8,128)S(1)} %add.133), channel_id=1, source_target_pairs={{0,8},{1,9},{2,10},{3,11},{4,12},{5,13},{6,14},{7,15},{8,0},{9,1},... | collective-permute-start | bytes 49160 | tf_op jit(solution)/shard_map/ppermute | solution.py:78
  71.0 14.9 %copy-start.6 = (bf16[1024,1024]{1,0:T(8,128)(2,1)S(1)}, bf16[1024,1024]{1,0:T(8,128)(2,1)}, u32[]{:S(2)}) copy-start(bf16[1024,1024]{1,0:T(8,128)(2,1)} %get-tuple-element.9) | copy-start | bytes 6291460
  84.3 2.0 %copy-start.1 = (bf16[1024,1024]{1,0:T(8,128)(2,1)S(1)}, bf16[1024,1024]{1,0:T(8,128)(2,1)}, u32[]{:S(2)}) copy-start(bf16[1024,1024]{1,0:T(8,128)(2,1)} %get-tuple-element.12) | copy-start | bytes 6291460
  85.2 20.9 %collective-permute-start.9 = (f32[64,1024]{1,0:T(8,128)S(1)}, f32[64,1024]{1,0:T(8,128)S(1)}, u32[]{:S(2)}, u32[]{:S(2)}) collective-permute-start(f32[64,1024]{1,0:T(8,128)S(1)} %get-tuple-element.48), channel_id=1, source_target_pairs={{0,0},{1,241},{2,226},{3,211},{4,196},{5,181},{6,166},{7,151},{8,8... | collective-permute-start | bytes 786440 | tf_op jit(solution)/shard_map/ppermute | solution.py:78
  86.3 1.6 copy-start.4
  88.9 17.1 %collective-permute-start.10 = (f32[64,1024]{1,0:T(8,128)S(1)}, f32[64,1024]{1,0:T(8,128)S(1)}, u32[]{:S(2)}, u32[]{:S(2)}) collective-permute-start(f32[64,1024]{1,0:T(8,128)S(1)} %fusion.9), channel_id=1, source_target_pairs={{0,8},{1,9},{2,10},{3,11},{4,12},{5,13},{6,14},{7,15},{8,16},{9,17... | collective-permute-start | bytes 786440 | tf_op jit(solution)/shard_map/ppermute | solution.py:78
  106.9 4.4 %collective-permute-start.11 = (f32[64,128]{1,0:T(8,128)S(1)}, f32[64,128]{1,0:T(8,128)S(1)}, u32[]{:S(2)}, u32[]{:S(2)}) collective-permute-start(f32[64,128]{1,0:T(8,128)S(1)} %maximum_maximum_fusion), channel_id=1, source_target_pairs={{0,128},{1,129},{2,130},{3,131},{4,132},{5,133},{6,134},{7,135},{8... | collective-permute-start | bytes 98312 | tf_op jit(solution)/shard_map/ppermute | solution.py:78
  110.0 17.2 %copy-start.5 = (bf16[1024,1024]{1,0:T(8,128)(2,1)S(1)}, bf16[1024,1024]{1,0:T(8,128)(2,1)}, u32[]{:S(2)}) copy-start(bf16[1024,1024]{1,0:T(8,128)(2,1)} %get-tuple-element.10) | copy-start | bytes 6291460
  110.0 25.0 %collective-permute-start.17 = (f32[64,1024]{1,0:T(8,128)S(1)}, f32[64,1024]{1,0:T(8,128)S(1)}, u32[]{:S(2)}, u32[]{:S(2)}) collective-permute-start(f32[64,1024]{1,0:T(8,128)S(1)} %add.140), channel_id=1, source_target_pairs={{0,0},{241,1},{226,2},{211,3},{196,4},{181,5},{166,6},{151,7},{8,8... | collective-permute-start | bytes 786440 | tf_op jit(solution)/shard_map/ppermute | solution.py:78
  111.4 7.0 %collective-permute-start.12 = (f32[64,128]{1,0:T(8,128)S(1)}, f32[64,128]{1,0:T(8,128)S(1)}, u32[]{:S(2)}, u32[]{:S(2)}) collective-permute-start(f32[64,128]{1,0:T(8,128)S(1)} %fusion.136), channel_id=1, source_target_pairs={{0,64},{1,65},{2,66},{3,67},{4,68},{5,69},{6,70},{7,71},{8,72},{9,... | collective-permute-start | bytes 98312 | tf_op jit(solution)/shard_map/ppermute | solution.py:78
  118.4 8.7 %collective-permute-start.13 = (f32[64,128]{1,0:T(8,128)S(1)}, f32[64,128]{1,0:T(8,128)S(1)}, u32[]{:S(2)}, u32[]{:S(2)}) collective-permute-start(f32[64,128]{1,0:T(8,128)S(1)} %add.144), channel_id=1, source_target_pairs={{0,32},{1,33},{2,34},{3,35},{4,36},{5,37},{6,38},{7,39},{8,40},{9,... | collective-permute-start | bytes 98312 | tf_op jit(solution)/shard_map/ppermute | solution.py:78
  120.8 12.6 %copy-start.2 = (bf16[1024,1024]{1,0:T(8,128)(2,1)S(1)}, bf16[1024,1024]{1,0:T(8,128)(2,1)}, u32[]{:S(2)}) copy-start(bf16[1024,1024]{1,0:T(8,128)(2,1)} %get-tuple-element.12) | copy-start | bytes 6291460
  120.8 12.5 %collective-permute-start.16 = (f32[64,1024]{1,0:T(8,128)S(1)}, f32[64,1024]{1,0:T(8,128)S(1)}, u32[]{:S(2)}, u32[]{:S(2)}) collective-permute-start(f32[64,1024]{1,0:T(8,128)S(1)} %collective-permute-done.9), channel_id=1, source_target_pairs={{8,0},{9,1},{10,2},{11,3},{12,4},{13,5},{14,6},{15,7},{16,8},{17,9... | collective-permute-start | bytes 786440 | tf_op jit(solution)/shard_map/ppermute | solution.py:78
  127.0 3.1 %collective-permute-start.14 = (f32[64,128]{1,0:T(8,128)S(1)}, f32[64,128]{1,0:T(8,128)S(1)}, u32[]{:S(2)}, u32[]{:S(2)}) collective-permute-start(f32[64,128]{1,0:T(8,128)S(1)} %add.145), channel_id=1, source_target_pairs={{0,16},{1,17},{2,18},{3,19},{4,20},{5,21},{6,22},{7,23},{8,24},{9,... | collective-permute-start | bytes 98312 | tf_op jit(solution)/shard_map/ppermute | solution.py:78
  130.1 17.4 %collective-permute-start.15 = (f32[64,128]{1,0:T(8,128)S(1)}, f32[64,128]{1,0:T(8,128)S(1)}, u32[]{:S(2)}, u32[]{:S(2)}) collective-permute-start(f32[64,128]{1,0:T(8,128)S(1)} %add.146), channel_id=1, source_target_pairs={{0,8},{1,9},{2,10},{3,11},{4,12},{5,13},{6,14},{7,15},{8,0},{9,1},... | collective-permute-start | bytes 98312 | tf_op jit(solution)/shard_map/ppermute | solution.py:78
  135.8 18.8 %all-to-all-start.2 = ((f32[8,64,128]{2,1,0:T(8,128)}), f32[8,64,128]{2,1,0:T(8,128)S(1)}, u32[]{:S(2)}, u32[]{:S(2)}) async-start(f32[8,64,128]{2,1,0:T(8,128)} %bitcast_bitcast_fusion), calls=%async_computation.2 | async-start | bytes 524288 | tf_op jit(solution)/shard_map/all_to_all | solution.py:35
  155.6 11.0 %all-to-all-start.3 = ((f32[8,96,128]{2,1,0:T(8,128)}), f32[8,96,128]{2,1,0:T(8,128)S(1)}, u32[]{:S(2)}, u32[]{:S(2)}) async-start(f32[8,96,128]{2,1,0:T(8,128)} %broadcast_in_dim.45), calls=%async_computation.3 | async-start | bytes 786432 | tf_op jit(solution)/shard_map/all_to_all | solution.py:35
  167.2 20.9 %copy-start.9 = (f32[64,64]{1,0:T(8,128)}, f32[64,64]{1,0:T(8,128)S(1)}, u32[]{:S(2)}) copy-start(f32[64,64]{1,0:T(8,128)S(1)} %fusion.87) | copy-start | bytes 49156
  182.5 4.4 %collective-permute-start.18 = (f32[32,128]{1,0:T(8,128)S(1)}, f32[32,128]{1,0:T(8,128)S(1)}, u32[]{:S(2)}, u32[]{:S(2)}) collective-permute-start(f32[32,128]{1,0:T(8,128)S(1)} %reduce_sum.49), channel_id=1, source_target_pairs={{0,8},{1,9},{2,10},{3,11},{4,12},{5,13},{6,14},{7,15},{8,0},{9,1},... | collective-permute-start | bytes 49160 | tf_op jit(solution)/shard_map/ppermute | solution.py:78

commit v5 on v4

--- a/solution.py
+++ b/solution.py
@@ -85,8 +85,8 @@
 
 
 def line_total(part, lay):
-    part = jnp.sum(sent_to_all(part, lay.line), axis=0)
-    return part + permuted(part, lay.flip[1])
+    part = part + permuted(part, lay.flip[1])
+    return jnp.sum(sent_to_all(part, lay.line), axis=0)
 
 
 def halves(array):
@@ -182,7 +182,8 @@
         lambda vecs, s: back_product(vecs, blocks[s]),
         lambda s, _: blocks[s],
     )
-    image = energy_chunk * moved_chunk + jnp.sum(exchange(cut(part, offs), lay.row), axis=0)
+    image = jnp.sum(exchange(cut(part, offs), lay.row), axis=0)
+    image = energy_chunk * moved_chunk + image
     fix = 1.5 * identity - 0.5 * unfolded(share[count // 2 :]) / total_rows
     chunk = exact(fix.T, moved_chunk - precond_chunk * image)
     stepped, ritz = spread(chunk, share[: count // 2])

time: 189 us -> 189 us (level)
  transfers between devices with their start and end apart: 22 -> 22, of which waited for: 11 -> 11; matrix products, arithmetic and copies ran while one was open for 16% -> 17% of each run, Pallas kernels for 0% -> 0%
where the time goes in v5:
time: 189 us; the launch traced here: 188 us
  starting transfers between devices  82 us (43%)
  waiting for transfers between devices  38.2 us (20%)
  blocking collectives  28.8 us (15%)
  matrix products  24.3 us (13%)
  other arithmetic  9.09 us (5%)
  local copies, waits for them, and re-layouts  4.16 us (2%)
    ppermute x19, starting transfers between devices, permuted(): return lax.ppermute(array, AXES, pairs)  54.3 us
    all_to_all x2, blocking collectives, exchange(): lax.all_to_all(array, AXES, 0, 0, axis_index_groups=groups, tiled=True)  28.8 us
    all_to_all x3, starting transfers between devices, exchange(): lax.all_to_all(array, AXES, 0, 0, axis_index_groups=groups, tiled=True)  27.7 us
    ppermute x19, waiting for transfers between devices, permuted(): return lax.ppermute(array, AXES, pairs)  24.1 us
    all_to_all x3, waiting for transfers between devices, exchange(): lax.all_to_all(array, AXES, 0, 0, axis_index_groups=groups, tiled=True)  14.1 us
    dot_general x12, matrix products, block_product(): lax.dot_general(left, right, (dims, ((), ())), preferred_element_type=jnp...  11.6 us
    dot_general x2, matrix products, back_first(): jnp.dot(vecs * masks[s], block_of(tiles, s), precision=lax.Precision.HIGH...  7.51 us
    convert_element_type x6, other arithmetic, halves(): return (high.astype(jnp.bfloat16), (array - high).astype(jnp.bfloat16))  4.84 us
  transfers between devices with their start and end apart: 22, of which 11 were waited for; matrix products, arithmetic and copies ran while one was open for 17% of the time, Pallas kernels for 0%

profile of v5, /device:TPU:1, one launch (start us, length us, event | category | flops | bytes accessed | tf_op | source)
XLA Modules:
  0.0 187.8 jit_solution(9216897286777226281)
XLA Ops:
  0.6 1.6 collective-permute-start
  2.2 0.7 compare_convert_fusion
  3.0 3.8 %fusion.2 = f32[64,1024]{1,0:T(8,128)S(1)} fusion(f32[1024,2048]{1,0:T(8,128)} %param.6, f32[64,1024]{1,0:T(8,128)} %param.5, f32[1024]{0:T(1024)S(1)} %bitcast.108), kind=kOutput, calls=%fused_computation.6 | convolution fusion | flops 402718720 | bytes 4722688 | tf_op jit(solution)/shard_map/dot_general | solution.py:135
  6.8 12.3 %collective-permute-start.2 = (f32[64,1024]{1,0:T(8,128)S(1)}, f32[64,1024]{1,0:T(8,128)S(1)}, u32[]{:S(2)}, u32[]{:S(2)}) collective-permute-start(f32[64,1024]{1,0:T(8,128)S(1)} %fusion.2), channel_id=1, source_target_pairs={{0,8},{1,9},{2,10},{3,11},{4,12},{5,13},{6,14},{7,15},{8,16},{9,17... | collective-permute-start | bytes 786440 | tf_op jit(solution)/shard_map/ppermute | solution.py:78
  19.1 1.3 fusion.97
  20.4 3.7 %fusion.4 = f32[64,1024]{1,0:T(8,128)S(1)} fusion(f32[1024,2048]{1,0:T(8,128)} %param.6, f32[64,1024]{1,0:T(8,128)} %param.5, f32[1024]{0:T(1024)S(1)} %bitcast.107), kind=kOutput, calls=%fused_computation.10 | convolution fusion | flops 402718720 | bytes 4722688 | tf_op jit(solution)/shard_map/dot_general | solution.py:135
  24.1 0.7 iota_compare_fusion.3
  24.8 2.7 %fusion = (bf16[1024,1024]{1,0:T(8,128)(2,1)}, bf16[1024,1024]{1,0:T(8,128)(2,1)}) fusion(f32[1024,2048]{1,0:T(8,128)S(1)} %copy-done.7, pred[1024]{0:T(1024)(128)(4,1)S(1)} %iota_compare_fusion.3), kind=kLoop, calls=%fused_computation.4 | loop fusion | flops 5242880 | bytes 8389632 | tf_op jit(solution)/shard_map/convert_element_type | solution.py:94
  27.5 0.6 iota_compare_fusion.2
  28.2 2.0 %fusion.1 = (bf16[1024,1024]{1,0:T(8,128)(2,1)S(1)}, bf16[1024,1024]{1,0:T(8,128)(2,1)}) fusion(f32[1024,2048]{1,0:T(8,128)S(1)} %copy-done.7, pred[1024]{0:T(1024)(128)(4,1)S(1)} %iota_compare_fusion.2), kind=kLoop, calls=%fused_computation.5 | loop fusion | flops 5242880 | bytes 8389632 | tf_op jit(solution)/shard_map/convert_element_type | solution.py:94
  30.2 0.4 fusion.16
  30.6 0.7 collective-permute-start.3
  31.3 0.4 fusion.98
  32.1 2.6 %fusion.24 = f32[128,1024]{1,0:T(8,128)S(1)} fusion(bf16[1024,1024]{1,0:T(8,128)(2,1)} %get-tuple-element.9, bf16[64,1024]{1,0:T(8,128)(2,1)S(1)} %get-tuple-element.26, bf16[64,1024]{1,0:T(8,128)(2,1)S(1)} %get-tuple-element.27), kind=kOutput, calls=%fused_computation.54 | convolution fusion | flops 268959744 | bytes 2883584 | tf_op jit(solution)/shard_map/dot_general | solution.py:100
  34.9 1.1 collective-permute-done.4
  36.0 2.6 %collective-permute-start.5 = (f32[32,128]{1,0:T(8,128)S(1)}, f32[32,128]{1,0:T(8,128)S(1)}, u32[]{:S(2)}, u32[]{:S(2)}) collective-permute-start(f32[32,128]{1,0:T(8,128)S(1)} %fusion.138), channel_id=1, source_target_pairs={{0,64},{1,65},{2,66},{3,67},{4,68},{5,69},{6,70},{7,71},{8,72},{9,... | collective-permute-start | bytes 49160 | tf_op jit(solution)/shard_map/ppermute | solution.py:78
  38.7 0.8 fusion.15
  39.4 3.1 %collective-permute-done.5 = f32[32,128]{1,0:T(8,128)S(1)} collective-permute-done((f32[32,128]{1,0:T(8,128)S(1)}, f32[32,128]{1,0:T(8,128)S(1)}, u32[]{:S(2)}, u32[]{:S(2)}) %collective-permute-start.5) | collective-permute-done | bytes 16416 | tf_op jit(solution)/shard_map/ppermute | solution.py:78
  42.6 3.9 %collective-permute-start.6 = (f32[32,128]{1,0:T(8,128)S(1)}, f32[32,128]{1,0:T(8,128)S(1)}, u32[]{:S(2)}, u32[]{:S(2)}) collective-permute-start(f32[32,128]{1,0:T(8,128)S(1)} %add.131), channel_id=1, source_target_pairs={{0,32},{1,33},{2,34},{3,35},{4,36},{5,37},{6,38},{7,39},{8,40},{9,... | collective-permute-start | bytes 49160 | tf_op jit(solution)/shard_map/ppermute | solution.py:78
  46.5 0.8 fusion.28
  47.4 0.8 fusion.13
  48.2 0.8 bitcast_bitcast_fusion.1
  48.9 12.5 %all-to-all-start = ((f32[8,64,128]{2,1,0:T(8,128)}), f32[8,64,128]{2,1,0:T(8,128)S(1)}, u32[]{:S(2)}, u32[]{:S(2)}) async-start(f32[8,64,128]{2,1,0:T(8,128)} %bitcast_bitcast_fusion.1), calls=%async_computation | async-start | bytes 524288 | tf_op jit(solution)/shard_map/all_to_all | solution.py:35
  61.5 1.3 collective-permute-start.7
  62.8 1.4 collective-permute-done.7
  64.2 5.9 %collective-permute-start.8 = (f32[32,128]{1,0:T(8,128)S(1)}, f32[32,128]{1,0:T(8,128)S(1)}, u32[]{:S(2)}, u32[]{:S(2)}) collective-permute-start(f32[32,128]{1,0:T(8,128)S(1)} %add.133), channel_id=1, source_target_pairs={{0,8},{1,9},{2,10},{3,11},{4,12},{5,13},{6,14},{7,15},{8,0},{9,1},... | collective-permute-start | bytes 49160 | tf_op jit(solution)/shard_map/ppermute | solution.py:78
  70.1 0.8 collective-permute-done.8
  71.1 13.2 %all_to_all.25 = f32[8,96,128]{2,1,0:T(8,128)S(1)} all-to-all(f32[8,96,128]{2,1,0:T(8,128)S(1)} %broadcast_in_dim.44), channel_id=1, replica_groups={{0,1,2,3,4,5,6,7},{8,9,10,11,12,13,14,15},{16,17,18,19,20,21,22,23},{24..., dimensions={0} | all-to-all | bytes 786432 | tf_op jit(solution)/shard_map/all_to_all | solution.py:35
  84.3 0.5 fusion.21
  85.2 0.7 collective-permute-start.9
  85.9 0.4 fusion.43
  86.3 0.4 fusion.42
  86.8 1.1 copy-done.4
  87.9 0.5 fusion.10
  88.4 0.5 fusion.9
  88.9 7.6 %collective-permute-start.10 = (f32[64,1024]{1,0:T(8,128)S(1)}, f32[64,1024]{1,0:T(8,128)S(1)}, u32[]{:S(2)}, u32[]{:S(2)}) collective-permute-start(f32[64,1024]{1,0:T(8,128)S(1)} %fusion.9), channel_id=1, source_target_pairs={{0,8},{1,9},{2,10},{3,11},{4,12},{5,13},{6,14},{7,15},{8,16},{9,17... | collective-permute-start | bytes 786440 | tf_op jit(solution)/shard_map/ppermute | solution.py:78
  96.5 0.4 convolution_multiply_fusion.2
  96.8 9.2 %collective-permute-done.10 = f32[64,1024]{1,0:T(8,128)S(1)} collective-permute-done((f32[64,1024]{1,0:T(8,128)S(1)}, f32[64,1024]{1,0:T(8,128)S(1)}, u32[]{:S(2)}, u32[]{:S(2)}) %collective-permute-start.10) | collective-permute-done | bytes 262176 | tf_op jit(solution)/shard_map/ppermute | solution.py:78
  106.1 0.4 fusion.99
  106.9 3.1 %collective-permute-start.11 = (f32[64,128]{1,0:T(8,128)S(1)}, f32[64,128]{1,0:T(8,128)S(1)}, u32[]{:S(2)}, u32[]{:S(2)}) collective-permute-start(f32[64,128]{1,0:T(8,128)S(1)} %maximum_maximum_fusion), channel_id=1, source_target_pairs={{0,128},{1,129},{2,130},{3,131},{4,132},{5,133},{6,134},{7,135},{8... | collective-permute-start | bytes 98312 | tf_op jit(solution)/shard_map/ppermute | solution.py:78
  110.0 0.8 collective-permute-start.17
  110.9 0.4 collective-permute-done.11
  111.4 2.0 %collective-permute-start.12 = (f32[64,128]{1,0:T(8,128)S(1)}, f32[64,128]{1,0:T(8,128)S(1)}, u32[]{:S(2)}, u32[]{:S(2)}) collective-permute-start(f32[64,128]{1,0:T(8,128)S(1)} %fusion.137), channel_id=1, source_target_pairs={{0,64},{1,65},{2,66},{3,67},{4,68},{5,69},{6,70},{7,71},{8,72},{9,... | collective-permute-start | bytes 98312 | tf_op jit(solution)/shard_map/ppermute | solution.py:78
  113.4 5.0 %collective-permute-done.12 = f32[64,128]{1,0:T(8,128)S(1)} collective-permute-done((f32[64,128]{1,0:T(8,128)S(1)}, f32[64,128]{1,0:T(8,128)S(1)}, u32[]{:S(2)}, u32[]{:S(2)}) %collective-permute-start.12) | collective-permute-done | bytes 32800 | tf_op jit(solution)/shard_map/ppermute | solution.py:78
  118.4 2.4 %fusion.32 = f32[128,1024]{1,0:T(8,128)S(1)} fusion(bf16[1024,1024]{1,0:T(8,128)(2,1)} %get-tuple-element.9, bf16[64,1024]{1,0:T(8,128)(2,1)S(1)} %get-tuple-element.20, bf16[64,1024]{1,0:T(8,128)(2,1)S(1)} %get-tuple-element.21), kind=kOutput, calls=%fused_computation.63 | convolution fusion | flops 268959744 | bytes 2883584 | tf_op jit(solution)/shard_map/dot_general | solution.py:100
  120.8 6.2 %collective-permute-start.16 = (f32[64,1024]{1,0:T(8,128)S(1)}, f32[64,1024]{1,0:T(8,128)S(1)}, u32[]{:S(2)}, u32[]{:S(2)}) collective-permute-start(f32[64,1024]{1,0:T(8,128)S(1)} %collective-permute-done.9), channel_id=1, source_target_pairs={{8,0},{9,1},{10,2},{11,3},{12,4},{13,5},{14,6},{15,7},{16,8},{17,9... | collective-permute-start | bytes 786440 | tf_op jit(solution)/shard_map/ppermute | solution.py:78
  127.2 0.8 fusion.8
  127.9 2.2 %collective-permute-done.14 = f32[64,128]{1,0:T(8,128)S(1)} collective-permute-done((f32[64,128]{1,0:T(8,128)S(1)}, f32[64,128]{1,0:T(8,128)S(1)}, u32[]{:S(2)}, u32[]{:S(2)}) %collective-permute-start.14) | collective-permute-done | bytes 32800 | tf_op jit(solution)/shard_map/ppermute | solution.py:78
  130.1 3.2 %collective-permute-start.15 = (f32[64,128]{1,0:T(8,128)S(1)}, f32[64,128]{1,0:T(8,128)S(1)}, u32[]{:S(2)}, u32[]{:S(2)}) collective-permute-start(f32[64,128]{1,0:T(8,128)S(1)} %add.146), channel_id=1, source_target_pairs={{0,8},{1,9},{2,10},{3,11},{4,12},{5,13},{6,14},{7,15},{8,0},{9,1},... | collective-permute-start | bytes 98312 | tf_op jit(solution)/shard_map/ppermute | solution.py:78
  133.4 0.8 fusion.36
  134.2 0.8 fusion.7
  135.0 0.7 bitcast_bitcast_fusion
  135.8 11.7 %all-to-all-start.2 = ((f32[8,64,128]{2,1,0:T(8,128)}), f32[8,64,128]{2,1,0:T(8,128)S(1)}, u32[]{:S(2)}, u32[]{:S(2)}) async-start(f32[8,64,128]{2,1,0:T(8,128)} %bitcast_bitcast_fusion), calls=%async_computation.2 | async-start | bytes 524288 | tf_op jit(solution)/shard_map/all_to_all | solution.py:35
  147.6 6.9 %all-to-all-done.2 = f32[8,64,128]{2,1,0:T(8,128)S(1)} async-done(((f32[8,64,128]{2,1,0:T(8,128)}), f32[8,64,128]{2,1,0:T(8,128)S(1)}, u32[]{:S(2)}, u32[]{:S(2)}) %all-to-all-start.2) | async-done | bytes 262176 | tf_op jit(solution)/shard_map/all_to_all | solution.py:35
  154.9 0.8 broadcast_in_dim.45
  155.6 3.5 %all-to-all-start.3 = ((f32[8,96,128]{2,1,0:T(8,128)}), f32[8,96,128]{2,1,0:T(8,128)S(1)}, u32[]{:S(2)}, u32[]{:S(2)}) async-start(f32[8,96,128]{2,1,0:T(8,128)} %broadcast_in_dim.45), calls=%async_computation.3 | async-start | bytes 786432 | tf_op jit(solution)/shard_map/all_to_all | solution.py:35
  159.1 0.4 fusion.86
  159.5 7.1 %all-to-all-done.3 = f32[8,96,128]{2,1,0:T(8,128)S(1)} async-done(((f32[8,96,128]{2,1,0:T(8,128)}), f32[8,96,128]{2,1,0:T(8,128)S(1)}, u32[]{:S(2)}, u32[]{:S(2)}) %all-to-all-start.3) | async-done | bytes 393248 | tf_op jit(solution)/shard_map/all_to_all | solution.py:35
  167.2 0.4 fusion.6
  167.6 0.4 fusion.101
  168.1 2.0 %collective-permute-start.18 = (f32[32,128]{1,0:T(8,128)S(1)}, f32[32,128]{1,0:T(8,128)S(1)}, u32[]{:S(2)}, u32[]{:S(2)}) collective-permute-start(f32[32,128]{1,0:T(8,128)S(1)} %pad_maximum_fusion.6), channel_id=1, source_target_pairs={{0,8},{1,9},{2,10},{3,11},{4,12},{5,13},{6,14},{7,15},{8,0},{9,1},... | collective-permute-start | bytes 49160 | tf_op jit(solution)/shard_map/ppermute | solution.py:78
  170.1 0.8 collective-permute-done.18
  171.0 15.6 %all_to_all.26 = f32[16,32,128]{2,1,0:T(8,128)S(1)} all-to-all(f32[16,32,128]{2,1,0:T(8,128)S(1)} %broadcast_in_dim.46), channel_id=1, replica_groups={{0,16,32,48,64,80,96,112,128,144,160,176,192,208,224,240},{1,17,33,49,6..., dimensions={0} | all-to-all | bytes 524288 | tf_op jit(solution)/shard_map/all_to_all | solution.py:35
  186.7 1.1 fusion.48
  (93 shorter events, 3.3 us)
Async XLA Ops:
  0.6 30.7 %collective-permute-start = (f32[64,1024]{1,0:T(8,128)}, f32[64,1024]{1,0:T(8,128)S(1)}, u32[]{:S(2)}, u32[]{:S(2)}) collective-permute-start(f32[64,1024]{1,0:T(8,128)} %param.5), channel_id=1, source_target_pairs={{0,0},{1,241},{2,226},{3,211},{4,196},{5,181},{6,166},{7,151},{8,8... | collective-permute-start | bytes 786440 | tf_op jit(solution)/shard_map/ppermute | solution.py:78
  3.0 21.8 %copy-start.7 = (f32[1024,2048]{1,0:T(8,128)S(1)}, f32[1024,2048]{1,0:T(8,128)}, u32[]{:S(2)}) copy-start(f32[1024,2048]{1,0:T(8,128)} %param.6) | copy-start | bytes 25165828
  6.8 23.7 %collective-permute-start.2 = (f32[64,1024]{1,0:T(8,128)S(1)}, f32[64,1024]{1,0:T(8,128)S(1)}, u32[]{:S(2)}, u32[]{:S(2)}) collective-permute-start(f32[64,1024]{1,0:T(8,128)S(1)} %fusion.2), channel_id=1, source_target_pairs={{0,8},{1,9},{2,10},{3,11},{4,12},{5,13},{6,14},{7,15},{8,16},{9,17... | collective-permute-start | bytes 786440 | tf_op jit(solution)/shard_map/ppermute | solution.py:78
  28.1 2.0 %copy-start.8 = (f32[64,1024]{1,0:T(8,128)S(1)}, f32[64,1024]{1,0:T(8,128)}, u32[]{:S(2)}) copy-start(f32[64,1024]{1,0:T(8,128)} %param.5) | copy-start | bytes 786436
  28.1 2.0 %copy-start.10 = (f32[1024]{0:T(1024)S(1)}, f32[1024]{0:T(1024)}, u32[]{:S(2)}) copy-start(f32[1024]{0:T(1024)} %param.8) | copy-start | bytes 12292
  30.6 17.5 %collective-permute-start.3 = (f32[64,1024]{1,0:T(8,128)S(1)}, f32[64,1024]{1,0:T(8,128)S(1)}, u32[]{:S(2)}, u32[]{:S(2)}) collective-permute-start(f32[64,1024]{1,0:T(8,128)S(1)} %add.125), channel_id=1, source_target_pairs={{0,0},{241,1},{226,2},{211,3},{196,4},{181,5},{166,6},{151,7},{8,8... | collective-permute-start | bytes 786440 | tf_op jit(solution)/shard_map/ppermute | solution.py:78
  31.7 6.9 %copy-start.3 = (bf16[1024,1024]{1,0:T(8,128)(2,1)S(1)}, bf16[1024,1024]{1,0:T(8,128)(2,1)}, u32[]{:S(2)}) copy-start(bf16[1024,1024]{1,0:T(8,128)(2,1)} %get-tuple-element.10) | copy-start | bytes 6291460
  31.8 4.1 %collective-permute-start.4 = (f32[32,128]{1,0:T(8,128)S(1)}, f32[32,128]{1,0:T(8,128)S(1)}, u32[]{:S(2)}, u32[]{:S(2)}) collective-permute-start(f32[32,128]{1,0:T(8,128)S(1)} %pad_maximum_fusion.5), channel_id=1, source_target_pairs={{0,128},{1,129},{2,130},{3,131},{4,132},{5,133},{6,134},{7,135},{8... | collective-permute-start | bytes 49160 | tf_op jit(solution)/shard_map/ppermute | solution.py:78
  34.8 11.7 %copy-start = (bf16[1024,1024]{1,0:T(8,128)(2,1)S(1)}, bf16[1024,1024]{1,0:T(8,128)(2,1)}, u32[]{:S(2)}) copy-start(bf16[1024,1024]{1,0:T(8,128)(2,1)} %get-tuple-element.12) | copy-start | bytes 6291460
  34.8 11.7 %collective-permute-start.1 = (f32[64,1024]{1,0:T(8,128)S(1)}, f32[64,1024]{1,0:T(8,128)S(1)}, u32[]{:S(2)}, u32[]{:S(2)}) collective-permute-start(f32[64,1024]{1,0:T(8,128)S(1)} %collective-permute-done), channel_id=1, source_target_pairs={{8,0},{9,1},{10,2},{11,3},{12,4},{13,5},{14,6},{15,7},{16,8},{17,9... | collective-permute-start | bytes 786440 | tf_op jit(solution)/shard_map/ppermute | solution.py:78
  36.0 6.5 %collective-permute-start.5 = (f32[32,128]{1,0:T(8,128)S(1)}, f32[32,128]{1,0:T(8,128)S(1)}, u32[]{:S(2)}, u32[]{:S(2)}) collective-permute-start(f32[32,128]{1,0:T(8,128)S(1)} %fusion.138), channel_id=1, source_target_pairs={{0,64},{1,65},{2,66},{3,67},{4,68},{5,69},{6,70},{7,71},{8,72},{9,... | collective-permute-start | bytes 49160 | tf_op jit(solution)/shard_map/ppermute | solution.py:78
  42.6 18.9 %collective-permute-start.6 = (f32[32,128]{1,0:T(8,128)S(1)}, f32[32,128]{1,0:T(8,128)S(1)}, u32[]{:S(2)}, u32[]{:S(2)}) collective-permute-start(f32[32,128]{1,0:T(8,128)S(1)} %add.131), channel_id=1, source_target_pairs={{0,32},{1,33},{2,34},{3,35},{4,36},{5,37},{6,38},{7,39},{8,40},{9,... | collective-permute-start | bytes 49160 | tf_op jit(solution)/shard_map/ppermute | solution.py:78
  47.4 22.7 %copy-start.11 = (f32[1024]{0:T(1024)S(1)}, f32[1024]{0:T(1024)}, u32[]{:S(2)}) copy-start(f32[1024]{0:T(1024)} %param.9) | copy-start | bytes 12292
  48.9 22.1 %all-to-all-start = ((f32[8,64,128]{2,1,0:T(8,128)}), f32[8,64,128]{2,1,0:T(8,128)S(1)}, u32[]{:S(2)}, u32[]{:S(2)}) async-start(f32[8,64,128]{2,1,0:T(8,128)} %bitcast_bitcast_fusion.1), calls=%async_computation | async-start | bytes 524288 | tf_op jit(solution)/shard_map/all_to_all | solution.py:35
  61.5 2.7 %collective-permute-start.7 = (f32[32,128]{1,0:T(8,128)S(1)}, f32[32,128]{1,0:T(8,128)S(1)}, u32[]{:S(2)}, u32[]{:S(2)}) collective-permute-start(f32[32,128]{1,0:T(8,128)S(1)} %add.132), channel_id=1, source_target_pairs={{0,16},{1,17},{2,18},{3,19},{4,20},{5,21},{6,22},{7,23},{8,24},{9,... | collective-permute-start | bytes 49160 | tf_op jit(solution)/shard_map/ppermute | solution.py:78
  64.2 6.8 %collective-permute-start.8 = (f32[32,128]{1,0:T(8,128)S(1)}, f32[32,128]{1,0:T(8,128)S(1)}, u32[]{:S(2)}, u32[]{:S(2)}) collective-permute-start(f32[32,128]{1,0:T(8,128)S(1)} %add.133), channel_id=1, source_target_pairs={{0,8},{1,9},{2,10},{3,11},{4,12},{5,13},{6,14},{7,15},{8,0},{9,1},... | collective-permute-start | bytes 49160 | tf_op jit(solution)/shard_map/ppermute | solution.py:78
  71.0 14.9 %copy-start.6 = (bf16[1024,1024]{1,0:T(8,128)(2,1)S(1)}, bf16[1024,1024]{1,0:T(8,128)(2,1)}, u32[]{:S(2)}) copy-start(bf16[1024,1024]{1,0:T(8,128)(2,1)} %get-tuple-element.9) | copy-start | bytes 6291460
  84.3 2.0 %copy-start.1 = (bf16[1024,1024]{1,0:T(8,128)(2,1)S(1)}, bf16[1024,1024]{1,0:T(8,128)(2,1)}, u32[]{:S(2)}) copy-start(bf16[1024,1024]{1,0:T(8,128)(2,1)} %get-tuple-element.12) | copy-start | bytes 6291460
  85.2 20.9 %collective-permute-start.9 = (f32[64,1024]{1,0:T(8,128)S(1)}, f32[64,1024]{1,0:T(8,128)S(1)}, u32[]{:S(2)}, u32[]{:S(2)}) collective-permute-start(f32[64,1024]{1,0:T(8,128)S(1)} %get-tuple-element.48), channel_id=1, source_target_pairs={{0,0},{1,241},{2,226},{3,211},{4,196},{5,181},{6,166},{7,151},{8,8... | collective-permute-start | bytes 786440 | tf_op jit(solution)/shard_map/ppermute | solution.py:78
  86.3 1.6 copy-start.4
  88.9 17.1 %collective-permute-start.10 = (f32[64,1024]{1,0:T(8,128)S(1)}, f32[64,1024]{1,0:T(8,128)S(1)}, u32[]{:S(2)}, u32[]{:S(2)}) collective-permute-start(f32[64,1024]{1,0:T(8,128)S(1)} %fusion.9), channel_id=1, source_target_pairs={{0,8},{1,9},{2,10},{3,11},{4,12},{5,13},{6,14},{7,15},{8,16},{9,17... | collective-permute-start | bytes 786440 | tf_op jit(solution)/shard_map/ppermute | solution.py:78
  106.9 4.4 %collective-permute-start.11 = (f32[64,128]{1,0:T(8,128)S(1)}, f32[64,128]{1,0:T(8,128)S(1)}, u32[]{:S(2)}, u32[]{:S(2)}) collective-permute-start(f32[64,128]{1,0:T(8,128)S(1)} %maximum_maximum_fusion), channel_id=1, source_target_pairs={{0,128},{1,129},{2,130},{3,131},{4,132},{5,133},{6,134},{7,135},{8... | collective-permute-start | bytes 98312 | tf_op jit(solution)/shard_map/ppermute | solution.py:78
  110.0 17.2 %copy-start.5 = (bf16[1024,1024]{1,0:T(8,128)(2,1)S(1)}, bf16[1024,1024]{1,0:T(8,128)(2,1)}, u32[]{:S(2)}) copy-start(bf16[1024,1024]{1,0:T(8,128)(2,1)} %get-tuple-element.10) | copy-start | bytes 6291460
  110.0 25.0 %collective-permute-start.17 = (f32[64,1024]{1,0:T(8,128)S(1)}, f32[64,1024]{1,0:T(8,128)S(1)}, u32[]{:S(2)}, u32[]{:S(2)}) collective-permute-start(f32[64,1024]{1,0:T(8,128)S(1)} %add.140), channel_id=1, source_target_pairs={{0,0},{241,1},{226,2},{211,3},{196,4},{181,5},{166,6},{151,7},{8,8... | collective-permute-start | bytes 786440 | tf_op jit(solution)/shard_map/ppermute | solution.py:78
  111.4 7.0 %collective-permute-start.12 = (f32[64,128]{1,0:T(8,128)S(1)}, f32[64,128]{1,0:T(8,128)S(1)}, u32[]{:S(2)}, u32[]{:S(2)}) collective-permute-start(f32[64,128]{1,0:T(8,128)S(1)} %fusion.137), channel_id=1, source_target_pairs={{0,64},{1,65},{2,66},{3,67},{4,68},{5,69},{6,70},{7,71},{8,72},{9,... | collective-permute-start | bytes 98312 | tf_op jit(solution)/shard_map/ppermute | solution.py:78
  118.4 8.7 %collective-permute-start.13 = (f32[64,128]{1,0:T(8,128)S(1)}, f32[64,128]{1,0:T(8,128)S(1)}, u32[]{:S(2)}, u32[]{:S(2)}) collective-permute-start(f32[64,128]{1,0:T(8,128)S(1)} %add.144), channel_id=1, source_target_pairs={{0,32},{1,33},{2,34},{3,35},{4,36},{5,37},{6,38},{7,39},{8,40},{9,... | collective-permute-start | bytes 98312 | tf_op jit(solution)/shard_map/ppermute | solution.py:78
  120.8 12.6 %copy-start.2 = (bf16[1024,1024]{1,0:T(8,128)(2,1)S(1)}, bf16[1024,1024]{1,0:T(8,128)(2,1)}, u32[]{:S(2)}) copy-start(bf16[1024,1024]{1,0:T(8,128)(2,1)} %get-tuple-element.12) | copy-start | bytes 6291460
  120.8 12.5 %collective-permute-start.16 = (f32[64,1024]{1,0:T(8,128)S(1)}, f32[64,1024]{1,0:T(8,128)S(1)}, u32[]{:S(2)}, u32[]{:S(2)}) collective-permute-start(f32[64,1024]{1,0:T(8,128)S(1)} %collective-permute-done.9), channel_id=1, source_target_pairs={{8,0},{9,1},{10,2},{11,3},{12,4},{13,5},{14,6},{15,7},{16,8},{17,9... | collective-permute-start | bytes 786440 | tf_op jit(solution)/shard_map/ppermute | solution.py:78
  127.0 3.1 %collective-permute-start.14 = (f32[64,128]{1,0:T(8,128)S(1)}, f32[64,128]{1,0:T(8,128)S(1)}, u32[]{:S(2)}, u32[]{:S(2)}) collective-permute-start(f32[64,128]{1,0:T(8,128)S(1)} %add.145), channel_id=1, source_target_pairs={{0,16},{1,17},{2,18},{3,19},{4,20},{5,21},{6,22},{7,23},{8,24},{9,... | collective-permute-start | bytes 98312 | tf_op jit(solution)/shard_map/ppermute | solution.py:78
  130.1 17.4 %collective-permute-start.15 = (f32[64,128]{1,0:T(8,128)S(1)}, f32[64,128]{1,0:T(8,128)S(1)}, u32[]{:S(2)}, u32[]{:S(2)}) collective-permute-start(f32[64,128]{1,0:T(8,128)S(1)} %add.146), channel_id=1, source_target_pairs={{0,8},{1,9},{2,10},{3,11},{4,12},{5,13},{6,14},{7,15},{8,0},{9,1},... | collective-permute-start | bytes 98312 | tf_op jit(solution)/shard_map/ppermute | solution.py:78
  135.8 18.8 %all-to-all-start.2 = ((f32[8,64,128]{2,1,0:T(8,128)}), f32[8,64,128]{2,1,0:T(8,128)S(1)}, u32[]{:S(2)}, u32[]{:S(2)}) async-start(f32[8,64,128]{2,1,0:T(8,128)} %bitcast_bitcast_fusion), calls=%async_computation.2 | async-start | bytes 524288 | tf_op jit(solution)/shard_map/all_to_all | solution.py:35
  155.6 11.0 %all-to-all-start.3 = ((f32[8,96,128]{2,1,0:T(8,128)}), f32[8,96,128]{2,1,0:T(8,128)S(1)}, u32[]{:S(2)}, u32[]{:S(2)}) async-start(f32[8,96,128]{2,1,0:T(8,128)} %broadcast_in_dim.45), calls=%async_computation.3 | async-start | bytes 786432 | tf_op jit(solution)/shard_map/all_to_all | solution.py:35
  167.2 20.7 %copy-start.9 = (f32[64,64]{1,0:T(8,128)}, f32[64,64]{1,0:T(8,128)S(1)}, u32[]{:S(2)}) copy-start(f32[64,64]{1,0:T(8,128)S(1)} %fusion.87) | copy-start | bytes 49156
  168.1 2.9 %collective-permute-start.18 = (f32[32,128]{1,0:T(8,128)S(1)}, f32[32,128]{1,0:T(8,128)S(1)}, u32[]{:S(2)}, u32[]{:S(2)}) collective-permute-start(f32[32,128]{1,0:T(8,128)S(1)} %pad_maximum_fusion.6), channel_id=1, source_target_pairs={{0,8},{1,9},{2,10},{3,11},{4,12},{5,13},{6,14},{7,15},{8,0},{9,1},... | collective-permute-start | bytes 49160 | tf_op jit(solution)/shard_map/ppermute | solution.py:78

commit v6 on v4

--- a/solution.py
+++ b/solution.py
@@ -22,10 +22,14 @@
             bit: [(number(row, p), number(row ^ bit, p)) for row, p in every]
             for bit in (1 << n for n in range(rows.bit_length() - 1))
         }
-        turn = lambda row: row // 2 * 2 % offs
-        self.fetch = [
-            (number(row, p ^ turn(row)), number(row - per_device * p, p)) for row, p in every
-        ]
+        cycle = (2, 0, 6, 4)
+        sender = {
+            (chip, cycle[(q // 2 + chip) % 4] + q % 2): q for chip in range(rows // 2) for q in range(8)
+        }
+        self.fetch = []
+        for row, p in every:
+            far = (row + per_device * p) % rows
+            self.fetch.append((number(far, sender[far // 2, p]), number(row, p)))
         self.back = [(b, a) for a, b in self.fetch]
         self.up = [(number(row, p), number(row + 1, p)) for row, p in every]
         self.down = [(b, a) for a, b in self.up]

time: 189 us -> 186 us (0.984)
  waiting for transfers between devices: 38.2 us -> 31.4 us
  starting transfers between devices: 83.5 us -> 89.1 us
    ppermute x19, waiting for transfers between devices: 24.1 us -> 17.3 us  [permuted(): return lax.ppermute(array, AXES, pairs)]
    ppermute x19, starting transfers between devices: 55.9 us -> 60.7 us  [permuted(): return lax.ppermute(array, AXES, pairs)]
  transfers between devices with their start and end apart: 22 -> 22, of which waited for: 11 -> 10; matrix products, arithmetic and copies ran while one was open for 16% -> 17% of each run, Pallas kernels for 0% -> 0%
where the time goes in v6:
time: 186 us; the launch traced here: 185 us
  starting transfers between devices  89.1 us (48%)
  waiting for transfers between devices  31.4 us (17%)
  blocking collectives  26.1 us (14%)
  matrix products  24.3 us (13%)
  other arithmetic  9.03 us (5%)
  local copies, waits for them, and re-layouts  4.16 us (2%)
    ppermute x19, starting transfers between devices, permuted(): return lax.ppermute(array, AXES, pairs)  60.7 us
    all_to_all x3, starting transfers between devices, exchange(): lax.all_to_all(array, AXES, 0, 0, axis_index_groups=groups, tiled=True)  28.4 us
    all_to_all x2, blocking collectives, exchange(): lax.all_to_all(array, AXES, 0, 0, axis_index_groups=groups, tiled=True)  26.1 us
    ppermute x19, waiting for transfers between devices, permuted(): return lax.ppermute(array, AXES, pairs)  17.3 us
    all_to_all x3, waiting for transfers between devices, exchange(): lax.all_to_all(array, AXES, 0, 0, axis_index_groups=groups, tiled=True)  14.1 us
    dot_general x12, matrix products, block_product(): lax.dot_general(left, right, (dims, ((), ())), preferred_element_type=jnp...  11.6 us
    dot_general x2, matrix products, back_first(): jnp.dot(vecs * masks[s], block_of(tiles, s), precision=lax.Precision.HIGH...  7.51 us
    convert_element_type x6, other arithmetic, halves(): return (high.astype(jnp.bfloat16), (array - high).astype(jnp.bfloat16))  4.85 us
  transfers between devices with their start and end apart: 22, of which 10 were waited for; matrix products, arithmetic and copies ran while one was open for 17% of the time, Pallas kernels for 0%

profile of v6, /device:TPU:1, one launch (start us, length us, event | category | flops | bytes accessed | tf_op | source)
XLA Modules:
  0.0 185.4 jit_solution(6418933606050406159)
XLA Ops:
  0.6 12.2 %collective-permute-start = (f32[64,1024]{1,0:T(8,128)}, f32[64,1024]{1,0:T(8,128)S(1)}, u32[]{:S(2)}, u32[]{:S(2)}) collective-permute-start(f32[64,1024]{1,0:T(8,128)} %param.5), channel_id=1, source_target_pairs={{2,0},{17,1},{36,2},{51,3},{70,4},{85,5},{96,6},{119,7},{10,8},{25... | collective-permute-start | bytes 786440 | tf_op jit(solution)/shard_map/ppermute | solution.py:82
  12.9 0.7 compare_convert_fusion
  13.6 3.8 %fusion.2 = f32[64,1024]{1,0:T(8,128)S(1)} fusion(f32[1024,2048]{1,0:T(8,128)} %param.6, f32[64,1024]{1,0:T(8,128)} %param.5, f32[1024]{0:T(1024)S(1)} %bitcast.108), kind=kOutput, calls=%fused_computation.6 | convolution fusion | flops 402718720 | bytes 4722688 | tf_op jit(solution)/shard_map/dot_general | solution.py:139
  17.5 1.3 fusion.97
  18.9 3.7 %fusion.4 = f32[64,1024]{1,0:T(8,128)S(1)} fusion(f32[1024,2048]{1,0:T(8,128)} %param.6, f32[64,1024]{1,0:T(8,128)} %param.5, f32[1024]{0:T(1024)S(1)} %bitcast.107), kind=kOutput, calls=%fused_computation.10 | convolution fusion | flops 402718720 | bytes 4722688 | tf_op jit(solution)/shard_map/dot_general | solution.py:139
  22.5 0.7 iota_compare_fusion.3
  23.2 2.7 %fusion = (bf16[1024,1024]{1,0:T(8,128)(2,1)}, bf16[1024,1024]{1,0:T(8,128)(2,1)}) fusion(f32[1024,2048]{1,0:T(8,128)S(1)} %copy-done.7, pred[1024]{0:T(1024)(128)(4,1)S(1)} %iota_compare_fusion.3), kind=kLoop, calls=%fused_computation.4 | loop fusion | flops 5242880 | bytes 8389632 | tf_op jit(solution)/shard_map/convert_element_type | solution.py:98
  25.9 0.6 iota_compare_fusion.2
  26.6 2.0 %fusion.1 = (bf16[1024,1024]{1,0:T(8,128)(2,1)S(1)}, bf16[1024,1024]{1,0:T(8,128)(2,1)}) fusion(f32[1024,2048]{1,0:T(8,128)S(1)} %copy-done.7, pred[1024]{0:T(1024)(128)(4,1)S(1)} %iota_compare_fusion.2), kind=kLoop, calls=%fused_computation.5 | loop fusion | flops 5242880 | bytes 8389632 | tf_op jit(solution)/shard_map/convert_element_type | solution.py:98
  28.6 0.4 fusion.16
  29.0 3.4 %collective-permute-start.3 = (f32[64,1024]{1,0:T(8,128)S(1)}, f32[64,1024]{1,0:T(8,128)S(1)}, u32[]{:S(2)}, u32[]{:S(2)}) collective-permute-start(f32[64,1024]{1,0:T(8,128)S(1)} %add.125), channel_id=1, source_target_pairs={{0,2},{1,17},{2,36},{3,51},{4,70},{5,85},{6,96},{7,119},{8,10},{9,... | collective-permute-start | bytes 786440 | tf_op jit(solution)/shard_map/ppermute | solution.py:82
  32.4 0.4 fusion.98
  33.0 0.2 collective-permute-start.4
  33.3 2.6 %fusion.24 = f32[128,1024]{1,0:T(8,128)S(1)} fusion(bf16[1024,1024]{1,0:T(8,128)(2,1)} %get-tuple-element.9, bf16[64,1024]{1,0:T(8,128)(2,1)S(1)} %get-tuple-element.26, bf16[64,1024]{1,0:T(8,128)(2,1)S(1)} %get-tuple-element.27), kind=kOutput, calls=%fused_computation.54 | convolution fusion | flops 268959744 | bytes 2883584 | tf_op jit(solution)/shard_map/dot_general | solution.py:104
  36.0 1.5 collective-permute-done.4
  37.6 4.1 %collective-permute-start.5 = (f32[32,128]{1,0:T(8,128)S(1)}, f32[32,128]{1,0:T(8,128)S(1)}, u32[]{:S(2)}, u32[]{:S(2)}) collective-permute-start(f32[32,128]{1,0:T(8,128)S(1)} %fusion.137), channel_id=1, source_target_pairs={{0,64},{1,65},{2,66},{3,67},{4,68},{5,69},{6,70},{7,71},{8,72},{9,... | collective-permute-start | bytes 49160 | tf_op jit(solution)/shard_map/ppermute | solution.py:82
  41.7 0.8 fusion.15
  42.5 1.9 %collective-permute-done.5 = f32[32,128]{1,0:T(8,128)S(1)} collective-permute-done((f32[32,128]{1,0:T(8,128)S(1)}, f32[32,128]{1,0:T(8,128)S(1)}, u32[]{:S(2)}, u32[]{:S(2)}) %collective-permute-start.5) | collective-permute-done | bytes 16416 | tf_op jit(solution)/shard_map/ppermute | solution.py:82
  44.4 3.5 %collective-permute-start.6 = (f32[32,128]{1,0:T(8,128)S(1)}, f32[32,128]{1,0:T(8,128)S(1)}, u32[]{:S(2)}, u32[]{:S(2)}) collective-permute-start(f32[32,128]{1,0:T(8,128)S(1)} %add.131), channel_id=1, source_target_pairs={{0,32},{1,33},{2,34},{3,35},{4,36},{5,37},{6,38},{7,39},{8,40},{9,... | collective-permute-start | bytes 49160 | tf_op jit(solution)/shard_map/ppermute | solution.py:82
  48.0 0.8 fusion.28
  48.8 0.8 fusion.13
  49.6 0.8 bitcast_bitcast_fusion.1
  50.3 11.4 %all-to-all-start = ((f32[8,64,128]{2,1,0:T(8,128)}), f32[8,64,128]{2,1,0:T(8,128)S(1)}, u32[]{:S(2)}, u32[]{:S(2)}) async-start(f32[8,64,128]{2,1,0:T(8,128)} %bitcast_bitcast_fusion.1), calls=%async_computation | async-start | bytes 524288 | tf_op jit(solution)/shard_map/all_to_all | solution.py:39
  61.8 0.9 collective-permute-start.7
  62.7 1.8 collective-permute-done.7
  64.5 4.7 %collective-permute-start.8 = (f32[32,128]{1,0:T(8,128)S(1)}, f32[32,128]{1,0:T(8,128)S(1)}, u32[]{:S(2)}, u32[]{:S(2)}) collective-permute-start(f32[32,128]{1,0:T(8,128)S(1)} %add.133), channel_id=1, source_target_pairs={{0,8},{1,9},{2,10},{3,11},{4,12},{5,13},{6,14},{7,15},{8,0},{9,1},... | collective-permute-start | bytes 49160 | tf_op jit(solution)/shard_map/ppermute | solution.py:82
  69.2 0.8 collective-permute-done.8
  70.2 13.2 %all_to_all.25 = f32[8,96,128]{2,1,0:T(8,128)S(1)} all-to-all(f32[8,96,128]{2,1,0:T(8,128)S(1)} %broadcast_in_dim.44), channel_id=1, replica_groups={{0,1,2,3,4,5,6,7},{8,9,10,11,12,13,14,15},{16,17,18,19,20,21,22,23},{24..., dimensions={0} | all-to-all | bytes 786432 | tf_op jit(solution)/shard_map/all_to_all | solution.py:39
  83.5 0.5 fusion.21
  83.9 0.4 fusion.100
  84.3 4.1 %collective-permute-start.9 = (f32[64,1024]{1,0:T(8,128)S(1)}, f32[64,1024]{1,0:T(8,128)S(1)}, u32[]{:S(2)}, u32[]{:S(2)}) collective-permute-start(f32[64,1024]{1,0:T(8,128)S(1)} %get-tuple-element.48), channel_id=1, source_target_pairs={{2,0},{17,1},{36,2},{51,3},{70,4},{85,5},{96,6},{119,7},{10,8},{25... | collective-permute-start | bytes 786440 | tf_op jit(solution)/shard_map/ppermute | solution.py:82
  88.4 0.4 fusion.43
  88.8 0.4 fusion.42
  89.3 1.1 copy-done.4
  90.4 0.5 fusion.10
  90.9 0.5 fusion.9
  91.6 0.4 convolution_multiply_fusion.2
  92.0 2.9 %collective-permute-done.10 = f32[64,1024]{1,0:T(8,128)S(1)} collective-permute-done((f32[64,1024]{1,0:T(8,128)S(1)}, f32[64,1024]{1,0:T(8,128)S(1)}, u32[]{:S(2)}, u32[]{:S(2)}) %collective-permute-start.10) | collective-permute-done | bytes 262176 | tf_op jit(solution)/shard_map/ppermute | solution.py:82
  95.0 0.4 fusion.99
  95.8 2.5 %collective-permute-start.11 = (f32[64,128]{1,0:T(8,128)S(1)}, f32[64,128]{1,0:T(8,128)S(1)}, u32[]{:S(2)}, u32[]{:S(2)}) collective-permute-start(f32[64,128]{1,0:T(8,128)S(1)} %maximum_maximum_fusion), channel_id=1, source_target_pairs={{0,128},{1,129},{2,130},{3,131},{4,132},{5,133},{6,134},{7,135},{8... | collective-permute-start | bytes 98312 | tf_op jit(solution)/shard_map/ppermute | solution.py:82
  98.3 8.8 %collective-permute-start.17 = (f32[64,1024]{1,0:T(8,128)S(1)}, f32[64,1024]{1,0:T(8,128)S(1)}, u32[]{:S(2)}, u32[]{:S(2)}) collective-permute-start(f32[64,1024]{1,0:T(8,128)S(1)} %add.140), channel_id=1, source_target_pairs={{0,2},{1,17},{2,36},{3,51},{4,70},{5,85},{6,96},{7,119},{8,10},{9,... | collective-permute-start | bytes 786440 | tf_op jit(solution)/shard_map/ppermute | solution.py:82
  107.2 6.6 %collective-permute-done.12 = f32[64,128]{1,0:T(8,128)S(1)} collective-permute-done((f32[64,128]{1,0:T(8,128)S(1)}, f32[64,128]{1,0:T(8,128)S(1)}, u32[]{:S(2)}, u32[]{:S(2)}) %collective-permute-start.12) | collective-permute-done | bytes 32800 | tf_op jit(solution)/shard_map/ppermute | solution.py:82
  114.0 2.4 %fusion.32 = f32[128,1024]{1,0:T(8,128)S(1)} fusion(bf16[1024,1024]{1,0:T(8,128)(2,1)} %get-tuple-element.9, bf16[64,1024]{1,0:T(8,128)(2,1)S(1)} %get-tuple-element.20, bf16[64,1024]{1,0:T(8,128)(2,1)S(1)} %get-tuple-element.21), kind=kOutput, calls=%fused_computation.63 | convolution fusion | flops 268959744 | bytes 2883584 | tf_op jit(solution)/shard_map/dot_general | solution.py:104
  116.4 4.2 %collective-permute-start.16 = (f32[64,1024]{1,0:T(8,128)S(1)}, f32[64,1024]{1,0:T(8,128)S(1)}, u32[]{:S(2)}, u32[]{:S(2)}) collective-permute-start(f32[64,1024]{1,0:T(8,128)S(1)} %collective-permute-done.9), channel_id=1, source_target_pairs={{8,0},{9,1},{10,2},{11,3},{12,4},{13,5},{14,6},{15,7},{16,8},{17,9... | collective-permute-start | bytes 786440 | tf_op jit(solution)/shard_map/ppermute | solution.py:82
  120.6 4.4 %collective-permute-start.14 = (f32[64,128]{1,0:T(8,128)S(1)}, f32[64,128]{1,0:T(8,128)S(1)}, u32[]{:S(2)}, u32[]{:S(2)}) collective-permute-start(f32[64,128]{1,0:T(8,128)S(1)} %add.145), channel_id=1, source_target_pairs={{0,16},{1,17},{2,18},{3,19},{4,20},{5,21},{6,22},{7,23},{8,24},{9,... | collective-permute-start | bytes 98312 | tf_op jit(solution)/shard_map/ppermute | solution.py:82
  125.0 0.8 fusion.8
  125.8 0.8 collective-permute-done.14
  126.6 3.6 %collective-permute-start.15 = (f32[64,128]{1,0:T(8,128)S(1)}, f32[64,128]{1,0:T(8,128)S(1)}, u32[]{:S(2)}, u32[]{:S(2)}) collective-permute-start(f32[64,128]{1,0:T(8,128)S(1)} %add.146), channel_id=1, source_target_pairs={{0,8},{1,9},{2,10},{3,11},{4,12},{5,13},{6,14},{7,15},{8,0},{9,1},... | collective-permute-start | bytes 98312 | tf_op jit(solution)/shard_map/ppermute | solution.py:82
  130.2 0.8 fusion.36
  131.1 0.8 fusion.7
  131.9 0.7 bitcast_bitcast_fusion
  132.6 13.6 %all-to-all-start.2 = ((f32[8,64,128]{2,1,0:T(8,128)}), f32[8,64,128]{2,1,0:T(8,128)S(1)}, u32[]{:S(2)}, u32[]{:S(2)}) async-start(f32[8,64,128]{2,1,0:T(8,128)} %bitcast_bitcast_fusion), calls=%async_computation.2 | async-start | bytes 524288 | tf_op jit(solution)/shard_map/all_to_all | solution.py:39
  146.3 6.9 %all-to-all-done.2 = f32[8,64,128]{2,1,0:T(8,128)S(1)} async-done(((f32[8,64,128]{2,1,0:T(8,128)}), f32[8,64,128]{2,1,0:T(8,128)S(1)}, u32[]{:S(2)}, u32[]{:S(2)}) %all-to-all-start.2) | async-done | bytes 262176 | tf_op jit(solution)/shard_map/all_to_all | solution.py:39
  153.3 0.2 fusion.58
  153.6 0.8 broadcast_in_dim.45
  154.3 3.5 %all-to-all-start.3 = ((f32[8,96,128]{2,1,0:T(8,128)}), f32[8,96,128]{2,1,0:T(8,128)S(1)}, u32[]{:S(2)}, u32[]{:S(2)}) async-start(f32[8,96,128]{2,1,0:T(8,128)} %broadcast_in_dim.45), calls=%async_computation.3 | async-start | bytes 786432 | tf_op jit(solution)/shard_map/all_to_all | solution.py:39
  157.8 0.4 fusion.86
  158.2 7.1 %all-to-all-done.3 = f32[8,96,128]{2,1,0:T(8,128)S(1)} async-done(((f32[8,96,128]{2,1,0:T(8,128)}), f32[8,96,128]{2,1,0:T(8,128)S(1)}, u32[]{:S(2)}, u32[]{:S(2)}) %all-to-all-start.3) | async-done | bytes 393248 | tf_op jit(solution)/shard_map/all_to_all | solution.py:39
  165.9 0.4 fusion.6
  166.3 0.4 fusion.101
  166.8 12.9 %all_to_all.26 = f32[16,32,128]{2,1,0:T(8,128)S(1)} all-to-all(f32[16,32,128]{2,1,0:T(8,128)S(1)} %broadcast_in_dim.46), channel_id=1, replica_groups={{0,16,32,48,64,80,96,112,128,144,160,176,192,208,224,240},{1,17,33,49,6..., dimensions={0} | all-to-all | bytes 524288 | tf_op jit(solution)/shard_map/all_to_all | solution.py:39
  179.7 3.6 %collective-permute-start.18 = (f32[32,128]{1,0:T(8,128)S(1)}, f32[32,128]{1,0:T(8,128)S(1)}, u32[]{:S(2)}, u32[]{:S(2)}) collective-permute-start(f32[32,128]{1,0:T(8,128)S(1)} %reduce_sum.49), channel_id=1, source_target_pairs={{0,8},{1,9},{2,10},{3,11},{4,12},{5,13},{6,14},{7,15},{8,0},{9,1},... | collective-permute-start | bytes 49160 | tf_op jit(solution)/shard_map/ppermute | solution.py:82
  183.4 0.8 collective-permute-done.18
  184.3 1.1 fusion.48
  (93 shorter events, 2.7 us)
Async XLA Ops:
  0.6 31.8 %collective-permute-start = (f32[64,1024]{1,0:T(8,128)}, f32[64,1024]{1,0:T(8,128)S(1)}, u32[]{:S(2)}, u32[]{:S(2)}) collective-permute-start(f32[64,1024]{1,0:T(8,128)} %param.5), channel_id=1, source_target_pairs={{2,0},{17,1},{36,2},{51,3},{70,4},{85,5},{96,6},{119,7},{10,8},{25... | collective-permute-start | bytes 786440 | tf_op jit(solution)/shard_map/ppermute | solution.py:82
  13.6 9.6 %copy-start.7 = (f32[1024,2048]{1,0:T(8,128)S(1)}, f32[1024,2048]{1,0:T(8,128)}, u32[]{:S(2)}) copy-start(f32[1024,2048]{1,0:T(8,128)} %param.6) | copy-start | bytes 25165828
  17.4 11.5 %collective-permute-start.2 = (f32[64,1024]{1,0:T(8,128)S(1)}, f32[64,1024]{1,0:T(8,128)S(1)}, u32[]{:S(2)}, u32[]{:S(2)}) collective-permute-start(f32[64,1024]{1,0:T(8,128)S(1)} %fusion.2), channel_id=1, source_target_pairs={{0,8},{1,9},{2,10},{3,11},{4,12},{5,13},{6,14},{7,15},{8,16},{9,17... | collective-permute-start | bytes 786440 | tf_op jit(solution)/shard_map/ppermute | solution.py:82
  26.6 2.0 %copy-start.8 = (f32[64,1024]{1,0:T(8,128)S(1)}, f32[64,1024]{1,0:T(8,128)}, u32[]{:S(2)}) copy-start(f32[64,1024]{1,0:T(8,128)} %param.5) | copy-start | bytes 786436
  26.6 2.0 %copy-start.10 = (f32[1024]{0:T(1024)S(1)}, f32[1024]{0:T(1024)}, u32[]{:S(2)}) copy-start(f32[1024]{0:T(1024)} %param.8) | copy-start | bytes 12292
  29.0 20.5 %collective-permute-start.3 = (f32[64,1024]{1,0:T(8,128)S(1)}, f32[64,1024]{1,0:T(8,128)S(1)}, u32[]{:S(2)}, u32[]{:S(2)}) collective-permute-start(f32[64,1024]{1,0:T(8,128)S(1)} %add.125), channel_id=1, source_target_pairs={{0,2},{1,17},{2,36},{3,51},{4,70},{5,85},{6,96},{7,119},{8,10},{9,... | collective-permute-start | bytes 786440 | tf_op jit(solution)/shard_map/ppermute | solution.py:82
  32.9 8.8 %copy-start.3 = (bf16[1024,1024]{1,0:T(8,128)(2,1)S(1)}, bf16[1024,1024]{1,0:T(8,128)(2,1)}, u32[]{:S(2)}) copy-start(bf16[1024,1024]{1,0:T(8,128)(2,1)} %get-tuple-element.10) | copy-start | bytes 6291460
  33.0 4.5 %collective-permute-start.4 = (f32[32,128]{1,0:T(8,128)S(1)}, f32[32,128]{1,0:T(8,128)S(1)}, u32[]{:S(2)}, u32[]{:S(2)}) collective-permute-start(f32[32,128]{1,0:T(8,128)S(1)} %pad_maximum_fusion.5), channel_id=1, source_target_pairs={{0,128},{1,129},{2,130},{3,131},{4,132},{5,133},{6,134},{7,135},{8... | collective-permute-start | bytes 49160 | tf_op jit(solution)/shard_map/ppermute | solution.py:82
  35.9 12.1 %copy-start = (bf16[1024,1024]{1,0:T(8,128)(2,1)S(1)}, bf16[1024,1024]{1,0:T(8,128)(2,1)}, u32[]{:S(2)}) copy-start(bf16[1024,1024]{1,0:T(8,128)(2,1)} %get-tuple-element.12) | copy-start | bytes 6291460
  35.9 12.0 %collective-permute-start.1 = (f32[64,1024]{1,0:T(8,128)S(1)}, f32[64,1024]{1,0:T(8,128)S(1)}, u32[]{:S(2)}, u32[]{:S(2)}) collective-permute-start(f32[64,1024]{1,0:T(8,128)S(1)} %collective-permute-done), channel_id=1, source_target_pairs={{8,0},{9,1},{10,2},{11,3},{12,4},{13,5},{14,6},{15,7},{16,8},{17,9... | collective-permute-start | bytes 786440 | tf_op jit(solution)/shard_map/ppermute | solution.py:82
  37.6 6.8 %collective-permute-start.5 = (f32[32,128]{1,0:T(8,128)S(1)}, f32[32,128]{1,0:T(8,128)S(1)}, u32[]{:S(2)}, u32[]{:S(2)}) collective-permute-start(f32[32,128]{1,0:T(8,128)S(1)} %fusion.137), channel_id=1, source_target_pairs={{0,64},{1,65},{2,66},{3,67},{4,68},{5,69},{6,70},{7,71},{8,72},{9,... | collective-permute-start | bytes 49160 | tf_op jit(solution)/shard_map/ppermute | solution.py:82
  44.4 17.4 %collective-permute-start.6 = (f32[32,128]{1,0:T(8,128)S(1)}, f32[32,128]{1,0:T(8,128)S(1)}, u32[]{:S(2)}, u32[]{:S(2)}) collective-permute-start(f32[32,128]{1,0:T(8,128)S(1)} %add.131), channel_id=1, source_target_pairs={{0,32},{1,33},{2,34},{3,35},{4,36},{5,37},{6,38},{7,39},{8,40},{9,... | collective-permute-start | bytes 49160 | tf_op jit(solution)/shard_map/ppermute | solution.py:82
  48.8 20.4 %copy-start.11 = (f32[1024]{0:T(1024)S(1)}, f32[1024]{0:T(1024)}, u32[]{:S(2)}) copy-start(f32[1024]{0:T(1024)} %param.9) | copy-start | bytes 12292
  50.3 19.7 %all-to-all-start = ((f32[8,64,128]{2,1,0:T(8,128)}), f32[8,64,128]{2,1,0:T(8,128)S(1)}, u32[]{:S(2)}, u32[]{:S(2)}) async-start(f32[8,64,128]{2,1,0:T(8,128)} %bitcast_bitcast_fusion.1), calls=%async_computation | async-start | bytes 524288 | tf_op jit(solution)/shard_map/all_to_all | solution.py:39
  61.8 2.7 %collective-permute-start.7 = (f32[32,128]{1,0:T(8,128)S(1)}, f32[32,128]{1,0:T(8,128)S(1)}, u32[]{:S(2)}, u32[]{:S(2)}) collective-permute-start(f32[32,128]{1,0:T(8,128)S(1)} %add.132), channel_id=1, source_target_pairs={{0,16},{1,17},{2,18},{3,19},{4,20},{5,21},{6,22},{7,23},{8,24},{9,... | collective-permute-start | bytes 49160 | tf_op jit(solution)/shard_map/ppermute | solution.py:82
  64.5 5.6 %collective-permute-start.8 = (f32[32,128]{1,0:T(8,128)S(1)}, f32[32,128]{1,0:T(8,128)S(1)}, u32[]{:S(2)}, u32[]{:S(2)}) collective-permute-start(f32[32,128]{1,0:T(8,128)S(1)} %add.133), channel_id=1, source_target_pairs={{0,8},{1,9},{2,10},{3,11},{4,12},{5,13},{6,14},{7,15},{8,0},{9,1},... | collective-permute-start | bytes 49160 | tf_op jit(solution)/shard_map/ppermute | solution.py:82
  70.1 18.3 %copy-start.6 = (bf16[1024,1024]{1,0:T(8,128)(2,1)S(1)}, bf16[1024,1024]{1,0:T(8,128)(2,1)}, u32[]{:S(2)}) copy-start(bf16[1024,1024]{1,0:T(8,128)(2,1)} %get-tuple-element.9) | copy-start | bytes 6291460
  83.5 5.4 %copy-start.1 = (bf16[1024,1024]{1,0:T(8,128)(2,1)S(1)}, bf16[1024,1024]{1,0:T(8,128)(2,1)}, u32[]{:S(2)}) copy-start(bf16[1024,1024]{1,0:T(8,128)(2,1)} %get-tuple-element.12) | copy-start | bytes 6291460
  84.3 10.7 %collective-permute-start.9 = (f32[64,1024]{1,0:T(8,128)S(1)}, f32[64,1024]{1,0:T(8,128)S(1)}, u32[]{:S(2)}, u32[]{:S(2)}) collective-permute-start(f32[64,1024]{1,0:T(8,128)S(1)} %get-tuple-element.48), channel_id=1, source_target_pairs={{2,0},{17,1},{36,2},{51,3},{70,4},{85,5},{96,6},{119,7},{10,8},{25... | collective-permute-start | bytes 786440 | tf_op jit(solution)/shard_map/ppermute | solution.py:82
  88.8 1.6 copy-start.4
  91.4 3.5 %collective-permute-start.10 = (f32[64,1024]{1,0:T(8,128)S(1)}, f32[64,1024]{1,0:T(8,128)S(1)}, u32[]{:S(2)}, u32[]{:S(2)}) collective-permute-start(f32[64,1024]{1,0:T(8,128)S(1)} %fusion.9), channel_id=1, source_target_pairs={{0,8},{1,9},{2,10},{3,11},{4,12},{5,13},{6,14},{7,15},{8,16},{9,17... | collective-permute-start | bytes 786440 | tf_op jit(solution)/shard_map/ppermute | solution.py:82
  95.8 11.3 %collective-permute-start.11 = (f32[64,128]{1,0:T(8,128)S(1)}, f32[64,128]{1,0:T(8,128)S(1)}, u32[]{:S(2)}, u32[]{:S(2)}) collective-permute-start(f32[64,128]{1,0:T(8,128)S(1)} %maximum_maximum_fusion), channel_id=1, source_target_pairs={{0,128},{1,129},{2,130},{3,131},{4,132},{5,133},{6,134},{7,135},{8... | collective-permute-start | bytes 98312 | tf_op jit(solution)/shard_map/ppermute | solution.py:82
  98.2 26.8 %copy-start.5 = (bf16[1024,1024]{1,0:T(8,128)(2,1)S(1)}, bf16[1024,1024]{1,0:T(8,128)(2,1)}, u32[]{:S(2)}) copy-start(bf16[1024,1024]{1,0:T(8,128)(2,1)} %get-tuple-element.10) | copy-start | bytes 6291460
  98.3 33.6 %collective-permute-start.17 = (f32[64,1024]{1,0:T(8,128)S(1)}, f32[64,1024]{1,0:T(8,128)S(1)}, u32[]{:S(2)}, u32[]{:S(2)}) collective-permute-start(f32[64,1024]{1,0:T(8,128)S(1)} %add.140), channel_id=1, source_target_pairs={{0,2},{1,17},{2,36},{3,51},{4,70},{5,85},{6,96},{7,119},{8,10},{9,... | collective-permute-start | bytes 786440 | tf_op jit(solution)/shard_map/ppermute | solution.py:82
  107.2 6.7 %collective-permute-start.12 = (f32[64,128]{1,0:T(8,128)S(1)}, f32[64,128]{1,0:T(8,128)S(1)}, u32[]{:S(2)}, u32[]{:S(2)}) collective-permute-start(f32[64,128]{1,0:T(8,128)S(1)} %fusion.136), channel_id=1, source_target_pairs={{0,64},{1,65},{2,66},{3,67},{4,68},{5,69},{6,70},{7,71},{8,72},{9,... | collective-permute-start | bytes 98312 | tf_op jit(solution)/shard_map/ppermute | solution.py:82
  113.9 6.7 %collective-permute-start.13 = (f32[64,128]{1,0:T(8,128)S(1)}, f32[64,128]{1,0:T(8,128)S(1)}, u32[]{:S(2)}, u32[]{:S(2)}) collective-permute-start(f32[64,128]{1,0:T(8,128)S(1)} %add.144), channel_id=1, source_target_pairs={{0,32},{1,33},{2,34},{3,35},{4,36},{5,37},{6,38},{7,39},{8,40},{9,... | collective-permute-start | bytes 98312 | tf_op jit(solution)/shard_map/ppermute | solution.py:82
  116.4 13.8 %copy-start.2 = (bf16[1024,1024]{1,0:T(8,128)(2,1)S(1)}, bf16[1024,1024]{1,0:T(8,128)(2,1)}, u32[]{:S(2)}) copy-start(bf16[1024,1024]{1,0:T(8,128)(2,1)} %get-tuple-element.12) | copy-start | bytes 6291460
  116.4 13.8 %collective-permute-start.16 = (f32[64,1024]{1,0:T(8,128)S(1)}, f32[64,1024]{1,0:T(8,128)S(1)}, u32[]{:S(2)}, u32[]{:S(2)}) collective-permute-start(f32[64,1024]{1,0:T(8,128)S(1)} %collective-permute-done.9), channel_id=1, source_target_pairs={{8,0},{9,1},{10,2},{11,3},{12,4},{13,5},{14,6},{15,7},{16,8},{17,9... | collective-permute-start | bytes 786440 | tf_op jit(solution)/shard_map/ppermute | solution.py:82
  120.6 6.0 %collective-permute-start.14 = (f32[64,128]{1,0:T(8,128)S(1)}, f32[64,128]{1,0:T(8,128)S(1)}, u32[]{:S(2)}, u32[]{:S(2)}) collective-permute-start(f32[64,128]{1,0:T(8,128)S(1)} %add.145), channel_id=1, source_target_pairs={{0,16},{1,17},{2,18},{3,19},{4,20},{5,21},{6,22},{7,23},{8,24},{9,... | collective-permute-start | bytes 98312 | tf_op jit(solution)/shard_map/ppermute | solution.py:82
  126.6 19.6 %collective-permute-start.15 = (f32[64,128]{1,0:T(8,128)S(1)}, f32[64,128]{1,0:T(8,128)S(1)}, u32[]{:S(2)}, u32[]{:S(2)}) collective-permute-start(f32[64,128]{1,0:T(8,128)S(1)} %add.146), channel_id=1, source_target_pairs={{0,8},{1,9},{2,10},{3,11},{4,12},{5,13},{6,14},{7,15},{8,0},{9,1},... | collective-permute-start | bytes 98312 | tf_op jit(solution)/shard_map/ppermute | solution.py:82
  132.6 20.7 %all-to-all-start.2 = ((f32[8,64,128]{2,1,0:T(8,128)}), f32[8,64,128]{2,1,0:T(8,128)S(1)}, u32[]{:S(2)}, u32[]{:S(2)}) async-start(f32[8,64,128]{2,1,0:T(8,128)} %bitcast_bitcast_fusion), calls=%async_computation.2 | async-start | bytes 524288 | tf_op jit(solution)/shard_map/all_to_all | solution.py:39
  154.3 11.0 %all-to-all-start.3 = ((f32[8,96,128]{2,1,0:T(8,128)}), f32[8,96,128]{2,1,0:T(8,128)S(1)}, u32[]{:S(2)}, u32[]{:S(2)}) async-start(f32[8,96,128]{2,1,0:T(8,128)} %broadcast_in_dim.45), calls=%async_computation.3 | async-start | bytes 786432 | tf_op jit(solution)/shard_map/all_to_all | solution.py:39
  165.9 19.6 %copy-start.9 = (f32[64,64]{1,0:T(8,128)}, f32[64,64]{1,0:T(8,128)S(1)}, u32[]{:S(2)}) copy-start(f32[64,64]{1,0:T(8,128)S(1)} %fusion.87) | copy-start | bytes 49156
  179.7 4.5 %collective-permute-start.18 = (f32[32,128]{1,0:T(8,128)S(1)}, f32[32,128]{1,0:T(8,128)S(1)}, u32[]{:S(2)}, u32[]{:S(2)}) collective-permute-start(f32[32,128]{1,0:T(8,128)S(1)} %reduce_sum.49), channel_id=1, source_target_pairs={{0,8},{1,9},{2,10},{3,11},{4,12},{5,13},{6,14},{7,15},{8,0},{9,1},... | collective-permute-start | bytes 49160 | tf_op jit(solution)/shard_map/ppermute | solution.py:82

commit v7 on v1

--- a/solution.py
+++ b/solution.py
@@ -79,8 +79,7 @@
 
 
 def row_total(part, lay):
-    far = lay.rows // 2
-    for bit in [1, far] + [bit for bit in lay.flip if bit not in (1, far)]:
+    for bit in sorted(lay.flip, reverse=True):
         part = part + permuted(part, lay.flip[bit])
     return part
 
@@ -116,7 +115,8 @@
     part = width // offs
     off_index = lax.axis_index("off")
     row_ids = jnp.arange(width, dtype=jnp.int32)
-    masks = [(row_ids < live[0, s]).astype(jnp.float32) for s in range(per_device)]
+    masks = (lax.broadcasted_iota(jnp.int32, (per_device, width), 1) < live.T).astype(jnp.float32)
+    masks = lax.optimization_barrier(masks)
     blocks = [tiles[:, s * width : (s + 1) * width] for s in range(per_device)]
     identity = jnp.eye(count, dtype=jnp.float32)
     own = lambda array: lax.dynamic_index_in_dim(cut(array, offs), off_index, 0, keepdims=False)
@@ -142,13 +142,15 @@
 
     chunk, precond_chunk, energy_chunk = own(vectors), own(precond[None]), own(energies[None])
     part, share = products(vectors, [])
-    image = energy_chunk * chunk + jnp.sum(exchange(cut(part, offs), lay.row), axis=0)
+    image = jnp.sum(exchange(cut(part, offs), lay.row), axis=0)
+    image = energy_chunk * chunk + image
     stepped, ritz = spread(chunk - precond_chunk * image, share)
     moved = stepped + precond * exact(ritz.T, vectors)
 
     moved_chunk = own(moved)
     part, share = products(moved, [folded(gram(moved, moved))])
-    image = energy_chunk * moved_chunk + jnp.sum(exchange(cut(part, offs), lay.row), axis=0)
+    image = jnp.sum(exchange(cut(part, offs), lay.row), axis=0)
+    image = energy_chunk * moved_chunk + image
     fix = 1.5 * identity - 0.5 * unfolded(share[count // 2 :]) / total_rows
     chunk = exact(fix.T, moved_chunk - precond_chunk * image)
     stepped, ritz = spread(chunk, share[: count // 2])

time: 200 us -> 201 us (level)
  waiting for transfers between devices: 31.8 us -> 39.5 us
  starting transfers between devices: 92.4 us -> 87.4 us
    ppermute x19, waiting for transfers between devices: 19.4 us -> 25.5 us  [permuted(): return lax.ppermute(array, AXES, pairs)]
    all_to_all x3, starting transfers between devices: 32.6 us -> 27.4 us  [exchange(): lax.all_to_all(array, AXES, 0, 0, axis_index_groups=groups, tiled=True)]
  transfers between devices with their start and end apart: 22 -> 22, of which waited for: 10 -> 9; matrix products, arithmetic and copies ran while one was open for 15% -> 14% of each run, Pallas kernels for 0% -> 0%
where the time goes in v7:
time: 201 us; the launch traced here: 200 us
  starting transfers between devices  87.4 us (43%)
  waiting for transfers between devices  39.5 us (20%)
  matrix products  36.7 us (18%)
  blocking collectives  30.9 us (15%)
  other arithmetic  2.85 us (1%)
    ppermute x19, starting transfers between devices, permuted(): return lax.ppermute(array, AXES, pairs)  60 us
    all_to_all x2, blocking collectives, exchange(): lax.all_to_all(array, AXES, 0, 0, axis_index_groups=groups, tiled=True)  30.9 us
    all_to_all x3, starting transfers between devices, exchange(): lax.all_to_all(array, AXES, 0, 0, axis_index_groups=groups, tiled=True)  27.4 us
    ppermute x19, waiting for transfers between devices, permuted(): return lax.ppermute(array, AXES, pairs)  25.5 us
    dot_general x4, matrix products, direct_product(): lax.dot_general(piece, block, (((1,), (1,)), ((), ())), precision=lax.Pre...  16.9 us
    dot_general x4, matrix products, back_product(): jnp.dot(vectors * mask, block, precision=lax.Precision.HIGH, preferred_el...  14.6 us
    all_to_all x3, waiting for transfers between devices, exchange(): lax.all_to_all(array, AXES, 0, 0, axis_index_groups=groups, tiled=True)  14.1 us
  transfers between devices with their start and end apart: 22, of which 9 were waited for; matrix products, arithmetic and copies ran while one was open for 14% of the time, Pallas kernels for 0%

profile of v7, /device:TPU:1, one launch (start us, length us, event | category | flops | bytes accessed | tf_op | source)
XLA Modules:
  0.0 200.0 jit_solution(1541451491068090593)
XLA Ops:
  0.7 1.7 collective-permute-start
  2.4 0.7 compare_convert_fusion
  3.1 3.7 %fusion.4 = f32[64,1024]{1,0:T(8,128)S(1)} fusion(f32[1024,2048]{1,0:T(8,128)} %param.6, f32[64,1024]{1,0:T(8,128)} %param.5, f32[1024]{0:T(1024)S(1)} %bitcast.77), kind=kOutput, calls=%fused_computation.4 | convolution fusion | flops 402718720 | bytes 4722688 | tf_op jit(solution)/shard_map/dot_general | solution.py:104
  6.8 12.3 %collective-permute-start.2 = (f32[64,1024]{1,0:T(8,128)S(1)}, f32[64,1024]{1,0:T(8,128)S(1)}, u32[]{:S(2)}, u32[]{:S(2)}) collective-permute-start(f32[64,1024]{1,0:T(8,128)S(1)} %fusion.4), channel_id=1, source_target_pairs={{0,8},{1,9},{2,10},{3,11},{4,12},{5,13},{6,14},{7,15},{8,16},{9,17... | collective-permute-start | bytes 786440 | tf_op jit(solution)/shard_map/ppermute | solution.py:78
  19.1 3.7 %fusion.12 = f32[64,1024]{1,0:T(8,128)S(1)} fusion(f32[1024,2048]{1,0:T(8,128)} %param.6, f32[64,1024]{1,0:T(8,128)} %param.5, f32[1024]{0:T(1024)S(1)} %bitcast.81), kind=kOutput, calls=%fused_computation.12 | convolution fusion | flops 402718720 | bytes 4722688 | tf_op jit(solution)/shard_map/dot_general | solution.py:104
  22.8 0.4 fusion.30
  23.2 1.2 collective-permute-done.2
  24.5 0.4 fusion.86
  24.9 0.1 copy.23
  25.0 0.1 pad_maximum_fusion.2
  25.1 2.8 %collective-permute-start.4 = (f32[32,128]{1,0:T(8,128)S(1)}, f32[32,128]{1,0:T(8,128)S(1)}, u32[]{:S(2)}, u32[]{:S(2)}) collective-permute-start(f32[32,128]{1,0:T(8,128)S(1)} %pad_maximum_fusion.2), channel_id=1, source_target_pairs={{0,128},{1,129},{2,130},{3,131},{4,132},{5,133},{6,134},{7,135},{8... | collective-permute-start | bytes 49160 | tf_op jit(solution)/shard_map/ppermute | solution.py:78
  27.8 0.7 collective-permute-start.3
  28.5 1.7 collective-permute-start.1
  30.2 0.1 fusion.111
  30.3 6.9 %collective-permute-start.5 = (f32[32,128]{1,0:T(8,128)S(1)}, f32[32,128]{1,0:T(8,128)S(1)}, u32[]{:S(2)}, u32[]{:S(2)}) collective-permute-start(f32[32,128]{1,0:T(8,128)S(1)} %fusion.111), channel_id=1, source_target_pairs={{0,64},{1,65},{2,66},{3,67},{4,68},{5,69},{6,70},{7,71},{8,72},{9,... | collective-permute-start | bytes 49160 | tf_op jit(solution)/shard_map/ppermute | solution.py:78
  37.2 4.2 %fusion.16 = f32[64,1024]{1,0:T(8,128)S(1)} fusion(f32[64,1024]{1,0:T(8,128)S(1)} %collective-permute-done, f32[1024,2048]{1,0:T(8,128)} %param.6, f32[1024]{0:T(1024)S(1)} %bitcast.82), kind=kOutput, calls=%fused_computation.16 | convolution fusion | flops 402718720 | bytes 4722688 | tf_op jit(solution)/shard_map/dot_general | solution.py:93
  41.4 2.1 %collective-permute-start.6 = (f32[32,128]{1,0:T(8,128)S(1)}, f32[32,128]{1,0:T(8,128)S(1)}, u32[]{:S(2)}, u32[]{:S(2)}) collective-permute-start(f32[32,128]{1,0:T(8,128)S(1)} %add.91), channel_id=1, source_target_pairs={{0,32},{1,33},{2,34},{3,35},{4,36},{5,37},{6,38},{7,39},{8,40},{9,... | collective-permute-start | bytes 49160 | tf_op jit(solution)/shard_map/ppermute | solution.py:78
  43.5 4.2 %fusion.22 = f32[64,1024]{1,0:T(8,128)S(1)} fusion(f32[64,1024]{1,0:T(8,128)S(1)} %collective-permute-done.1, f32[1024,2048]{1,0:T(8,128)} %param.6, f32[1024]{0:T(1024)S(1)} %bitcast.78), kind=kOutput, calls=%fused_computation.18 | convolution fusion | flops 402718720 | bytes 4722688 | tf_op jit(solution)/shard_map/dot_general | solution.py:93
  47.8 0.7 bitcast_bitcast_fusion.1
  48.5 11.1 %all-to-all-start = ((f32[8,64,128]{2,1,0:T(8,128)}), f32[8,64,128]{2,1,0:T(8,128)S(1)}, u32[]{:S(2)}, u32[]{:S(2)}) async-start(f32[8,64,128]{2,1,0:T(8,128)} %bitcast_bitcast_fusion.1), calls=%async_computation | async-start | bytes 524288 | tf_op jit(solution)/shard_map/all_to_all | solution.py:35
  59.7 1.5 collective-permute-start.7
  61.2 1.1 collective-permute-done.7
  62.4 6.4 %collective-permute-start.8 = (f32[32,128]{1,0:T(8,128)S(1)}, f32[32,128]{1,0:T(8,128)S(1)}, u32[]{:S(2)}, u32[]{:S(2)}) collective-permute-start(f32[32,128]{1,0:T(8,128)S(1)} %add.93), channel_id=1, source_target_pairs={{0,8},{1,9},{2,10},{3,11},{4,12},{5,13},{6,14},{7,15},{8,0},{9,1},... | collective-permute-start | bytes 49160 | tf_op jit(solution)/shard_map/ppermute | solution.py:78
  68.7 0.8 collective-permute-done.8
  69.7 13.1 %all_to_all.25 = f32[8,96,128]{2,1,0:T(8,128)S(1)} all-to-all(f32[8,96,128]{2,1,0:T(8,128)S(1)} %broadcast_in_dim.6), channel_id=1, replica_groups={{0,1,2,3,4,5,6,7},{8,9,10,11,12,13,14,15},{16,17,18,19,20,21,22,23},{24..., dimensions={0} | all-to-all | bytes 786432 | tf_op jit(solution)/shard_map/all_to_all | solution.py:35
  82.8 0.4 fusion.29
  83.2 0.4 fusion.88
  83.6 3.6 %fusion.2 = f32[64,1024]{1,0:T(8,128)S(1)} fusion(f32[1024,2048]{1,0:T(8,128)} %param.6, f32[64,1024]{1,0:T(8,128)S(1)} %fusion.29, f32[1024]{0:T(1024)S(1)} %bitcast.79), kind=kOutput, calls=%fused_computation.2 | convolution fusion | flops 402718720 | bytes 4722688 | tf_op jit(solution)/shard_map/dot_general | solution.py:104
  87.2 3.6 %fusion.10 = f32[64,1024]{1,0:T(8,128)S(1)} fusion(f32[1024,2048]{1,0:T(8,128)} %param.6, f32[64,1024]{1,0:T(8,128)S(1)} %fusion.29, f32[1024]{0:T(1024)S(1)} %bitcast.83), kind=kOutput, calls=%fused_computation.10 | convolution fusion | flops 402718720 | bytes 4722688 | tf_op jit(solution)/shard_map/dot_general | solution.py:104
  90.8 0.7 collective-permute-start.9
  91.5 6.2 %collective-permute-start.10 = (f32[64,1024]{1,0:T(8,128)S(1)}, f32[64,1024]{1,0:T(8,128)S(1)}, u32[]{:S(2)}, u32[]{:S(2)}) collective-permute-start(f32[64,1024]{1,0:T(8,128)S(1)} %fusion.2), channel_id=1, source_target_pairs={{0,8},{1,9},{2,10},{3,11},{4,12},{5,13},{6,14},{7,15},{8,16},{9,17... | collective-permute-start | bytes 786440 | tf_op jit(solution)/shard_map/ppermute | solution.py:78
  97.7 0.4 convolution_multiply_fusion.2
  98.1 13.6 %collective-permute-done.10 = f32[64,1024]{1,0:T(8,128)S(1)} collective-permute-done((f32[64,1024]{1,0:T(8,128)S(1)}, f32[64,1024]{1,0:T(8,128)S(1)}, u32[]{:S(2)}, u32[]{:S(2)}) %collective-permute-start.10) | collective-permute-done | bytes 262176 | tf_op jit(solution)/shard_map/ppermute | solution.py:78
  111.8 0.4 fusion.87
  112.4 0.1 maximum_maximum_fusion
  112.5 1.8 collective-permute-start.11
  114.3 2.5 %collective-permute-done.11 = f32[64,128]{1,0:T(8,128)S(1)} collective-permute-done((f32[64,128]{1,0:T(8,128)S(1)}, f32[64,128]{1,0:T(8,128)S(1)}, u32[]{:S(2)}, u32[]{:S(2)}) %collective-permute-start.11) | collective-permute-done | bytes 32800 | tf_op jit(solution)/shard_map/ppermute | solution.py:78
  116.8 0.1 fusion.110
  116.9 1.8 collective-permute-start.12
  118.7 5.2 %collective-permute-done.12 = f32[64,128]{1,0:T(8,128)S(1)} collective-permute-done((f32[64,128]{1,0:T(8,128)S(1)}, f32[64,128]{1,0:T(8,128)S(1)}, u32[]{:S(2)}, u32[]{:S(2)}) %collective-permute-start.12) | collective-permute-done | bytes 32800 | tf_op jit(solution)/shard_map/ppermute | solution.py:78
  124.0 0.7 collective-permute-start.17
  124.7 5.0 %collective-permute-start.16 = (f32[64,1024]{1,0:T(8,128)S(1)}, f32[64,1024]{1,0:T(8,128)S(1)}, u32[]{:S(2)}, u32[]{:S(2)}) collective-permute-start(f32[64,1024]{1,0:T(8,128)S(1)} %collective-permute-done.9), channel_id=1, source_target_pairs={{8,0},{9,1},{10,2},{11,3},{12,4},{13,5},{14,6},{15,7},{16,8},{17,9... | collective-permute-start | bytes 786440 | tf_op jit(solution)/shard_map/ppermute | solution.py:78
  129.7 1.0 collective-permute-start.14
  130.7 4.2 %fusion.19 = f32[64,1024]{1,0:T(8,128)S(1)} fusion(f32[64,1024]{1,0:T(8,128)S(1)} %collective-permute-done.9, f32[1024,2048]{1,0:T(8,128)} %param.6, f32[1024]{0:T(1024)S(1)} %bitcast.84), kind=kOutput, calls=%fused_computation.17 | convolution fusion | flops 402718720 | bytes 4722688 | tf_op jit(solution)/shard_map/dot_general | solution.py:93
  134.9 3.2 %collective-permute-start.15 = (f32[64,128]{1,0:T(8,128)S(1)}, f32[64,128]{1,0:T(8,128)S(1)}, u32[]{:S(2)}, u32[]{:S(2)}) collective-permute-start(f32[64,128]{1,0:T(8,128)S(1)} %add.102), channel_id=1, source_target_pairs={{0,8},{1,9},{2,10},{3,11},{4,12},{5,13},{6,14},{7,15},{8,0},{9,1},... | collective-permute-start | bytes 98312 | tf_op jit(solution)/shard_map/ppermute | solution.py:78
  138.1 4.2 %fusion.25 = f32[64,1024]{1,0:T(8,128)S(1)} fusion(f32[64,1024]{1,0:T(8,128)S(1)} %collective-permute-done.16, f32[1024,2048]{1,0:T(8,128)} %param.6, f32[1024]{0:T(1024)S(1)} %bitcast.80), kind=kOutput, calls=%fused_computation.19 | convolution fusion | flops 402718720 | bytes 4722688 | tf_op jit(solution)/shard_map/dot_general | solution.py:93
  142.3 0.7 bitcast_bitcast_fusion
  143.1 12.8 %all-to-all-start.2 = ((f32[8,64,128]{2,1,0:T(8,128)}), f32[8,64,128]{2,1,0:T(8,128)S(1)}, u32[]{:S(2)}, u32[]{:S(2)}) async-start(f32[8,64,128]{2,1,0:T(8,128)} %bitcast_bitcast_fusion), calls=%async_computation.2 | async-start | bytes 524288 | tf_op jit(solution)/shard_map/all_to_all | solution.py:35
  156.1 6.9 %all-to-all-done.2 = f32[8,64,128]{2,1,0:T(8,128)S(1)} async-done(((f32[8,64,128]{2,1,0:T(8,128)}), f32[8,64,128]{2,1,0:T(8,128)S(1)}, u32[]{:S(2)}, u32[]{:S(2)}) %all-to-all-start.2) | async-done | bytes 262176 | tf_op jit(solution)/shard_map/all_to_all | solution.py:35
  163.0 0.2 fusion.53
  163.3 0.8 broadcast_in_dim.7
  164.1 3.5 %all-to-all-start.3 = ((f32[8,96,128]{2,1,0:T(8,128)}), f32[8,96,128]{2,1,0:T(8,128)S(1)}, u32[]{:S(2)}, u32[]{:S(2)}) async-start(f32[8,96,128]{2,1,0:T(8,128)} %broadcast_in_dim.7), calls=%async_computation.3 | async-start | bytes 786432 | tf_op jit(solution)/shard_map/all_to_all | solution.py:35
  167.5 0.4 fusion.75
  167.9 7.1 %all-to-all-done.3 = f32[8,96,128]{2,1,0:T(8,128)S(1)} async-done(((f32[8,96,128]{2,1,0:T(8,128)}), f32[8,96,128]{2,1,0:T(8,128)S(1)}, u32[]{:S(2)}, u32[]{:S(2)}) %all-to-all-start.3) | async-done | bytes 393248 | tf_op jit(solution)/shard_map/all_to_all | solution.py:35
  175.2 0.2 fusion.46
  175.4 0.2 fusion.76
  175.6 0.4 fusion.28
  176.0 0.4 fusion.89
  176.4 0.1 pad_maximum_fusion.3
  176.5 17.8 %all_to_all.26 = f32[16,32,128]{2,1,0:T(8,128)S(1)} all-to-all(f32[16,32,128]{2,1,0:T(8,128)S(1)} %broadcast_in_dim.8), channel_id=1, replica_groups={{0,16,32,48,64,80,96,112,128,144,160,176,192,208,224,240},{1,17,33,49,6..., dimensions={0} | all-to-all | bytes 524288 | tf_op jit(solution)/shard_map/all_to_all | solution.py:35
  194.4 3.6 %collective-permute-start.18 = (f32[32,128]{1,0:T(8,128)S(1)}, f32[32,128]{1,0:T(8,128)S(1)}, u32[]{:S(2)}, u32[]{:S(2)}) collective-permute-start(f32[32,128]{1,0:T(8,128)S(1)} %reduce_sum.49), channel_id=1, source_target_pairs={{0,8},{1,9},{2,10},{3,11},{4,12},{5,13},{6,14},{7,15},{8,0},{9,1},... | collective-permute-start | bytes 49160 | tf_op jit(solution)/shard_map/ppermute | solution.py:78
  198.0 0.8 collective-permute-done.18
  198.8 0.1 fusion.82
  198.9 1.1 fusion.43
  (62 shorter events, 1.0 us)
Async XLA Ops:
  0.6 22.2 %copy-start = (f32[64,1024]{1,0:T(8,128)S(1)}, f32[64,1024]{1,0:T(8,128)}, u32[]{:S(2)}) copy-start(f32[64,1024]{1,0:T(8,128)} %param.5) | copy-start | bytes 786436
  0.6 22.2 %copy-start.2 = (f32[1024]{0:T(1024)S(1)}, f32[1024]{0:T(1024)}, u32[]{:S(2)}) copy-start(f32[1024]{0:T(1024)} %param.8) | copy-start | bytes 12292
  0.7 23.8 %collective-permute-start = (f32[64,1024]{1,0:T(8,128)}, f32[64,1024]{1,0:T(8,128)S(1)}, u32[]{:S(2)}, u32[]{:S(2)}) collective-permute-start(f32[64,1024]{1,0:T(8,128)} %param.5), channel_id=1, source_target_pairs={{0,0},{1,241},{2,226},{3,211},{4,196},{5,181},{6,166},{7,151},{8,8... | collective-permute-start | bytes 786440 | tf_op jit(solution)/shard_map/ppermute | solution.py:78
  6.8 17.6 %collective-permute-start.2 = (f32[64,1024]{1,0:T(8,128)S(1)}, f32[64,1024]{1,0:T(8,128)S(1)}, u32[]{:S(2)}, u32[]{:S(2)}) collective-permute-start(f32[64,1024]{1,0:T(8,128)S(1)} %fusion.4), channel_id=1, source_target_pairs={{0,8},{1,9},{2,10},{3,11},{4,12},{5,13},{6,14},{7,15},{8,16},{9,17... | collective-permute-start | bytes 786440 | tf_op jit(solution)/shard_map/ppermute | solution.py:78
  19.1 49.6 %copy-start.3 = (f32[1024]{0:T(1024)S(1)}, f32[1024]{0:T(1024)}, u32[]{:S(2)}) copy-start(f32[1024]{0:T(1024)} %param.9) | copy-start | bytes 12292
  25.1 5.2 %collective-permute-start.4 = (f32[32,128]{1,0:T(8,128)S(1)}, f32[32,128]{1,0:T(8,128)S(1)}, u32[]{:S(2)}, u32[]{:S(2)}) collective-permute-start(f32[32,128]{1,0:T(8,128)S(1)} %pad_maximum_fusion.2), channel_id=1, source_target_pairs={{0,128},{1,129},{2,130},{3,131},{4,132},{5,133},{6,134},{7,135},{8... | collective-permute-start | bytes 49160 | tf_op jit(solution)/shard_map/ppermute | solution.py:78
  27.8 19.9 %collective-permute-start.3 = (f32[64,1024]{1,0:T(8,128)S(1)}, f32[64,1024]{1,0:T(8,128)S(1)}, u32[]{:S(2)}, u32[]{:S(2)}) collective-permute-start(f32[64,1024]{1,0:T(8,128)S(1)} %add.85), channel_id=1, source_target_pairs={{0,0},{241,1},{226,2},{211,3},{196,4},{181,5},{166,6},{151,7},{8,8... | collective-permute-start | bytes 786440 | tf_op jit(solution)/shard_map/ppermute | solution.py:78
  28.5 15.0 %collective-permute-start.1 = (f32[64,1024]{1,0:T(8,128)S(1)}, f32[64,1024]{1,0:T(8,128)S(1)}, u32[]{:S(2)}, u32[]{:S(2)}) collective-permute-start(f32[64,1024]{1,0:T(8,128)S(1)} %collective-permute-done), channel_id=1, source_target_pairs={{8,0},{9,1},{10,2},{11,3},{12,4},{13,5},{14,6},{15,7},{16,8},{17,9... | collective-permute-start | bytes 786440 | tf_op jit(solution)/shard_map/ppermute | solution.py:78
  30.3 11.1 %collective-permute-start.5 = (f32[32,128]{1,0:T(8,128)S(1)}, f32[32,128]{1,0:T(8,128)S(1)}, u32[]{:S(2)}, u32[]{:S(2)}) collective-permute-start(f32[32,128]{1,0:T(8,128)S(1)} %fusion.111), channel_id=1, source_target_pairs={{0,64},{1,65},{2,66},{3,67},{4,68},{5,69},{6,70},{7,71},{8,72},{9,... | collective-permute-start | bytes 49160 | tf_op jit(solution)/shard_map/ppermute | solution.py:78
  41.4 18.2 %collective-permute-start.6 = (f32[32,128]{1,0:T(8,128)S(1)}, f32[32,128]{1,0:T(8,128)S(1)}, u32[]{:S(2)}, u32[]{:S(2)}) collective-permute-start(f32[32,128]{1,0:T(8,128)S(1)} %add.91), channel_id=1, source_target_pairs={{0,32},{1,33},{2,34},{3,35},{4,36},{5,37},{6,38},{7,39},{8,40},{9,... | collective-permute-start | bytes 49160 | tf_op jit(solution)/shard_map/ppermute | solution.py:78
  48.5 21.1 %all-to-all-start = ((f32[8,64,128]{2,1,0:T(8,128)}), f32[8,64,128]{2,1,0:T(8,128)S(1)}, u32[]{:S(2)}, u32[]{:S(2)}) async-start(f32[8,64,128]{2,1,0:T(8,128)} %bitcast_bitcast_fusion.1), calls=%async_computation | async-start | bytes 524288 | tf_op jit(solution)/shard_map/all_to_all | solution.py:35
  59.7 2.7 %collective-permute-start.7 = (f32[32,128]{1,0:T(8,128)S(1)}, f32[32,128]{1,0:T(8,128)S(1)}, u32[]{:S(2)}, u32[]{:S(2)}) collective-permute-start(f32[32,128]{1,0:T(8,128)S(1)} %add.92), channel_id=1, source_target_pairs={{0,16},{1,17},{2,18},{3,19},{4,20},{5,21},{6,22},{7,23},{8,24},{9,... | collective-permute-start | bytes 49160 | tf_op jit(solution)/shard_map/ppermute | solution.py:78
  62.4 7.2 %collective-permute-start.8 = (f32[32,128]{1,0:T(8,128)S(1)}, f32[32,128]{1,0:T(8,128)S(1)}, u32[]{:S(2)}, u32[]{:S(2)}) collective-permute-start(f32[32,128]{1,0:T(8,128)S(1)} %add.93), channel_id=1, source_target_pairs={{0,8},{1,9},{2,10},{3,11},{4,12},{5,13},{6,14},{7,15},{8,0},{9,1},... | collective-permute-start | bytes 49160 | tf_op jit(solution)/shard_map/ppermute | solution.py:78
  90.8 20.9 %collective-permute-start.9 = (f32[64,1024]{1,0:T(8,128)S(1)}, f32[64,1024]{1,0:T(8,128)S(1)}, u32[]{:S(2)}, u32[]{:S(2)}) collective-permute-start(f32[64,1024]{1,0:T(8,128)S(1)} %fusion.29), channel_id=1, source_target_pairs={{0,0},{1,241},{2,226},{3,211},{4,196},{5,181},{6,166},{7,151},{8,8... | collective-permute-start | bytes 786440 | tf_op jit(solution)/shard_map/ppermute | solution.py:78
  91.5 20.2 %collective-permute-start.10 = (f32[64,1024]{1,0:T(8,128)S(1)}, f32[64,1024]{1,0:T(8,128)S(1)}, u32[]{:S(2)}, u32[]{:S(2)}) collective-permute-start(f32[64,1024]{1,0:T(8,128)S(1)} %fusion.2), channel_id=1, source_target_pairs={{0,8},{1,9},{2,10},{3,11},{4,12},{5,13},{6,14},{7,15},{8,16},{9,17... | collective-permute-start | bytes 786440 | tf_op jit(solution)/shard_map/ppermute | solution.py:78
  112.5 4.3 %collective-permute-start.11 = (f32[64,128]{1,0:T(8,128)S(1)}, f32[64,128]{1,0:T(8,128)S(1)}, u32[]{:S(2)}, u32[]{:S(2)}) collective-permute-start(f32[64,128]{1,0:T(8,128)S(1)} %maximum_maximum_fusion), channel_id=1, source_target_pairs={{0,128},{1,129},{2,130},{3,131},{4,132},{5,133},{6,134},{7,135},{8... | collective-permute-start | bytes 98312 | tf_op jit(solution)/shard_map/ppermute | solution.py:78
  116.9 7.1 %collective-permute-start.12 = (f32[64,128]{1,0:T(8,128)S(1)}, f32[64,128]{1,0:T(8,128)S(1)}, u32[]{:S(2)}, u32[]{:S(2)}) collective-permute-start(f32[64,128]{1,0:T(8,128)S(1)} %fusion.110), channel_id=1, source_target_pairs={{0,64},{1,65},{2,66},{3,67},{4,68},{5,69},{6,70},{7,71},{8,72},{9,... | collective-permute-start | bytes 98312 | tf_op jit(solution)/shard_map/ppermute | solution.py:78
  124.0 5.7 %collective-permute-start.13 = (f32[64,128]{1,0:T(8,128)S(1)}, f32[64,128]{1,0:T(8,128)S(1)}, u32[]{:S(2)}, u32[]{:S(2)}) collective-permute-start(f32[64,128]{1,0:T(8,128)S(1)} %add.100), channel_id=1, source_target_pairs={{0,32},{1,33},{2,34},{3,35},{4,36},{5,37},{6,38},{7,39},{8,40},{9,... | collective-permute-start | bytes 98312 | tf_op jit(solution)/shard_map/ppermute | solution.py:78
  124.0 18.3 %collective-permute-start.17 = (f32[64,1024]{1,0:T(8,128)S(1)}, f32[64,1024]{1,0:T(8,128)S(1)}, u32[]{:S(2)}, u32[]{:S(2)}) collective-permute-start(f32[64,1024]{1,0:T(8,128)S(1)} %add.96), channel_id=1, source_target_pairs={{0,0},{241,1},{226,2},{211,3},{196,4},{181,5},{166,6},{151,7},{8,8... | collective-permute-start | bytes 786440 | tf_op jit(solution)/shard_map/ppermute | solution.py:78
  124.7 13.4 %collective-permute-start.16 = (f32[64,1024]{1,0:T(8,128)S(1)}, f32[64,1024]{1,0:T(8,128)S(1)}, u32[]{:S(2)}, u32[]{:S(2)}) collective-permute-start(f32[64,1024]{1,0:T(8,128)S(1)} %collective-permute-done.9), channel_id=1, source_target_pairs={{8,0},{9,1},{10,2},{11,3},{12,4},{13,5},{14,6},{15,7},{16,8},{17,9... | collective-permute-start | bytes 786440 | tf_op jit(solution)/shard_map/ppermute | solution.py:78
  129.7 5.2 %collective-permute-start.14 = (f32[64,128]{1,0:T(8,128)S(1)}, f32[64,128]{1,0:T(8,128)S(1)}, u32[]{:S(2)}, u32[]{:S(2)}) collective-permute-start(f32[64,128]{1,0:T(8,128)S(1)} %add.101), channel_id=1, source_target_pairs={{0,16},{1,17},{2,18},{3,19},{4,20},{5,21},{6,22},{7,23},{8,24},{9,... | collective-permute-start | bytes 98312 | tf_op jit(solution)/shard_map/ppermute | solution.py:78
  134.9 21.0 %collective-permute-start.15 = (f32[64,128]{1,0:T(8,128)S(1)}, f32[64,128]{1,0:T(8,128)S(1)}, u32[]{:S(2)}, u32[]{:S(2)}) collective-permute-start(f32[64,128]{1,0:T(8,128)S(1)} %add.102), channel_id=1, source_target_pairs={{0,8},{1,9},{2,10},{3,11},{4,12},{5,13},{6,14},{7,15},{8,0},{9,1},... | collective-permute-start | bytes 98312 | tf_op jit(solution)/shard_map/ppermute | solution.py:78
  143.1 19.9 %all-to-all-start.2 = ((f32[8,64,128]{2,1,0:T(8,128)}), f32[8,64,128]{2,1,0:T(8,128)S(1)}, u32[]{:S(2)}, u32[]{:S(2)}) async-start(f32[8,64,128]{2,1,0:T(8,128)} %bitcast_bitcast_fusion), calls=%async_computation.2 | async-start | bytes 524288 | tf_op jit(solution)/shard_map/all_to_all | solution.py:35
  164.1 11.0 %all-to-all-start.3 = ((f32[8,96,128]{2,1,0:T(8,128)}), f32[8,96,128]{2,1,0:T(8,128)S(1)}, u32[]{:S(2)}, u32[]{:S(2)}) async-start(f32[8,96,128]{2,1,0:T(8,128)} %broadcast_in_dim.7), calls=%async_computation.3 | async-start | bytes 786432 | tf_op jit(solution)/shard_map/all_to_all | solution.py:35
  175.6 24.5 %copy-start.1 = (f32[64,64]{1,0:T(8,128)}, f32[64,64]{1,0:T(8,128)S(1)}, u32[]{:S(2)}) copy-start(f32[64,64]{1,0:T(8,128)S(1)} %fusion.76) | copy-start | bytes 49156
  194.4 4.5 %collective-permute-start.18 = (f32[32,128]{1,0:T(8,128)S(1)}, f32[32,128]{1,0:T(8,128)S(1)}, u32[]{:S(2)}, u32[]{:S(2)}) collective-permute-start(f32[32,128]{1,0:T(8,128)S(1)} %reduce_sum.49), channel_id=1, source_target_pairs={{0,8},{1,9},{2,10},{3,11},{4,12},{5,13},{6,14},{7,15},{8,0},{9,1},... | collective-permute-start | bytes 49160 | tf_op jit(solution)/shard_map/ppermute | solution.py:78
